TPU v7x, 32 devices: a whole 2x2x4 slice. The times are simulated.
32 devices in a mesh: row: 8 (over y, x, core), col: 4 (over z).
Axes of the slice: x: 2, y: 2, z: 4, core: 2. Of those that a mesh axis runs over, the one named last changes fastest.
Arguments:
- tiles: bfloat16 [128, 64, 128, 128], P('row', 'col'), may hold values from -0.09375 to 0.09375
- col_index: int32 [128, 64], P('row', 'col'), may hold values from 0 to 15
- counts: int32 [128, 4], P('row', 'col'), may hold values from 1 to 16, as said below
- sketch: bfloat16 [8192, 512], P('col'), may hold values from -6 to 6
Outputs:
- basis: float32 [16384, 512], P(('row', 'col'))
- factor: float32 [512, 512], replicated
Inputs may be any that keep to these rules, and one draw needn't show every extreme that they name: Slots at or beyond counts hold values that are ignored. Some tile row fills all 16 slots of some ignition block.
All inputs are finite; a program needn't handle non-finite values.
Results may differ from a plain program's by a relative error of at most 0.003.
Values may be sent and summed in bfloat16 or wider, within the bound.
No kernel may reach another device: no remote copies, remote signals or barrier semaphores. Data moves between devices by JAX's collectives and lax.ppermute only.
A program may use at most 128 MiB of HBM per device.

v0:
```python
import jax
import jax.numpy as jnp
from jax import lax
from jax.sharding import PartitionSpec as P


def swapped(value, axis, distance):
    mask = 2**distance
    pairs = [(source, source ^ mask) for source in range(lax.axis_size(axis))]
    return lax.ppermute(value, axis, pairs)


def local(tiles, col_index, counts, sketch):
    tile_rows, slots, tile = (tiles.shape[0], tiles.shape[1], tiles.shape[2])
    width = sketch.shape[1]
    col_tiles = sketch.shape[0] // tile
    total_rows = tile_rows * tile * lax.axis_size("row")
    live = (jnp.arange(slots)[None, :] < counts).astype(jnp.bfloat16)
    live_float = live.astype(jnp.float32)
    share_rows = tile_rows * tile // lax.axis_size("col")

    def project_rows(x_tiles):
        many = share_rows * lax.axis_size("col") // tile
        picked = jnp.take(x_tiles, col_index, axis=0) * live[:, :, None, None]
        matrix_product = jnp.einsum(
            "rsab,rsbk->rak", tiles, picked, preferred_element_type=jnp.float32
        )
        return lax.psum_scatter(
            matrix_product.reshape(many * tile, width), "col", scatter_dimension=0, tiled=True
        )

    def orthonormal(panel):
        gram = jnp.dot(
            panel.T, panel, precision=lax.Precision.HIGHEST, preferred_element_type=jnp.float32
        )
        for level in range(lax.axis_size(("row", "col")).bit_length() - 1):
            gram = gram + swapped(gram, ("row", "col"), level)
        lower = jnp.linalg.cholesky(gram / total_rows)
        basis = lax.linalg.triangular_solve(
            lower, panel, left_side=False, lower=True, transpose_a=True
        )
        return (basis, lower.T)

    first = project_rows(sketch.reshape(col_tiles, tile, width))
    first_q, unused = orthonormal(first)
    q_local = lax.all_gather(first_q.astype(jnp.bfloat16), "col", axis=0, tiled=True).reshape(
        tile_rows, tile, width
    )

    def accumulate(index, total):
        matrix_product = jnp.einsum(
            "sab,ak->sbk", tiles[index], q_local[index], preferred_element_type=jnp.float32
        )
        matrix_product = matrix_product * live_float[index][:, None, None]
        return total.at[col_index[index]].add(matrix_product)

    back_part = lax.fori_loop(
        0, tile_rows, accumulate, jnp.zeros((col_tiles, tile, width), jnp.float32)
    )
    back = lax.psum(back_part, "row").astype(jnp.bfloat16)
    second = project_rows(back)
    basis, factor = orthonormal(second)
    return (basis, factor)


def solution(mesh):
    return jax.shard_map(
        local,
        mesh=mesh,
        in_specs=(P("row", "col", None, None), P("row", "col"), P("row", "col"), P("col", None)),
        out_specs=(P(("row", "col"), None), P()),
        check_vma=False,
    )
```

profile of v0, /device:TPU:0, one launch (start us, length us, event | category | flops | bytes accessed | tf_op | source)
XLA Modules:
  0.0 1161.5 jit_solution(8305503465037512460)
XLA Ops:
  8.9 13.7 %gather_fusion = bf16[256,128,512]{2,1,0:T(8,128)(2,1)} fusion(bf16[16,128,512]{2,1,0:T(8,128)(2,1)S(1)} %bitcast.151, s32[1024]{0:T(1024)S(1)} %pad_clamp_fusion), kind=kCustom, calls=%fused_computation.clone | custom fusion | bytes 67109888 | tf_op jit(solution)/shard_map/jit(_take)/gather | solution.py:24
  22.7 19.1 %fusion.9 = f32[16,512,128,1]{1,2,3,0:T(8,128)} fusion(bf16[16,16,128,128]{3,2,1,0:T(8,128)(2,1)} %param.11, bf16[16,16,128,512]{3,2,1,0:T(8,128)(2,1)} %bitcast.153, pred[16,16]{1,0:T(8,128)(4,1)S(1)} %get-tuple-element.199, bf16[16,16]{1,0:T(8,128)(2,1)S(1)} %get-tuple-element.194), kind=kOutput, calls=%fused_computation.22 | convolution fusion | flops 4378853376 | bytes 46138112 | tf_op jit(solution)/shard_map/rsab,rsbk->rak/dot_general | solution.py:25
  42.0 79.6 %reduce-scatter.3.cloned.1.call-done = f32[512,512]{1,0:T(8,128)} async-done(((f32[2048,512]{1,0:T(8,128)}), f32[512,512]{1,0:T(8,128)}) %reduce-scatter.3.cloned.1.call-update) | async-done | bytes 1048592 | tf_op jit(solution)/shard_map/reduce_scatter | solution.py:28
  126.6 23.1 %collective-permute-done = f32[512,512]{0,1:T(8,128)S(1)} collective-permute-done((f32[512,512]{0,1:T(8,128)S(1)}, f32[512,512]{0,1:T(8,128)S(1)}, u32[]{:S(2)}, u32[]{:S(2)}) %collective-permute-start) | collective-permute-done | bytes 1048608 | tf_op jit(solution)/shard_map/ppermute | solution.py:10
  153.1 44.7 %collective-permute-done.1 = f32[512,512]{0,1:T(8,128)S(1)} collective-permute-done((f32[512,512]{0,1:T(8,128)S(1)}, f32[512,512]{0,1:T(8,128)S(1)}, u32[]{:S(2)}, u32[]{:S(2)}) %collective-permute-start.1) | collective-permute-done | bytes 1048608 | tf_op jit(solution)/shard_map/ppermute | solution.py:10
  202.5 23.7 %collective-permute-done.3 = f32[512,512]{0,1:T(8,128)S(1)} collective-permute-done((f32[512,512]{0,1:T(8,128)S(1)}, f32[512,512]{0,1:T(8,128)S(1)}, u32[]{:S(2)}, u32[]{:S(2)}) %collective-permute-start.3) | collective-permute-done | bytes 1048608 | tf_op jit(solution)/shard_map/ppermute | solution.py:10
  228.0 23.0 %collective-permute-done.4 = f32[512,512]{0,1:T(8,128)} collective-permute-done((f32[512,512]{0,1:T(8,128)S(1)}, f32[512,512]{0,1:T(8,128)}, u32[]{:S(2)}, u32[]{:S(2)}) %collective-permute-start.4) | collective-permute-done | bytes 1048608 | tf_op jit(solution)/shard_map/ppermute | solution.py:10
  254.0 11.7 %cholesky.286 = f32[128,128]{1,0:T(8,128)S(1)} custom-call(f32[128,128]{1,0:T(8,128)S(1)} %cholesky.426), custom_call_target="Cholesky" | custom-call | tf_op jit(solution)/shard_map/jit(cholesky)/cholesky | solution.py:38
  265.9 9.8 custom-call.27
  278.2 12.1 %cholesky.305 = f32[128,128]{1,0:T(8,128)S(1)} custom-call(f32[128,128]{1,0:T(8,128)S(1)} %cholesky.430), custom_call_target="Cholesky" | custom-call | tf_op jit(solution)/shard_map/jit(cholesky)/cholesky | solution.py:38
  291.7 9.8 custom-call.28
  303.1 11.7 %cholesky.326 = f32[128,128]{1,0:T(8,128)S(1)} custom-call(f32[128,128]{1,0:T(8,128)S(1)} %cholesky.435), custom_call_target="Cholesky" | custom-call | tf_op jit(solution)/shard_map/jit(cholesky)/cholesky | solution.py:38
  315.5 9.8 custom-call.29
  326.8 11.9 %cholesky.343 = f32[128,128]{1,0:T(8,128)S(1)} custom-call(f32[128,128]{1,0:T(8,128)S(1)} %convolution_subtract_fusion.11), custom_call_target="Cholesky" | custom-call | tf_op jit(solution)/shard_map/jit(cholesky)/cholesky | solution.py:38
  342.0 8.5 while.18
  350.5 39.3 %custom-call.30 = f32[4,128,128]{1,2,0:T(8,128)S(1)} custom-call(f32[4,128,128]{2,1,0:T(8,128)S(1)} %get-tuple-element.129), custom_call_target="InvertDiagBlocksLowerTriangular" | custom-call | tf_op jit(solution)/shard_map/triangular_solve/custom-call.3 | solution.py:39
  395.5 45.8 %all-gather.2.cloned.1.call-done = bf16[2048,512]{0,1:T(8,128)(2,1)} async-done(((bf16[512,512]{0,1:T(8,128)(2,1)}), bf16[2048,512]{0,1:T(8,128)(2,1)}) %all-gather.2.cloned.1.call-update) | async-done | bytes 2097168 | tf_op jit(solution)/shard_map/all_gather | solution.py:46
  446.7 221.7 %while.17 = (s32[]{:T(128)}, f32[16,128,512]{2,1,0:T(8,128)}, s32[16,16]{1,0:T(8,128)}, bf16[16,16,128,128]{3,2,1,0:T(8,128)(2,1)}, bf16[16,128,512]{2,1,0:T(8,128)(2,1)S(1)}, /*index=5*/f32[16,16]{1,0:T(8,128)S(1)}, s32[]{:T(128)}) while((s32[]{:T(128)}, f32[16,128,512]{2,1,0:T(8,128)}, s32[16,16]{1,0:T(8,128)}, ...), condition=%wide.region_11.15_spmd, body=%wide.region_9.14_spmd.sunk | while | flops 270532672 | bytes 17434516 | solution.py:57
  446.8 3.7 convolution_multiply_fusion.2
  451.2 9.6 scatter_fusion
  460.8 3.7 convolution_multiply_fusion.2
  465.2 9.5 scatter_fusion
  474.7 3.7 convolution_multiply_fusion.2
  479.1 9.3 scatter_fusion
  488.4 3.7 convolution_multiply_fusion.2
  492.8 9.4 scatter_fusion
  502.2 3.7 convolution_multiply_fusion.2
  506.6 9.3 scatter_fusion
  520.4 9.6 scatter_fusion
  534.3 9.3 scatter_fusion
  543.7 3.7 convolution_multiply_fusion.2
  548.1 9.5 scatter_fusion
  557.6 3.7 convolution_multiply_fusion.2
  562.0 9.3 scatter_fusion
  571.3 3.7 convolution_multiply_fusion.2
  575.7 9.4 scatter_fusion
  585.1 3.7 convolution_multiply_fusion.2
  589.5 9.6 scatter_fusion
  599.1 3.7 convolution_multiply_fusion.2
  603.5 9.4 scatter_fusion
  613.0 3.7 convolution_multiply_fusion.2
  617.4 9.4 scatter_fusion
  626.7 3.7 convolution_multiply_fusion.2
  631.1 9.6 scatter_fusion
  640.7 3.7 convolution_multiply_fusion.2
  645.1 9.3 scatter_fusion
  658.8 9.7 scatter_fusion
  668.5 88.3 %all-reduce.2 = bf16[16,128,512]{2,1,0:T(8,128)(2,1)S(1)} all-reduce(f32[16,128,512]{2,1,0:T(8,128)} %get-tuple-element.114), channel_id=1, replica_groups=mesh['row'=8,'col'=4] {'row'}, use_global_device_ids=true, to_apply=%region_12.16 | all-reduce | flops 1048576 | bytes 6291456 | tf_op jit(solution)/shard_map/psum | solution.py:60
  756.8 13.7 %gather_fusion.1 = bf16[256,128,512]{2,1,0:T(8,128)(2,1)} fusion(bf16[16,128,512]{2,1,0:T(8,128)(2,1)S(1)} %all-reduce.2, s32[1024]{0:T(1024)S(1)} %pad_clamp_fusion), kind=kCustom, calls=%fused_computation.1.clone | custom fusion | bytes 67109888 | tf_op jit(solution)/shard_map/jit(_take)/gather | solution.py:24
  770.5 19.4 %fusion.8 = f32[16,512,128,1]{1,2,3,0:T(8,128)} fusion(bf16[16,16,128,128]{3,2,1,0:T(8,128)(2,1)} %get-tuple-element.379, bf16[16,16,128,512]{3,2,1,0:T(8,128)(2,1)} %bitcast.152, pred[16,16]{1,0:T(8,128)(4,1)S(1)} %get-tuple-element.199, bf16[16,16]{1,0:T(8,128)(2,1)S(1)} %get-tuple-element.194), kind=kOutput, calls=%fused_computation.20 | convolution fusion | flops 4378853376 | bytes 46138112 | tf_op jit(solution)/shard_map/rsab,rsbk->rak/dot_general | solution.py:25
  790.0 74.4 %reduce-scatter.5.cloned.1.call-done = f32[512,512]{1,0:T(8,128)} async-done(((f32[2048,512]{1,0:T(8,128)}), f32[512,512]{1,0:T(8,128)}) %reduce-scatter.5.cloned.1.call-update) | async-done | bytes 1048592 | tf_op jit(solution)/shard_map/reduce_scatter | solution.py:28
  869.4 23.1 %collective-permute-done.5 = f32[512,512]{0,1:T(8,128)S(1)} collective-permute-done((f32[512,512]{0,1:T(8,128)S(1)}, f32[512,512]{0,1:T(8,128)S(1)}, u32[]{:S(2)}, u32[]{:S(2)}) %collective-permute-start.5) | collective-permute-done | bytes 1048608 | tf_op jit(solution)/shard_map/ppermute | solution.py:10
  896.0 44.7 %collective-permute-done.6 = f32[512,512]{0,1:T(8,128)S(1)} collective-permute-done((f32[512,512]{0,1:T(8,128)S(1)}, f32[512,512]{0,1:T(8,128)S(1)}, u32[]{:S(2)}, u32[]{:S(2)}) %collective-permute-start.6) | collective-permute-done | bytes 1048608 | tf_op jit(solution)/shard_map/ppermute | solution.py:10
  945.4 23.7 %collective-permute-done.8 = f32[512,512]{0,1:T(8,128)S(1)} collective-permute-done((f32[512,512]{0,1:T(8,128)S(1)}, f32[512,512]{0,1:T(8,128)S(1)}, u32[]{:S(2)}, u32[]{:S(2)}) %collective-permute-start.8) | collective-permute-done | bytes 1048608 | tf_op jit(solution)/shard_map/ppermute | solution.py:10
  970.8 22.9 %collective-permute-done.9 = f32[512,512]{0,1:T(8,128)S(1)} collective-permute-done((f32[512,512]{0,1:T(8,128)S(1)}, f32[512,512]{0,1:T(8,128)S(1)}, u32[]{:S(2)}, u32[]{:S(2)}) %collective-permute-start.9) | collective-permute-done | bytes 1048608 | tf_op jit(solution)/shard_map/ppermute | solution.py:10
  995.5 11.7 %cholesky.358 = f32[128,128]{1,0:T(8,128)S(1)} custom-call(f32[128,128]{1,0:T(8,128)S(1)} %cholesky.439), custom_call_target="Cholesky" | custom-call | tf_op jit(solution)/shard_map/jit(cholesky)/cholesky | solution.py:38
  1008.3 9.8 custom-call.31
  1021.3 11.9 %cholesky.377 = f32[128,128]{1,0:T(8,128)S(1)} custom-call(f32[128,128]{1,0:T(8,128)S(1)} %cholesky.443), custom_call_target="Cholesky" | custom-call | tf_op jit(solution)/shard_map/jit(cholesky)/cholesky | solution.py:38
  1035.2 9.8 custom-call.32
  1047.4 11.7 %cholesky.398 = f32[128,128]{1,0:T(8,128)S(1)} custom-call(f32[128,128]{1,0:T(8,128)S(1)} %cholesky.448), custom_call_target="Cholesky" | custom-call | tf_op jit(solution)/shard_map/jit(cholesky)/cholesky | solution.py:38
  1060.4 9.8 custom-call.33
  1072.5 11.9 %cholesky.415 = f32[128,128]{1,0:T(8,128)S(1)} custom-call(f32[128,128]{1,0:T(8,128)S(1)} %convolution_subtract_fusion.10), custom_call_target="Cholesky" | custom-call | tf_op jit(solution)/shard_map/jit(cholesky)/cholesky | solution.py:38
  1091.0 11.5 while.19
  1103.2 40.1 %custom-call.34 = f32[4,128,128]{1,2,0:T(8,128)S(1)} custom-call(f32[4,128,128]{2,1,0:T(8,128)} %copy-done.6), custom_call_target="InvertDiagBlocksLowerTriangular" | custom-call | tf_op jit(solution)/shard_map/triangular_solve/custom-call.3 | solution.py:39
  (173 shorter events, 126.4 us)
Async XLA Ops:
  7.2 1.8 copy-start
  7.2 114.4 %reduce-scatter.3.cloned.1.call-start = ((), (), s32[]{:S(2)}) async-start(), calls=%async_computation.2 | async-start | bytes 5242880 | tf_op jit(solution)/shard_map/reduce_scatter | solution.py:28
  41.8 399.6 %all-gather.2.cloned.1.call-start = ((), (), s32[]{:S(2)}) async-start(), calls=%async_computation.3 | async-start | bytes 2621440 | tf_op jit(solution)/shard_map/all_gather | solution.py:46
  125.0 24.7 %collective-permute-start = (f32[512,512]{0,1:T(8,128)S(1)}, f32[512,512]{0,1:T(8,128)S(1)}, u32[]{:S(2)}, u32[]{:S(2)}) collective-permute-start(f32[512,512]{0,1:T(8,128)S(1)} %fusion.93), channel_id=1, source_target_pairs={{0,1},{1,0},{2,3},{3,2},{4,5},{5,4},{6,7},{7,6},{8,9},{9,8},{10,11... | collective-permute-start | bytes 3145736 | tf_op jit(solution)/shard_map/ppermute | solution.py:10
  149.9 48.0 %collective-permute-start.1 = (f32[512,512]{0,1:T(8,128)S(1)}, f32[512,512]{0,1:T(8,128)S(1)}, u32[]{:S(2)}, u32[]{:S(2)}) collective-permute-start(f32[512,512]{0,1:T(8,128)S(1)} %add.113), channel_id=1, source_target_pairs={{0,2},{1,3},{2,0},{3,1},{4,6},{5,7},{6,4},{7,5},{8,10},{9,11},{10,... | collective-permute-start | bytes 3145736 | tf_op jit(solution)/shard_map/ppermute | solution.py:10
  198.1 2.7 collective-permute-start.2
  201.0 25.3 %collective-permute-start.3 = (f32[512,512]{0,1:T(8,128)S(1)}, f32[512,512]{0,1:T(8,128)S(1)}, u32[]{:S(2)}, u32[]{:S(2)}) collective-permute-start(f32[512,512]{0,1:T(8,128)S(1)} %add.115), channel_id=1, source_target_pairs={{0,8},{1,9},{2,10},{3,11},{4,12},{5,13},{6,14},{7,15},{8,0},{9,1},... | collective-permute-start | bytes 3145736 | tf_op jit(solution)/shard_map/ppermute | solution.py:10
  226.5 163.4 %copy-start.2 = (f32[512,512]{1,0:T(8,128)S(1)}, f32[512,512]{1,0:T(8,128)}, u32[]{:S(2)}) copy-start(f32[512,512]{1,0:T(8,128)} %reduce-scatter.3.cloned.1.call-done) | copy-start | bytes 3145732
  226.5 24.5 %collective-permute-start.4 = (f32[512,512]{0,1:T(8,128)S(1)}, f32[512,512]{0,1:T(8,128)}, u32[]{:S(2)}, u32[]{:S(2)}) collective-permute-start(f32[512,512]{0,1:T(8,128)S(1)} %add.116), channel_id=1, source_target_pairs={{0,16},{1,17},{2,18},{3,19},{4,20},{5,21},{6,22},{7,23},{8,24},{9,... | collective-permute-start | bytes 3145736 | tf_op jit(solution)/shard_map/ppermute | solution.py:10
  253.0 1.0 copy-start.4
  395.5 468.9 %reduce-scatter.5.cloned.1.call-start = ((), (), s32[]{:S(2)}) async-start(), calls=%async_computation.4 | async-start | bytes 5242880 | tf_op jit(solution)/shard_map/reduce_scatter | solution.py:28
  867.8 24.7 %collective-permute-start.5 = (f32[512,512]{0,1:T(8,128)S(1)}, f32[512,512]{0,1:T(8,128)S(1)}, u32[]{:S(2)}, u32[]{:S(2)}) collective-permute-start(f32[512,512]{0,1:T(8,128)S(1)} %fusion.94), channel_id=1, source_target_pairs={{0,1},{1,0},{2,3},{3,2},{4,5},{5,4},{6,7},{7,6},{8,9},{9,8},{10,11... | collective-permute-start | bytes 3145736 | tf_op jit(solution)/shard_map/ppermute | solution.py:10
  892.7 47.9 %collective-permute-start.6 = (f32[512,512]{0,1:T(8,128)S(1)}, f32[512,512]{0,1:T(8,128)S(1)}, u32[]{:S(2)}, u32[]{:S(2)}) collective-permute-start(f32[512,512]{0,1:T(8,128)S(1)} %add.118), channel_id=1, source_target_pairs={{0,2},{1,3},{2,0},{3,1},{4,6},{5,7},{6,4},{7,5},{8,10},{9,11},{10,... | collective-permute-start | bytes 3145736 | tf_op jit(solution)/shard_map/ppermute | solution.py:10
  940.9 2.7 collective-permute-start.7
  943.8 25.3 %collective-permute-start.8 = (f32[512,512]{0,1:T(8,128)S(1)}, f32[512,512]{0,1:T(8,128)S(1)}, u32[]{:S(2)}, u32[]{:S(2)}) collective-permute-start(f32[512,512]{0,1:T(8,128)S(1)} %add.120), channel_id=1, source_target_pairs={{0,8},{1,9},{2,10},{3,11},{4,12},{5,13},{6,14},{7,15},{8,0},{9,1},... | collective-permute-start | bytes 3145736 | tf_op jit(solution)/shard_map/ppermute | solution.py:10
  969.3 174.0 %copy-start.3 = (f32[512,512]{1,0:T(8,128)S(1)}, f32[512,512]{1,0:T(8,128)}, u32[]{:S(2)}) copy-start(f32[512,512]{1,0:T(8,128)} %reduce-scatter.5.cloned.1.call-done) | copy-start | bytes 3145732
  969.3 24.4 %collective-permute-start.9 = (f32[512,512]{0,1:T(8,128)S(1)}, f32[512,512]{0,1:T(8,128)S(1)}, u32[]{:S(2)}, u32[]{:S(2)}) collective-permute-start(f32[512,512]{0,1:T(8,128)S(1)} %add.121), channel_id=1, source_target_pairs={{0,16},{1,17},{2,18},{3,19},{4,20},{5,21},{6,22},{7,23},{8,24},{9,... | collective-permute-start | bytes 3145736 | tf_op jit(solution)/shard_map/ppermute | solution.py:10
  994.5 1.0 copy-start.5
  1070.2 84.5 %copy-start.1 = (bf16[2048,512]{1,0:T(8,128)(2,1)S(1)}, bf16[2048,512]{1,0:T(8,128)(2,1)}, u32[]{:S(2)}) copy-start(bf16[2048,512]{1,0:T(8,128)(2,1)} %param.14) | copy-start | bytes 6291460
  1102.5 0.7 copy-start.6
Sparse Core Ops, SparseCore 0:
  41.9 79.6 reduce-scatter.2
  395.6 45.7 all-gather.1
  790.1 74.2 reduce-scatter.4
where the time goes:
time: 1170 us; the launch traced here: 1160 us
  waiting for transfers between devices  434 us (37%)
  other arithmetic  412 us (35%)
  matrix products  130 us (11%)
  blocking collectives  88.3 us (8%)
  local copies, waits for them, and re-layouts  61.3 us (5%)
  between operations  19.6 us (2%)
  starting transfers between devices  16.2 us (1%)
    ppermute x10, waiting for transfers between devices, swapped(): return lax.ppermute(value, axis, pairs)  234 us
    another operation x30, other arithmetic, orthonormal(): lower = jnp.linalg.cholesky(gram / total_rows)  161 us
    reduce_scatter x2, waiting for transfers between devices, project_rows(): lax.psum_scatter(matrix_product.reshape(many * tile, width), 'col', scatt...  154 us
    scatter-add x16, other arithmetic, accumulate(): return total.at[col_index[index]].add(matrix_product)  151 us
    psum x1, blocking collectives, local(): back = lax.psum(back_part, 'row').astype(jnp.bfloat16)  88.3 us
    another operation x5, other arithmetic, orthonormal(): lax.linalg.triangular_solve(lower, panel, left_side=False, lower=True, tr...  79.6 us
    dot_general x16, matrix products, accumulate(): jnp.einsum('sab,ak->sbk', tiles[index], q_local[index], preferred_element...  59.4 us
    all_gather x1, waiting for transfers between devices, local(): lax.all_gather(first_q.astype(jnp.bfloat16), 'col', axis=0, tiled=True)  45.8 us
  transfers between devices with their start and end apart: 13, of which 13 were waited for; matrix products, arithmetic and copies ran while one was open for 0% of the time, Pallas kernels for 0%

commit v1 on v0

v1 whole, which is shorter than its diff:
```python
import functools

import jax
import jax.numpy as jnp
from jax import lax
from jax.experimental import pallas as pl
from jax.experimental.pallas import tpu as pltpu
from jax.sharding import PartitionSpec as P

HI = lax.Precision.HIGHEST
NT = (((1,), (1,)), ((), ()))
TN = (((0,), (0,)), ((), ()))


def forward_body(group, base, idx_ref, cnt_ref, t_ref, x_ref, o_ref, acc_ref):
    tile = t_ref.shape[2]
    row = pl.program_id(0) + base
    count = cnt_ref[row]
    acc_ref[...] = jnp.zeros_like(acc_ref)

    def step(p, carry):
        lhs, rhs = [], []
        for q in range(group):
            s = p * group + q
            t = t_ref[0, s]
            lhs.append(t if q == 0 else jnp.where(s < count, t, jnp.zeros_like(t)))
            c = pl.multiple_of(idx_ref[row, s] * tile, tile)
            rhs.append(x_ref[pl.ds(c, tile), :])
        acc_ref[...] += jnp.dot(
            jnp.concatenate(lhs, 1), jnp.concatenate(rhs, 0), preferred_element_type=jnp.float32
        )
        return carry

    lax.fori_loop(0, (count + group - 1) // group, step, 0)
    o_ref[...] = acc_ref[...]


def forward(tiles, col_index, counts, x, base, rows):
    slots, tile = tiles.shape[1], tiles.shape[2]
    width = x.shape[1]
    group = next(g for g in (8, 4, 2, 1) if slots % g == 0)
    return pl.pallas_call(
        functools.partial(forward_body, group, base),
        out_shape=jax.ShapeDtypeStruct((rows * tile, width), jnp.float32),
        grid_spec=pltpu.PrefetchScalarGridSpec(
            num_scalar_prefetch=2,
            grid=(rows,),
            in_specs=[
                pl.BlockSpec((1, slots, tile, tile), lambda r, *_: (r + base, 0, 0, 0)),
                pl.BlockSpec(x.shape, lambda r, *_: (0, 0)),
            ],
            out_specs=pl.BlockSpec((tile, width), lambda r, *_: (r, 0)),
            scratch_shapes=[pltpu.VMEM((tile, width), jnp.float32)],
        ),
        name="forward_rows",
    )(col_index, counts, tiles, x)


def backward_body(group, idx_ref, cnt_ref, t_ref, f_ref, z_ref):
    tile = t_ref.shape[2]
    row = pl.program_id(0)
    count = cnt_ref[row]

    @pl.when(row == 0)
    def _():
        z_ref[...] = jnp.zeros_like(z_ref)

    def step(p, carry):
        lhs = []
        for q in range(group):
            s = p * group + q
            t = t_ref[0, s]
            lhs.append(t if q == 0 else jnp.where(s < count, t, jnp.zeros_like(t)))
        out = lax.dot_general(
            jnp.concatenate(lhs, 1), f_ref[...], TN, preferred_element_type=jnp.float32
        )
        for q in range(group):
            c = pl.multiple_of(idx_ref[row, p * group + q] * tile, tile)
            z_ref[pl.ds(c, tile), :] += out[q * tile:(q + 1) * tile]
        return carry

    lax.fori_loop(0, (count + group - 1) // group, step, 0)


def backward(tiles, col_index, counts, panel, col_rows):
    rows, slots, tile = tiles.shape[:3]
    width = panel.shape[1]
    group = next(g for g in (4, 2, 1) if slots % g == 0)
    return pl.pallas_call(
        functools.partial(backward_body, group),
        out_shape=jax.ShapeDtypeStruct((col_rows, width), jnp.float32),
        grid_spec=pltpu.PrefetchScalarGridSpec(
            num_scalar_prefetch=2,
            grid=(rows,),
            in_specs=[
                pl.BlockSpec((1, slots, tile, tile), lambda r, *_: (r, 0, 0, 0)),
                pl.BlockSpec((tile, width), lambda r, *_: (r, 0)),
            ],
            out_specs=pl.BlockSpec((col_rows, width), lambda r, *_: (0, 0)),
        ),
        name="backward_rows",
    )(col_index, counts, tiles, panel)


def factor_block(read, r_ref, t_ref, group):
    n = 128
    vr = n // 8
    a = [read(v) for v in range(vr)]
    lane = lax.broadcasted_iota(jnp.int32, (8, n), 1)
    sub = lax.broadcasted_iota(jnp.int32, (8, n), 0)
    e = [(lane == sub + 8 * v).astype(jnp.float32) for v in range(vr)]
    full = lambda x: jnp.broadcast_to(x, (8, n))
    for g in range(n // group):
        j0 = g * group
        v0, o = j0 // 8, j0 % 8
        P = [full(a[v0][o + k:o + k + 1, :]) for k in range(group)]
        PE = [full(e[v0][o + k:o + k + 1, :]) for k in range(group)]
        el = [[full(P[i][:, j0 + k:j0 + k + 1]) for k in range(i + 1)] for i in range(group)]
        vs = [v for v in range(vr) if v > v0 or (v == v0 and o + group < 8)]
        mult = {v: [full(a[v][:, j0 + k:j0 + k + 1]) for k in range(group)] for v in vs}
        R, RE, S = [], [], []
        W = [None] * group
        WE = [None] * group
        L = [[None] * group for _ in range(group)]
        for c in range(group):
            inv = lax.rsqrt(el[c][c])
            for i in range(c + 1, group):
                L[i][c] = el[i][c] * inv
            for i in range(c + 1, group):
                for k in range(c + 1, i + 1):
                    el[i][k] = el[i][k] - L[i][c] * L[k][c]
            s = []
            for k in range(c):
                t = L[c][k] * S[k][k]
                for j in range(k + 1, c):
                    t = t + L[c][j] * S[j][k]
                s.append(-(t * inv))
            s.append(inv)
            S.append(s)
            r = P[c] * s[c]
            re = PE[c] * s[c]
            for k in range(c):
                r = r + P[k] * s[k]
                re = re + PE[k] * s[k]
            R.append(r); RE.append(re)
            for k in range(c + 1):
                W[k] = s[k] * r if W[k] is None else W[k] + s[k] * r
                WE[k] = s[k] * re if WE[k] is None else WE[k] + s[k] * re
            r_ref[j0 + c:j0 + c + 1, :] = r[0:1, :]
            t_ref[j0 + c:j0 + c + 1, :] = re[0:1, :]
        for v in vs:
            u = mult[v][0] * W[0]
            ue = mult[v][0] * WE[0]
            for k in range(1, group):
                u = u + mult[v][k] * W[k]
                ue = ue + mult[v][k] * WE[k]
            a[v] = a[v] - u
            e[v] = e[v] - ue


def chol_body(scale, group, g_ref, r_ref, t_ref, a_ref, rk_ref, tk_ref):
    n = g_ref.shape[0]
    b = 128
    a_ref[...] = g_ref[...] * scale
    rows = lax.broadcasted_iota(jnp.int32, (n, n), 0)
    cols = lax.broadcasted_iota(jnp.int32, (n, n), 1)
    t_ref[...] = jnp.where(rows == cols, 1.0, 0.0).astype(jnp.float32)

    def block(k, carry):
        at = pl.multiple_of(k * b, b)
        factor_block(lambda v: a_ref[pl.ds(pl.multiple_of(at + 8 * v, 8), 8), pl.ds(at, b)], rk_ref, tk_ref, group)
        inv = tk_ref[...]
        rp = jnp.dot(inv, a_ref[pl.ds(at, b), :], precision=HI, preferred_element_type=jnp.float32)
        ep = jnp.dot(inv, t_ref[pl.ds(at, b), :], precision=HI, preferred_element_type=jnp.float32)
        row = lax.broadcasted_iota(jnp.int32, rp.shape, 0) + at
        col = lax.broadcasted_iota(jnp.int32, rp.shape, 1)
        r_ref[pl.ds(at, b), :] = jnp.where(col >= row, rp, 0.0)
        t_ref[pl.ds(at, b), :] = jnp.where(col <= row, ep, 0.0)

        def below(i, carry):
            to = pl.multiple_of(i * b, b)
            l = r_ref[pl.ds(at, b), pl.ds(to, b)]
            a_ref[pl.ds(to, b), :] -= lax.dot_general(l, r_ref[pl.ds(at, b), :], TN, precision=HI, preferred_element_type=jnp.float32)
            t_ref[pl.ds(to, b), :] -= lax.dot_general(l, t_ref[pl.ds(at, b), :], TN, precision=HI, preferred_element_type=jnp.float32)
            return carry
        lax.fori_loop(k + 1, n // b, below, 0)
        return carry
    lax.fori_loop(0, n // b, block, 0)


def cholesky(gram, scale, group=8):
    n = gram.shape[0]
    s = jax.ShapeDtypeStruct((n, n), jnp.float32)
    return pl.pallas_call(
        functools.partial(chol_body, scale, group),
        out_shape=(s, s),
        scratch_shapes=[pltpu.VMEM((n, n), jnp.float32), pltpu.VMEM((128, 128), jnp.float32), pltpu.VMEM((128, 128), jnp.float32)],
        name="factorize",
    )(gram)


def line_sum(value, wire):
    n = lax.axis_size("col")
    z = lax.axis_index("col")
    for s in range(n // 2 - 1):
        pairs = [(s, s + 1), (n - 1 - s, n - 2 - s)]
        value = value + lax.ppermute(value.astype(wire), "col", pairs).astype(value.dtype)
    pairs = [(n // 2 - 1, n // 2), (n // 2, n // 2 - 1)]
    value = value + lax.ppermute(value.astype(wire), "col", pairs).astype(value.dtype)
    value = value.astype(wire)
    for s in reversed(range(n // 2 - 1)):
        pairs = [(s + 1, s), (n - 2 - s, n - 1 - s)]
        got = lax.ppermute(value, "col", pairs)
        value = jnp.where((z == s) | (z == n - 1 - s), got, value)
    return value


def halving(bits):
    size = 2**bits
    me = lax.axis_index("row")
    odd = me & 1
    for step in range(bits):
        even_bit = step
        odd_bit = 0 if step == 0 else bits - step
        pairs = [(i, i ^ (1 << (odd_bit if i & 1 else even_bit))) for i in range(size)]
        own = jnp.where(odd == 1, (me >> odd_bit) & 1, (me >> even_bit) & 1)
        yield pairs, own


def row_scatter(value, wires):
    bits = lax.axis_size("row").bit_length() - 1
    offset = jnp.int32(0)
    for step, (pairs, own) in enumerate(halving(bits)):
        half = value.shape[0] // 2
        give = lax.dynamic_slice_in_dim(value, (1 - own) * half, half, 0).astype(wires[min(step, len(wires) - 1)])
        keep = lax.dynamic_slice_in_dim(value, own * half, half, 0)
        value = keep + lax.ppermute(give, "row", pairs).astype(value.dtype)
        offset = offset + own * half
    return value, offset


def row_gather(part, offset, total):
    bits = lax.axis_size("row").bit_length() - 1
    steps = list(halving(bits))
    for pairs, own in reversed(steps):
        got = lax.ppermute(part, "row", pairs)
        low = jnp.where(own == 0, part, got)
        high = jnp.where(own == 0, got, part)
        part = jnp.concatenate([low, high], 0)
    return part


def gram_sum(gram):
    part, offset = row_scatter(gram, (jnp.float32,))
    part = line_sum(part, jnp.float32)
    return row_gather(part, offset, gram.shape[0])


def line_scatter(value):
    n = lax.axis_size("col")
    z = lax.axis_index("col")
    share = value.shape[0] // n

    def own(q):
        return lax.dynamic_slice_in_dim(value, jnp.clip(q, 0, n - 1) * share, share, 0)

    right = left = None
    for t in range(1, n):
        up = own(n - 1 - (t - 1 - z))
        down = own(t - 1 - (n - 1 - z))
        if right is not None:
            up = up + right.astype(up.dtype)
            down = down + left.astype(down.dtype)
        wire = jnp.float32 if t == n - 1 else jnp.bfloat16
        right = lax.ppermute(up.astype(wire), "col", [(i, i + 1) for i in range(t)])
        left = lax.ppermute(down.astype(wire), "col", [(n - 1 - i, n - 2 - i) for i in range(t)])
    return own(z) + right.astype(value.dtype) + left.astype(value.dtype)


def local(tiles, col_index, counts, sketch):
    tile_rows, slots, tile = tiles.shape[:3]
    n_col = lax.axis_size("col")
    total_rows = tile_rows * tile * lax.axis_size("row")
    counts = counts.reshape(-1)
    z = lax.axis_index("col")

    chunk = tile_rows // n_col
    firsts = []
    for j in range(n_col):
        part = forward(tiles, col_index, counts, sketch, j * chunk, chunk)
        firsts.append(line_sum(part, jnp.bfloat16))
    first = jnp.concatenate(firsts, 0)

    share = first.shape[0] // n_col
    mine = lax.dynamic_slice_in_dim(first, z * share, share, 0)
    gram = lax.dot_general(mine, mine, TN, preferred_element_type=jnp.float32)
    unused, inverse = cholesky(gram_sum(gram), 1.0 / total_rows)

    back = backward(tiles, col_index, counts, first, sketch.shape[0])
    part, offset = row_scatter(back, (jnp.float32, jnp.bfloat16, jnp.float32))
    part = lax.dot_general(part, inverse, NT, precision=HI, preferred_element_type=jnp.float32)
    back = row_gather(part.astype(jnp.bfloat16), offset, sketch.shape[0])

    second = line_scatter(forward(tiles, col_index, counts, back, 0, tile_rows))
    gram = lax.dot_general(second, second, TN, precision=HI, preferred_element_type=jnp.float32)
    factor, inverse = cholesky(gram_sum(gram), 1.0 / total_rows)
    basis = lax.dot_general(second, inverse, NT, precision=HI, preferred_element_type=jnp.float32)
    return (basis, factor)


def solution(mesh):
    return jax.shard_map(
        local,
        mesh=mesh,
        in_specs=(P("row", "col", None, None), P("row", "col"), P("row", "col"), P("col", None)),
        out_specs=(P(("row", "col"), None), P()),
        check_vma=False,
    )
```

time: 1170 us -> 433 us (0.37)
  other arithmetic: 412 us -> 35.6 us
  waiting for transfers between devices: 434 us -> 200 us
  matrix products: 130 us -> 8.67 us
  Pallas kernels: 0 us -> 120 us
  blocking collectives: 88.3 us -> 0 us
  local copies, waits for them, and re-layouts: 61.3 us -> 5.49 us
  starting transfers between devices: 16.2 us -> 58.9 us
  between operations: 19.6 us -> 1.41 us
    another operation x35 -> x0, other arithmetic: 240 us -> none  [the longest x30 161 us: orthonormal(): lower = jnp.linalg.cholesky(gram / total_rows)]
    reduce_scatter x2 -> x0, waiting for transfers between devices: 154 us -> none  [project_rows(): lax.psum_scatter(matrix_product.reshape(many * tile, width), 'col', scatt...]
    scatter-add x16 -> x0, other arithmetic: 151 us -> none  [accumulate(): return total.at[col_index[index]].add(matrix_product)]
    pallas_call x0 -> x8, Pallas kernels: none -> 120 us  [the longest x2 60.4 us: cholesky(): pl.pallas_call(functools.partial(chol_body, scale, group), out_shape=(s,...]
    dot_general x20 -> x4, matrix products: 105 us -> 8.67 us  [the longest x1 4.05 us: local(): lax.dot_general(second, inverse, NT, precision=HI, preferred_element_type...]
    psum x1 -> x0, blocking collectives: 88.3 us -> none  [local(): back = lax.psum(back_part, 'row').astype(jnp.bfloat16)]
    all_gather x1 -> x0, waiting for transfers between devices: 45.8 us -> none  [local(): lax.all_gather(first_q.astype(jnp.bfloat16), 'col', axis=0, tiled=True)]
    ppermute x10 -> x42, starting transfers between devices: 15.9 us -> 58.9 us  [the longest x12 20 us: line_sum(): lax.ppermute(value.astype(wire), 'col', pairs).astype(value.dtype)]
  transfers between devices with their start and end apart: 13 -> 42, of which waited for: 13 -> 28; matrix products, arithmetic and copies ran while one was open for 0% -> 7% of each run, Pallas kernels for 0% -> 16%
where the time goes in v1:
time: 433 us; the launch traced here: 430 us
  waiting for transfers between devices  200 us (46%)
  Pallas kernels  120 us (28%)
  starting transfers between devices  58.9 us (14%)
  other arithmetic  35.6 us (8%)
  matrix products  8.67 us (2%)
  local copies, waits for them, and re-layouts  5.49 us (1%)
    ppermute x6, waiting for transfers between devices, line_sum(): got = lax.ppermute(value, 'col', pairs)  66.9 us
    pallas_call x2, Pallas kernels, cholesky(): pl.pallas_call(functools.partial(chol_body, scale, group), out_shape=(s,...  60.4 us
    pallas_call x5, Pallas kernels, forward(): pl.pallas_call(functools.partial(forward_body, group, base), out_shape=ja...  40.6 us
    ppermute x9, waiting for transfers between devices, row_gather(): got = lax.ppermute(part, 'row', pairs)  39.7 us
    ppermute x3, waiting for transfers between devices, line_scatter(): right = lax.ppermute(up.astype(wire), 'col', [(i, i + 1) for i in range(t)])  36.8 us
    ppermute x9, waiting for transfers between devices, row_scatter(): value = keep + lax.ppermute(give, 'row', pairs).astype(value.dtype)  27.3 us
    ppermute x12, starting transfers between devices, line_sum(): lax.ppermute(value.astype(wire), 'col', pairs).astype(value.dtype)  20 us
    pallas_call x1, Pallas kernels, backward(): pl.pallas_call(functools.partial(backward_body, group), out_shape=jax.Sha...  19 us
  transfers between devices with their start and end apart: 42, of which 28 were waited for; matrix products, arithmetic and copies ran while one was open for 7% of the time, Pallas kernels for 16%

profile of v1, /device:TPU:0, one launch (start us, length us, event | category | flops | bytes accessed | tf_op | source)
XLA Modules:
  0.0 430.4 jit_solution(8105908379756571712)
XLA Ops:
  0.6 6.1 %forward_rows.8 = f32[512,512]{1,0:T(8,128)} custom-call(s32[16,16]{1,0:T(8,128)} %idx_ref.11, s32[16]{0:T(128)} %bitcast.6, bf16[16,16,128,128]{3,2,1,0:T(8,128)(2,1)} %t_ref.11, bf16[2048,512]{1,0:T(8,128)(2,1)} %x_ref.7), custom_call_target="tpu_custom_call" | custom-call | tf_op jit(solution)/shard_map/forward_rows/pallas_call | solution.py:42
  6.7 2.1 convert_element_type.108
  8.8 6.1 %collective-permute-start.9 = (bf16[512,512]{1,0:T(8,128)(2,1)}, bf16[512,512]{1,0:T(8,128)(2,1)}, u32[]{:S(2)}, u32[]{:S(2)}) collective-permute-start(bf16[512,512]{1,0:T(8,128)(2,1)} %convert_element_type.108), channel_id=1, source_target_pairs={{0,1},{3,2},{4,5},{7,6},{8,9},{11,10},{12,13},{15,14},{16,17},{19,... | collective-permute-start | bytes 1572872 | tf_op jit(solution)/shard_map/ppermute | solution.py:207
  14.9 5.9 %forward_rows.7 = f32[512,512]{1,0:T(8,128)} custom-call(s32[16,16]{1,0:T(8,128)} %idx_ref.11, s32[16]{0:T(128)} %bitcast.7, bf16[16,16,128,128]{3,2,1,0:T(8,128)(2,1)} %t_ref.11, bf16[2048,512]{1,0:T(8,128)(2,1)} %x_ref.7), custom_call_target="tpu_custom_call" | custom-call | tf_op jit(solution)/shard_map/forward_rows/pallas_call | solution.py:42
  20.8 2.1 convert_element_type.103
  22.9 2.1 collective-permute-start.6
  24.9 6.4 %forward_rows.6 = f32[512,512]{1,0:T(8,128)} custom-call(s32[16,16]{1,0:T(8,128)} %idx_ref.11, s32[16]{0:T(128)} %bitcast.8, bf16[16,16,128,128]{3,2,1,0:T(8,128)(2,1)} %t_ref.11, bf16[2048,512]{1,0:T(8,128)(2,1)} %x_ref.7), custom_call_target="tpu_custom_call" | custom-call | tf_op jit(solution)/shard_map/forward_rows/pallas_call | solution.py:42
  31.4 2.1 convert_element_type.98
  33.5 1.3 collective-permute-start.3
  34.8 6.0 %forward_rows.5 = f32[512,512]{1,0:T(8,128)} custom-call(s32[16,16]{1,0:T(8,128)} %idx_ref.11, s32[16]{0:T(128)} %bitcast.9, bf16[16,16,128,128]{3,2,1,0:T(8,128)(2,1)} %t_ref.11, bf16[2048,512]{1,0:T(8,128)(2,1)} %x_ref.7), custom_call_target="tpu_custom_call" | custom-call | tf_op jit(solution)/shard_map/forward_rows/pallas_call | solution.py:42
  40.8 2.2 convert_element_type.93
  49.5 9.5 %collective-permute-done = bf16[512,512]{1,0:T(8,128)(2,1)S(1)} collective-permute-done((bf16[512,512]{1,0:T(8,128)(2,1)}, bf16[512,512]{1,0:T(8,128)(2,1)S(1)}, u32[]{:S(2)}, u32[]{:S(2)}) %collective-permute-start) | collective-permute-done | bytes 524320 | tf_op jit(solution)/shard_map/ppermute | solution.py:207
  68.1 12.0 %collective-permute-done.11 = bf16[512,512]{1,0:T(8,128)(2,1)S(1)} collective-permute-done((bf16[512,512]{1,0:T(8,128)(2,1)S(1)}, bf16[512,512]{1,0:T(8,128)(2,1)S(1)}, u32[]{:S(2)}, u32[]{:S(2)}) %collective-permute-start.11) | collective-permute-done | bytes 524320 | tf_op jit(solution)/shard_map/ppermute | solution.py:213
  80.1 11.2 %collective-permute-done.8 = bf16[512,512]{1,0:T(8,128)(2,1)S(1)} collective-permute-done((bf16[512,512]{1,0:T(8,128)(2,1)S(1)}, bf16[512,512]{1,0:T(8,128)(2,1)S(1)}, u32[]{:S(2)}, u32[]{:S(2)}) %collective-permute-start.8) | collective-permute-done | bytes 524320 | tf_op jit(solution)/shard_map/ppermute | solution.py:213
  91.3 11.2 %collective-permute-done.5 = bf16[512,512]{1,0:T(8,128)(2,1)S(1)} collective-permute-done((bf16[512,512]{1,0:T(8,128)(2,1)S(1)}, bf16[512,512]{1,0:T(8,128)(2,1)S(1)}, u32[]{:S(2)}, u32[]{:S(2)}) %collective-permute-start.5) | collective-permute-done | bytes 524320 | tf_op jit(solution)/shard_map/ppermute | solution.py:213
  102.6 9.7 %collective-permute-done.2 = bf16[512,512]{1,0:T(8,128)(2,1)S(1)} collective-permute-done((bf16[512,512]{1,0:T(8,128)(2,1)S(1)}, bf16[512,512]{1,0:T(8,128)(2,1)S(1)}, u32[]{:S(2)}, u32[]{:S(2)}) %collective-permute-start.2) | collective-permute-done | bytes 524320 | tf_op jit(solution)/shard_map/ppermute | solution.py:213
  114.0 19.0 %backward_rows.1 = f32[2048,512]{1,0:T(8,128)} custom-call(s32[16,16]{1,0:T(8,128)} %idx_ref.11, s32[16]{0:T(128)} %bitcast.10, bf16[16,16,128,128]{3,2,1,0:T(8,128)(2,1)} %t_ref.11, bf16[2048,512]{1,0:T(8,128)(2,1)} %copy-done.4), custom_call_target="tpu_custom_call" | custom-call | tf_op jit(solution)/shard_map/backward_rows/pallas_call | solution.py:89
  133.0 1.8 constant_dynamic-slice_fusion.7
  136.8 4.7 %collective-permute-start.16 = (f32[128,512]{1,0:T(8,128)S(1)}, f32[128,512]{1,0:T(8,128)S(1)}, u32[]{:S(2)}, u32[]{:S(2)}) collective-permute-start(f32[128,512]{1,0:T(8,128)S(1)} %constant_dynamic-slice_fusion.4), channel_id=1, source_target_pairs={{0,8},{4,20},{8,0},{12,28},{16,24},{20,4},{24,16},{28,12},{1,9},{5... | collective-permute-start | bytes 786440 | tf_op jit(solution)/shard_map/ppermute | solution.py:237
  141.5 4.4 %collective-permute-done.16 = f32[128,512]{1,0:T(8,128)S(1)} collective-permute-done((f32[128,512]{1,0:T(8,128)S(1)}, f32[128,512]{1,0:T(8,128)S(1)}, u32[]{:S(2)}, u32[]{:S(2)}) %collective-permute-start.16) | collective-permute-done | bytes 262176 | tf_op jit(solution)/shard_map/ppermute | solution.py:237
  147.0 4.9 %collective-permute-done.17 = f32[64,512]{1,0:T(8,128)S(1)} collective-permute-done((f32[64,512]{1,0:T(8,128)S(1)}, f32[64,512]{1,0:T(8,128)S(1)}, u32[]{:S(2)}, u32[]{:S(2)}) %collective-permute-start.17) | collective-permute-done | bytes 131104 | tf_op jit(solution)/shard_map/ppermute | solution.py:237
  153.3 2.5 collective-permute-done.18
  156.5 1.5 collective-permute-start.20
  158.0 11.4 %collective-permute-done.20 = f32[64,512]{1,0:T(8,128)S(1)} collective-permute-done((f32[64,512]{1,0:T(8,128)S(1)}, f32[64,512]{1,0:T(8,128)S(1)}, u32[]{:S(2)}, u32[]{:S(2)}) %collective-permute-start.20) | collective-permute-done | bytes 131104 | tf_op jit(solution)/shard_map/ppermute | solution.py:213
  169.5 6.3 %collective-permute-done.21 = f32[64,512]{1,0:T(8,128)S(1)} collective-permute-done((f32[64,512]{1,0:T(8,128)S(1)}, f32[64,512]{1,0:T(8,128)S(1)}, u32[]{:S(2)}, u32[]{:S(2)}) %collective-permute-start.21) | collective-permute-done | bytes 131104 | tf_op jit(solution)/shard_map/ppermute | solution.py:246
  175.8 2.1 collective-permute-start.22
  177.9 2.7 dynamic-slice_add_fusion
  180.8 1.6 collective-permute-done.22
  184.3 6.8 %collective-permute-done.13 = bf16[512,512]{1,0:T(8,128)(2,1)} collective-permute-done((bf16[512,512]{1,0:T(8,128)(2,1)S(1)}, bf16[512,512]{1,0:T(8,128)(2,1)}, u32[]{:S(2)}, u32[]{:S(2)}) %collective-permute-start.13) | collective-permute-done | bytes 524320 | tf_op jit(solution)/shard_map/ppermute | solution.py:237
  194.7 30.2 %factorize.2 = (f32[512,512]{1,0:T(8,128)}, f32[512,512]{1,0:T(8,128)}) custom-call(f32[512,512]{1,0:T(8,128)} %pad_maximum_fusion.2.g_ref), custom_call_target="tpu_custom_call" | custom-call | tf_op jit(solution)/shard_map/factorize/pallas_call | solution.py:194
  224.9 2.3 convolution_convert_fusion
  227.2 2.1 collective-permute-start.24
  229.2 7.2 %collective-permute-done.24 = bf16[256,512]{1,0:T(8,128)(2,1)S(1)} collective-permute-done((bf16[256,512]{1,0:T(8,128)(2,1)S(1)}, bf16[256,512]{1,0:T(8,128)(2,1)S(1)}, u32[]{:S(2)}, u32[]{:S(2)}) %collective-permute-start.24) | collective-permute-done | bytes 262176 | tf_op jit(solution)/shard_map/ppermute | solution.py:246
  236.6 9.2 %collective-permute-done.25 = bf16[512,512]{1,0:T(8,128)(2,1)S(1)} collective-permute-done((bf16[512,512]{1,0:T(8,128)(2,1)S(1)}, bf16[512,512]{1,0:T(8,128)(2,1)S(1)}, u32[]{:S(2)}, u32[]{:S(2)}) %collective-permute-start.25) | collective-permute-done | bytes 524320 | tf_op jit(solution)/shard_map/ppermute | solution.py:246
  246.1 2.6 collective-permute-done.26
  249.1 1.5 pad_maximum_fusion.1.x_ref
  250.6 16.2 %forward_rows.9 = f32[2048,512]{1,0:T(8,128)} custom-call(s32[16,16]{1,0:T(8,128)} %idx_ref.11, s32[16]{0:T(128)} %bitcast.11, bf16[16,16,128,128]{3,2,1,0:T(8,128)(2,1)} %t_ref.11, bf16[2048,512]{1,0:T(8,128)(2,1)} %pad_maximum_fusion.1.x_ref), custom_call_target="tpu_custom_call" | custom-call | tf_op jit(solution)/shard_map/forward_rows/pallas_call | solution.py:42
  266.9 1.7 dynamic-slice_convert_fusion.1
  268.5 2.1 collective-permute-start.27
  271.4 10.2 %collective-permute-done.27 = bf16[512,512]{1,0:T(8,128)(2,1)S(1)} collective-permute-done((bf16[512,512]{1,0:T(8,128)(2,1)S(1)}, bf16[512,512]{1,0:T(8,128)(2,1)S(1)}, u32[]{:S(2)}, u32[]{:S(2)}) %collective-permute-start.27) | collective-permute-done | bytes 524320 | tf_op jit(solution)/shard_map/ppermute | solution.py:275
  281.6 1.4 add_convert_fusion.1
  283.0 4.4 %collective-permute-start.28 = (bf16[512,512]{1,0:T(8,128)(2,1)S(1)}, bf16[512,512]{1,0:T(8,128)(2,1)S(1)}, u32[]{:S(2)}, u32[]{:S(2)}) collective-permute-start(bf16[512,512]{1,0:T(8,128)(2,1)S(1)} %add_convert_fusion.1), channel_id=1, source_target_pairs={{0,1},{1,2},{4,5},{5,6},{8,9},{9,10},{12,13},{13,14},{16,17},{17,1... | collective-permute-start | bytes 1572872 | tf_op jit(solution)/shard_map/ppermute | solution.py:275
  287.4 10.0 %collective-permute-done.28 = bf16[512,512]{1,0:T(8,128)(2,1)S(1)} collective-permute-done((bf16[512,512]{1,0:T(8,128)(2,1)S(1)}, bf16[512,512]{1,0:T(8,128)(2,1)S(1)}, u32[]{:S(2)}, u32[]{:S(2)}) %collective-permute-start.28) | collective-permute-done | bytes 524320 | tf_op jit(solution)/shard_map/ppermute | solution.py:275
  297.4 1.9 convert_add_fusion.1
  300.0 5.0 %collective-permute-start.29 = (f32[512,512]{1,0:T(8,128)S(1)}, f32[512,512]{1,0:T(8,128)S(1)}, u32[]{:S(2)}, u32[]{:S(2)}) collective-permute-start(f32[512,512]{1,0:T(8,128)S(1)} %get-tuple-element.8), channel_id=1, source_target_pairs={{0,1},{1,2},{2,3},{4,5},{5,6},{6,7},{8,9},{9,10},{10,11},{12,13},{... | collective-permute-start | bytes 3145736 | tf_op jit(solution)/shard_map/ppermute | solution.py:275
  305.1 2.4 convert_add_fusion
  307.5 1.5 collective-permute-start.32
  309.0 16.5 %collective-permute-done.29 = f32[512,512]{1,0:T(8,128)S(1)} collective-permute-done((f32[512,512]{1,0:T(8,128)S(1)}, f32[512,512]{1,0:T(8,128)S(1)}, u32[]{:S(2)}, u32[]{:S(2)}) %collective-permute-start.29) | collective-permute-done | bytes 1048608 | tf_op jit(solution)/shard_map/ppermute | solution.py:275
  325.5 14.8 %collective-permute-done.32 = f32[512,512]{1,0:T(8,128)S(1)} collective-permute-done((f32[512,512]{1,0:T(8,128)}, f32[512,512]{1,0:T(8,128)S(1)}, u32[]{:S(2)}, u32[]{:S(2)}) %collective-permute-start.32) | collective-permute-done | bytes 1048608 | tf_op jit(solution)/shard_map/ppermute | solution.py:276
  340.3 1.6 add_add_fusion
  341.8 1.9 fusion.10
  343.8 1.9 collective-permute-done.33
  345.9 5.0 %collective-permute-start.34 = (f32[128,512]{1,0:T(8,128)S(1)}, f32[128,512]{1,0:T(8,128)S(1)}, u32[]{:S(2)}, u32[]{:S(2)}) collective-permute-start(f32[128,512]{1,0:T(8,128)S(1)} %constant_dynamic-slice_fusion.1), channel_id=1, source_target_pairs={{0,8},{4,20},{8,0},{12,28},{16,24},{20,4},{24,16},{28,12},{1,9},{5... | collective-permute-start | bytes 786440 | tf_op jit(solution)/shard_map/ppermute | solution.py:237
  350.8 4.4 %collective-permute-done.34 = f32[128,512]{1,0:T(8,128)S(1)} collective-permute-done((f32[128,512]{1,0:T(8,128)S(1)}, f32[128,512]{1,0:T(8,128)S(1)}, u32[]{:S(2)}, u32[]{:S(2)}) %collective-permute-start.34) | collective-permute-done | bytes 262176 | tf_op jit(solution)/shard_map/ppermute | solution.py:237
  355.3 5.0 %collective-permute-done.35 = f32[64,512]{1,0:T(8,128)S(1)} collective-permute-done((f32[64,512]{1,0:T(8,128)S(1)}, f32[64,512]{1,0:T(8,128)S(1)}, u32[]{:S(2)}, u32[]{:S(2)}) %collective-permute-start.35) | collective-permute-done | bytes 131104 | tf_op jit(solution)/shard_map/ppermute | solution.py:237
  360.3 3.6 collective-permute-start.36
  364.0 2.5 collective-permute-done.36
  368.5 11.5 %collective-permute-done.38 = f32[64,512]{1,0:T(8,128)S(1)} collective-permute-done((f32[64,512]{1,0:T(8,128)S(1)}, f32[64,512]{1,0:T(8,128)S(1)}, u32[]{:S(2)}, u32[]{:S(2)}) %collective-permute-start.38) | collective-permute-done | bytes 131104 | tf_op jit(solution)/shard_map/ppermute | solution.py:213
  380.1 6.3 %collective-permute-done.39 = f32[64,512]{1,0:T(8,128)S(1)} collective-permute-done((f32[64,512]{1,0:T(8,128)S(1)}, f32[64,512]{1,0:T(8,128)S(1)}, u32[]{:S(2)}, u32[]{:S(2)}) %collective-permute-start.39) | collective-permute-done | bytes 131104 | tf_op jit(solution)/shard_map/ppermute | solution.py:246
  386.4 1.8 collective-permute-start.40
  388.3 4.6 %collective-permute-done.40 = f32[128,512]{1,0:T(8,128)S(1)} collective-permute-done((f32[128,512]{1,0:T(8,128)S(1)}, f32[128,512]{1,0:T(8,128)S(1)}, u32[]{:S(2)}, u32[]{:S(2)}) %collective-permute-start.40) | collective-permute-done | bytes 262176 | tf_op jit(solution)/shard_map/ppermute | solution.py:246
  393.1 1.9 collective-permute-done.41
  396.1 30.2 %factorize.3 = (f32[512,512]{1,0:T(8,128)}, f32[512,512]{1,0:T(8,128)}) custom-call(f32[512,512]{1,0:T(8,128)} %pad_maximum_fusion.4.g_ref), custom_call_target="tpu_custom_call" | custom-call | tf_op jit(solution)/shard_map/factorize/pallas_call | solution.py:194
  426.3 4.0 fusion.11
  (109 shorter events, 34.3 us)
Async XLA Ops:
  8.8 35.5 %collective-permute-start.9 = (bf16[512,512]{1,0:T(8,128)(2,1)}, bf16[512,512]{1,0:T(8,128)(2,1)}, u32[]{:S(2)}, u32[]{:S(2)}) collective-permute-start(bf16[512,512]{1,0:T(8,128)(2,1)} %convert_element_type.108), channel_id=1, source_target_pairs={{0,1},{3,2},{4,5},{7,6},{8,9},{11,10},{12,13},{15,14},{16,17},{19,... | collective-permute-start | bytes 1572872 | tf_op jit(solution)/shard_map/ppermute | solution.py:207
  22.9 23.6 %collective-permute-start.6 = (bf16[512,512]{1,0:T(8,128)(2,1)}, bf16[512,512]{1,0:T(8,128)(2,1)}, u32[]{:S(2)}, u32[]{:S(2)}) collective-permute-start(bf16[512,512]{1,0:T(8,128)(2,1)} %convert_element_type.103), channel_id=1, source_target_pairs={{0,1},{3,2},{4,5},{7,6},{8,9},{11,10},{12,13},{15,14},{16,17},{19,... | collective-permute-start | bytes 1572872 | tf_op jit(solution)/shard_map/ppermute | solution.py:207
  33.5 15.2 %collective-permute-start.3 = (bf16[512,512]{1,0:T(8,128)(2,1)}, bf16[512,512]{1,0:T(8,128)(2,1)S(1)}, u32[]{:S(2)}, u32[]{:S(2)}) collective-permute-start(bf16[512,512]{1,0:T(8,128)(2,1)} %convert_element_type.98), channel_id=1, source_target_pairs={{0,1},{3,2},{4,5},{7,6},{8,9},{11,10},{12,13},{15,14},{16,17},{19,... | collective-permute-start | bytes 1572872 | tf_op jit(solution)/shard_map/ppermute | solution.py:207
  34.8 9.5 %copy-start.3 = (f32[512,512]{1,0:T(8,128)S(1)}, f32[512,512]{1,0:T(8,128)}, u32[]{:S(2)}) copy-start(f32[512,512]{1,0:T(8,128)} %forward_rows.8) | copy-start | bytes 3145732
  40.8 5.7 %copy-start.2 = (f32[512,512]{1,0:T(8,128)S(1)}, f32[512,512]{1,0:T(8,128)}, u32[]{:S(2)}) copy-start(f32[512,512]{1,0:T(8,128)} %forward_rows.7) | copy-start | bytes 3145732
  43.0 16.1 %collective-permute-start = (bf16[512,512]{1,0:T(8,128)(2,1)}, bf16[512,512]{1,0:T(8,128)(2,1)S(1)}, u32[]{:S(2)}, u32[]{:S(2)}) collective-permute-start(bf16[512,512]{1,0:T(8,128)(2,1)} %convert_element_type.93), channel_id=1, source_target_pairs={{0,1},{3,2},{4,5},{7,6},{8,9},{11,10},{12,13},{15,14},{16,17},{19,... | collective-permute-start | bytes 1572872 | tf_op jit(solution)/shard_map/ppermute | solution.py:207
  44.3 4.4 %copy-start.1 = (f32[512,512]{1,0:T(8,128)S(1)}, f32[512,512]{1,0:T(8,128)}, u32[]{:S(2)}) copy-start(f32[512,512]{1,0:T(8,128)} %forward_rows.6) | copy-start | bytes 3145732
  45.6 13.4 %copy-start = (f32[512,512]{1,0:T(8,128)S(1)}, f32[512,512]{1,0:T(8,128)}, u32[]{:S(2)}) copy-start(f32[512,512]{1,0:T(8,128)} %forward_rows.5) | copy-start | bytes 3145732
  45.6 14.3 %collective-permute-start.10 = (bf16[512,512]{1,0:T(8,128)(2,1)S(1)}, bf16[512,512]{1,0:T(8,128)(2,1)S(1)}, u32[]{:S(2)}, u32[]{:S(2)}) collective-permute-start(bf16[512,512]{1,0:T(8,128)(2,1)S(1)} %fusion.3), channel_id=1, source_target_pairs={{1,2},{2,1},{5,6},{6,5},{9,10},{10,9},{13,14},{14,13},{17,18},{18,... | collective-permute-start | bytes 1572872 | tf_op jit(solution)/shard_map/ppermute | solution.py:209
  47.7 14.8 %collective-permute-start.7 = (bf16[512,512]{1,0:T(8,128)(2,1)S(1)}, bf16[512,512]{1,0:T(8,128)(2,1)S(1)}, u32[]{:S(2)}, u32[]{:S(2)}) collective-permute-start(bf16[512,512]{1,0:T(8,128)(2,1)S(1)} %fusion.2), channel_id=1, source_target_pairs={{1,2},{2,1},{5,6},{6,5},{9,10},{10,9},{13,14},{14,13},{17,18},{18,... | collective-permute-start | bytes 1572872 | tf_op jit(solution)/shard_map/ppermute | solution.py:209
  48.8 16.2 %collective-permute-start.4 = (bf16[512,512]{1,0:T(8,128)(2,1)S(1)}, bf16[512,512]{1,0:T(8,128)(2,1)S(1)}, u32[]{:S(2)}, u32[]{:S(2)}) collective-permute-start(bf16[512,512]{1,0:T(8,128)(2,1)S(1)} %fusion.1), channel_id=1, source_target_pairs={{1,2},{2,1},{5,6},{6,5},{9,10},{10,9},{13,14},{14,13},{17,18},{18,... | collective-permute-start | bytes 1572872 | tf_op jit(solution)/shard_map/ppermute | solution.py:209
  59.2 7.4 %collective-permute-start.1 = (bf16[512,512]{1,0:T(8,128)(2,1)S(1)}, bf16[512,512]{1,0:T(8,128)(2,1)S(1)}, u32[]{:S(2)}, u32[]{:S(2)}) collective-permute-start(bf16[512,512]{1,0:T(8,128)(2,1)S(1)} %fusion), channel_id=1, source_target_pairs={{1,2},{2,1},{5,6},{6,5},{9,10},{10,9},{13,14},{14,13},{17,18},{18,... | collective-permute-start | bytes 1572872 | tf_op jit(solution)/shard_map/ppermute | solution.py:209
  61.2 18.9 %collective-permute-start.11 = (bf16[512,512]{1,0:T(8,128)(2,1)S(1)}, bf16[512,512]{1,0:T(8,128)(2,1)S(1)}, u32[]{:S(2)}, u32[]{:S(2)}) collective-permute-start(bf16[512,512]{1,0:T(8,128)(2,1)S(1)} %add_convert_fusion.2), channel_id=1, source_target_pairs={{1,0},{2,3},{5,4},{6,7},{9,8},{10,11},{13,12},{14,15},{17,16},{18,... | collective-permute-start | bytes 1572872 | tf_op jit(solution)/shard_map/ppermute | solution.py:213
  63.7 27.6 %collective-permute-start.8 = (bf16[512,512]{1,0:T(8,128)(2,1)S(1)}, bf16[512,512]{1,0:T(8,128)(2,1)S(1)}, u32[]{:S(2)}, u32[]{:S(2)}) collective-permute-start(bf16[512,512]{1,0:T(8,128)(2,1)S(1)} %add_convert_fusion.3), channel_id=1, source_target_pairs={{1,0},{2,3},{5,4},{6,7},{9,8},{10,11},{13,12},{14,15},{17,16},{18,... | collective-permute-start | bytes 1572872 | tf_op jit(solution)/shard_map/ppermute | solution.py:213
  65.3 37.3 %collective-permute-start.5 = (bf16[512,512]{1,0:T(8,128)(2,1)S(1)}, bf16[512,512]{1,0:T(8,128)(2,1)S(1)}, u32[]{:S(2)}, u32[]{:S(2)}) collective-permute-start(bf16[512,512]{1,0:T(8,128)(2,1)S(1)} %add_convert_fusion.4), channel_id=1, source_target_pairs={{1,0},{2,3},{5,4},{6,7},{9,8},{10,11},{13,12},{14,15},{17,16},{18,... | collective-permute-start | bytes 1572872 | tf_op jit(solution)/shard_map/ppermute | solution.py:213
  66.8 45.5 %collective-permute-start.2 = (bf16[512,512]{1,0:T(8,128)(2,1)S(1)}, bf16[512,512]{1,0:T(8,128)(2,1)S(1)}, u32[]{:S(2)}, u32[]{:S(2)}) collective-permute-start(bf16[512,512]{1,0:T(8,128)(2,1)S(1)} %add_convert_fusion.5), channel_id=1, source_target_pairs={{1,0},{2,3},{5,4},{6,7},{9,8},{10,11},{13,12},{14,15},{17,16},{18,... | collective-permute-start | bytes 1572872 | tf_op jit(solution)/shard_map/ppermute | solution.py:213
  112.5 1.5 copy-start.4
  113.9 20.9 %collective-permute-start.15 = (f32[256,512]{1,0:T(8,128)}, f32[256,512]{1,0:T(8,128)}, u32[]{:S(2)}, u32[]{:S(2)}) collective-permute-start(f32[256,512]{1,0:T(8,128)} %constant_dynamic-slice_fusion.5), channel_id=1, source_target_pairs={{0,4},{4,0},{8,12},{12,8},{16,20},{20,16},{24,28},{28,24},{1,5},{5... | collective-permute-start | bytes 1572872 | tf_op jit(solution)/shard_map/ppermute | solution.py:237
  134.8 43.2 %collective-permute-start.12 = (f32[1024,512]{1,0:T(8,128)S(1)}, f32[1024,512]{1,0:T(8,128)}, u32[]{:S(2)}, u32[]{:S(2)}) collective-permute-start(f32[1024,512]{1,0:T(8,128)S(1)} %constant_dynamic-slice_fusion.7), channel_id=1, source_target_pairs={{0,4},{4,0},{8,12},{12,8},{16,20},{20,16},{24,28},{28,24},{1,5},{5... | collective-permute-start | bytes 6291464 | tf_op jit(solution)/shard_map/ppermute | solution.py:237
  136.0 0.8 copy-start.6
  136.8 9.1 %collective-permute-start.16 = (f32[128,512]{1,0:T(8,128)S(1)}, f32[128,512]{1,0:T(8,128)S(1)}, u32[]{:S(2)}, u32[]{:S(2)}) collective-permute-start(f32[128,512]{1,0:T(8,128)S(1)} %constant_dynamic-slice_fusion.4), channel_id=1, source_target_pairs={{0,8},{4,20},{8,0},{12,28},{16,24},{20,4},{24,16},{28,12},{1,9},{5... | collective-permute-start | bytes 786440 | tf_op jit(solution)/shard_map/ppermute | solution.py:237
  146.9 5.0 %collective-permute-start.17 = (f32[64,512]{1,0:T(8,128)S(1)}, f32[64,512]{1,0:T(8,128)S(1)}, u32[]{:S(2)}, u32[]{:S(2)}) collective-permute-start(f32[64,512]{1,0:T(8,128)S(1)} %constant_dynamic-slice_fusion.3), channel_id=1, source_target_pairs={{0,16},{4,12},{8,24},{12,4},{16,0},{20,28},{24,8},{28,20},{1,17},{... | collective-permute-start | bytes 393224 | tf_op jit(solution)/shard_map/ppermute | solution.py:237
  151.9 3.8 collective-permute-start.18
  155.8 0.7 collective-permute-start.19
  156.5 12.8 %collective-permute-start.20 = (f32[64,512]{1,0:T(8,128)S(1)}, f32[64,512]{1,0:T(8,128)S(1)}, u32[]{:S(2)}, u32[]{:S(2)}) collective-permute-start(f32[64,512]{1,0:T(8,128)S(1)} %add.175), channel_id=1, source_target_pairs={{1,0},{2,3},{5,4},{6,7},{9,8},{10,11},{13,12},{14,15},{17,16},{18,... | collective-permute-start | bytes 393224 | tf_op jit(solution)/shard_map/ppermute | solution.py:213
  169.3 6.4 %collective-permute-start.21 = (f32[64,512]{1,0:T(8,128)S(1)}, f32[64,512]{1,0:T(8,128)S(1)}, u32[]{:S(2)}, u32[]{:S(2)}) collective-permute-start(f32[64,512]{1,0:T(8,128)S(1)} %broadcast_select_fusion.19), channel_id=1, source_target_pairs={{0,16},{4,12},{8,24},{12,4},{16,0},{20,28},{24,8},{28,20},{1,17},{... | collective-permute-start | bytes 393224 | tf_op jit(solution)/shard_map/ppermute | solution.py:246
  175.8 6.5 %collective-permute-start.22 = (f32[128,512]{1,0:T(8,128)S(1)}, f32[128,512]{1,0:T(8,128)}, u32[]{:S(2)}, u32[]{:S(2)}) collective-permute-start(f32[128,512]{1,0:T(8,128)S(1)} %pad_maximum_fusion.8), channel_id=1, source_target_pairs={{0,8},{4,20},{8,0},{12,28},{16,24},{20,4},{24,16},{28,12},{1,9},{5... | collective-permute-start | bytes 786440 | tf_op jit(solution)/shard_map/ppermute | solution.py:246
  180.7 10.3 %collective-permute-start.13 = (bf16[512,512]{1,0:T(8,128)(2,1)S(1)}, bf16[512,512]{1,0:T(8,128)(2,1)}, u32[]{:S(2)}, u32[]{:S(2)}) collective-permute-start(bf16[512,512]{1,0:T(8,128)(2,1)S(1)} %dynamic-slice_convert_fusion.2), channel_id=1, source_target_pairs={{0,8},{4,20},{8,0},{12,28},{16,24},{20,4},{24,16},{28,12},{1,9},{5... | collective-permute-start | bytes 1572872 | tf_op jit(solution)/shard_map/ppermute | solution.py:237
  183.4 0.9 copy-start.5
  184.2 8.2 %collective-permute-start.23 = (f32[256,512]{1,0:T(8,128)}, f32[256,512]{1,0:T(8,128)}, u32[]{:S(2)}, u32[]{:S(2)}) collective-permute-start(f32[256,512]{1,0:T(8,128)} %pad_maximum_fusion.5), channel_id=1, source_target_pairs={{0,4},{4,0},{8,12},{12,8},{16,20},{20,16},{24,28},{28,24},{1,5},{5... | collective-permute-start | bytes 1572872 | tf_op jit(solution)/shard_map/ppermute | solution.py:246
  192.3 32.6 %collective-permute-start.14 = (f32[256,512]{1,0:T(8,128)S(1)}, f32[256,512]{1,0:T(8,128)S(1)}, u32[]{:S(2)}, u32[]{:S(2)}) collective-permute-start(f32[256,512]{1,0:T(8,128)S(1)} %constant_dynamic-slice_fusion.6), channel_id=1, source_target_pairs={{0,16},{4,12},{8,24},{12,4},{16,0},{20,28},{24,8},{28,20},{1,17},{... | collective-permute-start | bytes 1572872 | tf_op jit(solution)/shard_map/ppermute | solution.py:237
  227.2 9.2 %collective-permute-start.24 = (bf16[256,512]{1,0:T(8,128)(2,1)S(1)}, bf16[256,512]{1,0:T(8,128)(2,1)S(1)}, u32[]{:S(2)}, u32[]{:S(2)}) collective-permute-start(bf16[256,512]{1,0:T(8,128)(2,1)S(1)} %convolution_convert_fusion), channel_id=1, source_target_pairs={{0,16},{4,12},{8,24},{12,4},{16,0},{20,28},{24,8},{28,20},{1,17},{... | collective-permute-start | bytes 786440 | tf_op jit(solution)/shard_map/ppermute | solution.py:246
  236.5 9.2 %collective-permute-start.25 = (bf16[512,512]{1,0:T(8,128)(2,1)S(1)}, bf16[512,512]{1,0:T(8,128)(2,1)S(1)}, u32[]{:S(2)}, u32[]{:S(2)}) collective-permute-start(bf16[512,512]{1,0:T(8,128)(2,1)S(1)} %pad_maximum_fusion.6), channel_id=1, source_target_pairs={{0,8},{4,20},{8,0},{12,28},{16,24},{20,4},{24,16},{28,12},{1,9},{5... | collective-permute-start | bytes 1572872 | tf_op jit(solution)/shard_map/ppermute | solution.py:246
  246.0 2.7 collective-permute-start.26
  268.5 13.0 %collective-permute-start.27 = (bf16[512,512]{1,0:T(8,128)(2,1)S(1)}, bf16[512,512]{1,0:T(8,128)(2,1)S(1)}, u32[]{:S(2)}, u32[]{:S(2)}) collective-permute-start(bf16[512,512]{1,0:T(8,128)(2,1)S(1)} %get-tuple-element.10), channel_id=1, source_target_pairs={{0,1},{4,5},{8,9},{12,13},{16,17},{20,21},{24,25},{28,29}} | collective-permute-start | bytes 1572872 | tf_op jit(solution)/shard_map/ppermute | solution.py:275
  270.7 16.7 %collective-permute-start.30 = (bf16[512,512]{1,0:T(8,128)(2,1)S(1)}, bf16[512,512]{1,0:T(8,128)(2,1)S(1)}, u32[]{:S(2)}, u32[]{:S(2)}) collective-permute-start(bf16[512,512]{1,0:T(8,128)(2,1)S(1)} %get-tuple-element.11), channel_id=1, source_target_pairs={{3,2},{7,6},{11,10},{15,14},{19,18},{23,22},{27,26},{31,30}} | collective-permute-start | bytes 1572872 | tf_op jit(solution)/shard_map/ppermute | solution.py:276
  283.0 14.5 %collective-permute-start.28 = (bf16[512,512]{1,0:T(8,128)(2,1)S(1)}, bf16[512,512]{1,0:T(8,128)(2,1)S(1)}, u32[]{:S(2)}, u32[]{:S(2)}) collective-permute-start(bf16[512,512]{1,0:T(8,128)(2,1)S(1)} %add_convert_fusion.1), channel_id=1, source_target_pairs={{0,1},{1,2},{4,5},{5,6},{8,9},{9,10},{12,13},{13,14},{16,17},{17,1... | collective-permute-start | bytes 1572872 | tf_op jit(solution)/shard_map/ppermute | solution.py:275
  299.3 5.8 %collective-permute-start.31 = (bf16[512,512]{1,0:T(8,128)(2,1)S(1)}, bf16[512,512]{1,0:T(8,128)(2,1)S(1)}, u32[]{:S(2)}, u32[]{:S(2)}) collective-permute-start(bf16[512,512]{1,0:T(8,128)(2,1)S(1)} %get-tuple-element.9), channel_id=1, source_target_pairs={{3,2},{2,1},{7,6},{6,5},{11,10},{10,9},{15,14},{14,13},{19,18},{18... | collective-permute-start | bytes 1572872 | tf_op jit(solution)/shard_map/ppermute | solution.py:276
  300.0 25.5 %collective-permute-start.29 = (f32[512,512]{1,0:T(8,128)S(1)}, f32[512,512]{1,0:T(8,128)S(1)}, u32[]{:S(2)}, u32[]{:S(2)}) collective-permute-start(f32[512,512]{1,0:T(8,128)S(1)} %get-tuple-element.8), channel_id=1, source_target_pairs={{0,1},{1,2},{2,3},{4,5},{5,6},{6,7},{8,9},{9,10},{10,11},{12,13},{... | collective-permute-start | bytes 3145736 | tf_op jit(solution)/shard_map/ppermute | solution.py:275
  307.5 32.8 %collective-permute-start.32 = (f32[512,512]{1,0:T(8,128)}, f32[512,512]{1,0:T(8,128)S(1)}, u32[]{:S(2)}, u32[]{:S(2)}) collective-permute-start(f32[512,512]{1,0:T(8,128)} %convert_add_fusion), channel_id=1, source_target_pairs={{3,2},{2,1},{1,0},{7,6},{6,5},{5,4},{11,10},{10,9},{9,8},{15,14},{... | collective-permute-start | bytes 3145736 | tf_op jit(solution)/shard_map/ppermute | solution.py:276
  343.8 2.0 collective-permute-start.33
  345.9 9.3 %collective-permute-start.34 = (f32[128,512]{1,0:T(8,128)S(1)}, f32[128,512]{1,0:T(8,128)S(1)}, u32[]{:S(2)}, u32[]{:S(2)}) collective-permute-start(f32[128,512]{1,0:T(8,128)S(1)} %constant_dynamic-slice_fusion.1), channel_id=1, source_target_pairs={{0,8},{4,20},{8,0},{12,28},{16,24},{20,4},{24,16},{28,12},{1,9},{5... | collective-permute-start | bytes 786440 | tf_op jit(solution)/shard_map/ppermute | solution.py:237
  355.2 5.0 %collective-permute-start.35 = (f32[64,512]{1,0:T(8,128)S(1)}, f32[64,512]{1,0:T(8,128)S(1)}, u32[]{:S(2)}, u32[]{:S(2)}) collective-permute-start(f32[64,512]{1,0:T(8,128)S(1)} %constant_dynamic-slice_fusion), channel_id=1, source_target_pairs={{0,16},{4,12},{8,24},{12,4},{16,0},{20,28},{24,8},{28,20},{1,17},{... | collective-permute-start | bytes 393224 | tf_op jit(solution)/shard_map/ppermute | solution.py:237
  360.3 6.2 %collective-permute-start.36 = (f32[64,512]{1,0:T(8,128)S(1)}, f32[64,512]{1,0:T(8,128)S(1)}, u32[]{:S(2)}, u32[]{:S(2)}) collective-permute-start(f32[64,512]{1,0:T(8,128)S(1)} %dynamic-slice_add_fusion.5), channel_id=1, source_target_pairs={{0,1},{3,2},{4,5},{7,6},{8,9},{11,10},{12,13},{15,14},{16,17},{19,... | collective-permute-start | bytes 393224 | tf_op jit(solution)/shard_map/ppermute | solution.py:207
  366.5 0.7 collective-permute-start.37
  367.2 12.8 %collective-permute-start.38 = (f32[64,512]{1,0:T(8,128)S(1)}, f32[64,512]{1,0:T(8,128)S(1)}, u32[]{:S(2)}, u32[]{:S(2)}) collective-permute-start(f32[64,512]{1,0:T(8,128)S(1)} %add.193), channel_id=1, source_target_pairs={{1,0},{2,3},{5,4},{6,7},{9,8},{10,11},{13,12},{14,15},{17,16},{18,... | collective-permute-start | bytes 393224 | tf_op jit(solution)/shard_map/ppermute | solution.py:213
  380.1 6.3 %collective-permute-start.39 = (f32[64,512]{1,0:T(8,128)S(1)}, f32[64,512]{1,0:T(8,128)S(1)}, u32[]{:S(2)}, u32[]{:S(2)}) collective-permute-start(f32[64,512]{1,0:T(8,128)S(1)} %broadcast_select_fusion.18), channel_id=1, source_target_pairs={{0,16},{4,12},{8,24},{12,4},{16,0},{20,28},{24,8},{28,20},{1,17},{... | collective-permute-start | bytes 393224 | tf_op jit(solution)/shard_map/ppermute | solution.py:246
  386.4 6.4 %collective-permute-start.40 = (f32[128,512]{1,0:T(8,128)S(1)}, f32[128,512]{1,0:T(8,128)S(1)}, u32[]{:S(2)}, u32[]{:S(2)}) collective-permute-start(f32[128,512]{1,0:T(8,128)S(1)} %pad_maximum_fusion.9), channel_id=1, source_target_pairs={{0,8},{4,20},{8,0},{12,28},{16,24},{20,4},{24,16},{28,12},{1,9},{5... | collective-permute-start | bytes 786440 | tf_op jit(solution)/shard_map/ppermute | solution.py:246
  393.0 2.0 collective-permute-start.41

commit v2 on v1

--- a/solution.py
+++ b/solution.py
@@ -12,9 +12,9 @@
 TN = (((0,), (0,)), ((), ()))
 
 
-def forward_body(group, base, idx_ref, cnt_ref, t_ref, x_ref, o_ref, acc_ref):
+def forward_body(group, base_ref, idx_ref, cnt_ref, t_ref, x_ref, o_ref, acc_ref):
     tile = t_ref.shape[2]
-    row = pl.program_id(0) + base
+    row = pl.program_id(0) + base_ref[0]
     count = cnt_ref[row]
     acc_ref[...] = jnp.zeros_like(acc_ref)
 
@@ -40,30 +40,31 @@
     width = x.shape[1]
     group = next(g for g in (8, 4, 2, 1) if slots % g == 0)
     return pl.pallas_call(
-        functools.partial(forward_body, group, base),
+        functools.partial(forward_body, group),
         out_shape=jax.ShapeDtypeStruct((rows * tile, width), jnp.float32),
         grid_spec=pltpu.PrefetchScalarGridSpec(
-            num_scalar_prefetch=2,
+            num_scalar_prefetch=3,
             grid=(rows,),
             in_specs=[
-                pl.BlockSpec((1, slots, tile, tile), lambda r, *_: (r + base, 0, 0, 0)),
+                pl.BlockSpec((1, slots, tile, tile), lambda r, at, *_: (r + at[0], 0, 0, 0)),
                 pl.BlockSpec(x.shape, lambda r, *_: (0, 0)),
             ],
             out_specs=pl.BlockSpec((tile, width), lambda r, *_: (r, 0)),
             scratch_shapes=[pltpu.VMEM((tile, width), jnp.float32)],
         ),
         name="forward_rows",
-    )(col_index, counts, tiles, x)
-
-
-def backward_body(group, idx_ref, cnt_ref, t_ref, f_ref, z_ref):
+    )(jnp.full((1,), base, jnp.int32), col_index, counts, tiles, x)
+
+
+def backward_body(group, base, first, idx_ref, cnt_ref, t_ref, f_ref, *refs):
+    z_ref = refs[-1]
     tile = t_ref.shape[2]
-    row = pl.program_id(0)
+    row = pl.program_id(0) + base
     count = cnt_ref[row]
 
-    @pl.when(row == 0)
+    @pl.when(pl.program_id(0) == 0)
     def _():
-        z_ref[...] = jnp.zeros_like(z_ref)
+        z_ref[...] = jnp.zeros_like(z_ref) if first else refs[0][...]
 
     def step(p, carry):
         lhs = []
@@ -82,24 +83,26 @@
     lax.fori_loop(0, (count + group - 1) // group, step, 0)
 
 
-def backward(tiles, col_index, counts, panel, col_rows):
-    rows, slots, tile = tiles.shape[:3]
+def backward(tiles, col_index, counts, panel, col_rows, base, total):
+    slots, tile = tiles.shape[1], tiles.shape[2]
     width = panel.shape[1]
     group = next(g for g in (4, 2, 1) if slots % g == 0)
+    whole = pl.BlockSpec((col_rows, width), lambda r, *_: (0, 0), pipeline_mode=pl.Buffered(1))
+    more = () if total is None else (total,)
     return pl.pallas_call(
-        functools.partial(backward_body, group),
+        functools.partial(backward_body, group, base, total is None),
         out_shape=jax.ShapeDtypeStruct((col_rows, width), jnp.float32),
         grid_spec=pltpu.PrefetchScalarGridSpec(
             num_scalar_prefetch=2,
-            grid=(rows,),
+            grid=(panel.shape[0] // tile,),
             in_specs=[
-                pl.BlockSpec((1, slots, tile, tile), lambda r, *_: (r, 0, 0, 0)),
+                pl.BlockSpec((1, slots, tile, tile), lambda r, *_: (r + base, 0, 0, 0)),
                 pl.BlockSpec((tile, width), lambda r, *_: (r, 0)),
-            ],
+            ] + [whole] * len(more),
             out_specs=pl.BlockSpec((col_rows, width), lambda r, *_: (0, 0)),
         ),
         name="backward_rows",
-    )(col_index, counts, tiles, panel)
+    )(col_index, counts, tiles, panel, *more)
 
 
 def factor_block(read, r_ref, t_ref, group):
@@ -199,19 +202,38 @@
     )(gram)
 
 
-def line_sum(value, wire):
+def line_inward(value, wire):
+    n = lax.axis_size("col")
+    got = jnp.zeros_like(value).astype(wire)
+    for s in range(n // 2 - 1):
+        if s:
+            value = value + got.astype(value.dtype)
+        got = lax.ppermute(value.astype(wire), "col", [(s, s + 1), (n - 1 - s, n - 2 - s)])
+    return value, got
+
+
+def line_across(value, wire):
+    n = lax.axis_size("col")
+    pairs = [(n // 2 - 1, n // 2), (n // 2, n // 2 - 1)]
+    return (value + lax.ppermute(value.astype(wire), "col", pairs).astype(value.dtype)).astype(wire)
+
+
+def line_outward(value, beside=None):
     n = lax.axis_size("col")
     z = lax.axis_index("col")
-    for s in range(n // 2 - 1):
-        pairs = [(s, s + 1), (n - 1 - s, n - 2 - s)]
-        value = value + lax.ppermute(value.astype(wire), "col", pairs).astype(value.dtype)
-    pairs = [(n // 2 - 1, n // 2), (n // 2, n // 2 - 1)]
-    value = value + lax.ppermute(value.astype(wire), "col", pairs).astype(value.dtype)
-    value = value.astype(wire)
     for s in reversed(range(n // 2 - 1)):
         pairs = [(s + 1, s), (n - 2 - s, n - 1 - s)]
         got = lax.ppermute(value, "col", pairs)
+        if beside is not None:
+            value, beside = lax.optimization_barrier((value, beside))
         value = jnp.where((z == s) | (z == n - 1 - s), got, value)
+    return value, beside
+
+
+def col_sum(value):
+    n = lax.axis_size("col")
+    for bit in range(n.bit_length() - 1):
+        value = value + lax.ppermute(value, "col", [(i, i ^ (1 << bit)) for i in range(n)])
     return value
 
 
@@ -252,29 +274,40 @@
 
 def gram_sum(gram):
     part, offset = row_scatter(gram, (jnp.float32,))
-    part = line_sum(part, jnp.float32)
+    part = col_sum(part)
     return row_gather(part, offset, gram.shape[0])
 
 
-def line_scatter(value):
+def share_order(k):
     n = lax.axis_size("col")
     z = lax.axis_index("col")
-    share = value.shape[0] // n
-
-    def own(q):
-        return lax.dynamic_slice_in_dim(value, jnp.clip(q, 0, n - 1) * share, share, 0)
+    low = jnp.where(k < n - 1 - z, n - 1 - k, k - (n - 1 - z))
+    high = jnp.where(k < z, k, n - 1 - (k - z))
+    return jnp.where(k == n - 1, z, jnp.where(z < n // 2, low, high))
+
+
+def line_scatter(parts):
+    n = lax.axis_size("col")
+    z = lax.axis_index("col")
+
+    def pick(t, lag):
+        value = parts[t - 1]
+        for d in range(1, min(n // 2, t)):
+            value = jnp.where(lag == d, parts[t - 1 - d], value)
+        return value
 
     right = left = None
     for t in range(1, n):
-        up = own(n - 1 - (t - 1 - z))
-        down = own(t - 1 - (n - 1 - z))
+        up = pick(t, jnp.where(z < n // 2, z, 0))
+        down = pick(t, jnp.where(z < n // 2, 0, n - 1 - z))
         if right is not None:
             up = up + right.astype(up.dtype)
             down = down + left.astype(down.dtype)
         wire = jnp.float32 if t == n - 1 else jnp.bfloat16
         right = lax.ppermute(up.astype(wire), "col", [(i, i + 1) for i in range(t)])
         left = lax.ppermute(down.astype(wire), "col", [(n - 1 - i, n - 2 - i) for i in range(t)])
-    return own(z) + right.astype(value.dtype) + left.astype(value.dtype)
+        right, left = lax.optimization_barrier((right, left))
+    return parts[n - 1] + right.astype(jnp.float32) + left.astype(jnp.float32)
 
 
 def local(tiles, col_index, counts, sketch):
@@ -285,23 +318,42 @@
     z = lax.axis_index("col")
 
     chunk = tile_rows // n_col
-    firsts = []
+    halves, sums, sent = [], [], []
     for j in range(n_col):
-        part = forward(tiles, col_index, counts, sketch, j * chunk, chunk)
-        firsts.append(line_sum(part, jnp.bfloat16))
-    first = jnp.concatenate(firsts, 0)
+        live = counts
+        if j >= 2:
+            live, halves[j - 2] = lax.optimization_barrier((counts, halves[j - 2]))
+        part = forward(tiles, col_index, live, sketch, j * chunk, chunk)
+        if j >= 1:
+            value, got = sent[j - 1]
+            value, part = lax.optimization_barrier((value, part))
+            halves.append(value + got.astype(value.dtype))
+        sent.append(line_inward(part, jnp.bfloat16))
+    value, got = sent[-1]
+    halves.append(value + got.astype(value.dtype))
+    crossed = [line_across(half, jnp.bfloat16) for half in halves]
+    back = None
+    for j in range(n_col):
+        total, back = line_outward(crossed[j], back)
+        sums.append(total)
+        if j < n_col - 1:
+            back = backward(tiles, col_index, counts, total, sketch.shape[0], j * chunk, back)
+    first = jnp.concatenate(sums, 0)
 
     share = first.shape[0] // n_col
     mine = lax.dynamic_slice_in_dim(first, z * share, share, 0)
     gram = lax.dot_general(mine, mine, TN, preferred_element_type=jnp.float32)
     unused, inverse = cholesky(gram_sum(gram), 1.0 / total_rows)
 
-    back = backward(tiles, col_index, counts, first, sketch.shape[0])
+    back = backward(tiles, col_index, counts, sums[-1], sketch.shape[0], (n_col - 1) * chunk, back)
     part, offset = row_scatter(back, (jnp.float32, jnp.bfloat16, jnp.float32))
     part = lax.dot_general(part, inverse, NT, precision=HI, preferred_element_type=jnp.float32)
     back = row_gather(part.astype(jnp.bfloat16), offset, sketch.shape[0])
 
-    second = line_scatter(forward(tiles, col_index, counts, back, 0, tile_rows))
+    parts = [
+        forward(tiles, col_index, counts, back, share_order(k) * chunk, chunk) for k in range(n_col)
+    ]
+    second = line_scatter(parts)
     gram = lax.dot_general(second, second, TN, precision=HI, preferred_element_type=jnp.float32)
     factor, inverse = cholesky(gram_sum(gram), 1.0 / total_rows)
     basis = lax.dot_general(second, inverse, NT, precision=HI, preferred_element_type=jnp.float32)

time: 433 us -> 392 us (0.905)
  waiting for transfers between devices: 200 us -> 144 us
  Pallas kernels: 120 us -> 136 us
  starting transfers between devices: 58.9 us -> 54.5 us
    ppermute x18 -> x16, waiting for transfers between devices: 81.7 us -> 45.1 us  [the longest x4 22.3 us: col_sum(): lax.ppermute(value, 'col', [(i, i ^ 1 << bit) for i in range(n)])]
    pallas_call x6 -> x12, Pallas kernels: 59.7 us -> 75.8 us  [the longest x8 46.5 us: forward(): pl.pallas_call(functools.partial(forward_body, group), out_shape=jax.Shap...]
    ppermute x3, waiting for transfers between devices: 36.8 us -> 23.1 us  [line_scatter(): right = lax.ppermute(up.astype(wire), 'col', [(i, i + 1) for i in range(t)])]
    ppermute x3, waiting for transfers between devices: 14.8 us -> 4.08 us  [line_scatter(): lax.ppermute(down.astype(wire), 'col', [(n - 1 - i, n - 2 - i) for i in r...]
    convert_element_type x12 -> x13, other arithmetic: 14.2 us -> 15.1 us  [the longest x4 5.77 us: line_across(): (value + lax.ppermute(value.astype(wire), 'col', pairs).astype(value.dtyp...]
    ppermute x18 -> x16, starting transfers between devices: 27.9 us -> 27.8 us  [the longest x4 14.7 us: line_inward(): lax.ppermute(value.astype(wire), 'col', [(s, s + 1), (n - 1 - s, n - 2 -...]
  transfers between devices with their start and end apart: 42 -> 40, of which waited for: 28 -> 28; matrix products, arithmetic and copies ran while one was open for 7% -> 7% of each run, Pallas kernels for 16% -> 24%
where the time goes in v2:
time: 392 us; the launch traced here: 389 us
  waiting for transfers between devices  144 us (37%)
  Pallas kernels  136 us (35%)
  starting transfers between devices  54.5 us (14%)
  other arithmetic  37.4 us (10%)
  matrix products  11.8 us (3%)
    pallas_call x2, Pallas kernels, cholesky(): pl.pallas_call(functools.partial(chol_body, scale, group), out_shape=(s,...  60.4 us
    pallas_call x8, Pallas kernels, forward(): pl.pallas_call(functools.partial(forward_body, group), out_shape=jax.Shap...  46.5 us
    ppermute x9, waiting for transfers between devices, row_gather(): got = lax.ppermute(part, 'row', pairs)  42.2 us
    pallas_call x4, Pallas kernels, backward(): pl.pallas_call(functools.partial(backward_body, group, base, total is Non...  29.3 us
    ppermute x9, waiting for transfers between devices, row_scatter(): value = keep + lax.ppermute(give, 'row', pairs).astype(value.dtype)  29.2 us
    ppermute x3, waiting for transfers between devices, line_scatter(): right = lax.ppermute(up.astype(wire), 'col', [(i, i + 1) for i in range(t)])  23.1 us
    ppermute x4, waiting for transfers between devices, col_sum(): lax.ppermute(value, 'col', [(i, i ^ 1 << bit) for i in range(n)])  22.3 us
    ppermute x4, waiting for transfers between devices, line_inward(): lax.ppermute(value.astype(wire), 'col', [(s, s + 1), (n - 1 - s, n - 2 -...  16.5 us
  transfers between devices with their start and end apart: 40, of which 28 were waited for; matrix products, arithmetic and copies ran while one was open for 7% of the time, Pallas kernels for 24%

profile of v2, /device:TPU:0, one launch (start us, length us, event | category | flops | bytes accessed | tf_op | source)
XLA Modules:
  0.0 388.9 jit_solution(7371819913913002161)
XLA Ops:
  0.6 5.8 %forward_rows.8 = f32[512,512]{1,0:T(8,128)} custom-call(s32[1]{0:T(128)} %constant.9.clone.1.base_ref, s32[16,16]{1,0:T(8,128)} %idx_ref.23, s32[16]{0:T(128)} %bitcast.7, bf16[16,16,128,128]{3,2,1,0:T(8,128)(2,1)} %t_ref.23, bf16[2048,512]{1,0:T(8,128)(2,1)} %x_ref.7), custom_call_target="tpu_custom_call" | custom-call | tf_op jit(solution)/shard_map/forward_rows/pallas_call | solution.py:42
  7.7 5.0 %collective-permute-start = (bf16[512,512]{1,0:T(8,128)(2,1)S(1)}, bf16[512,512]{1,0:T(8,128)(2,1)S(1)}, u32[]{:S(2)}, u32[]{:S(2)}) collective-permute-start(bf16[512,512]{1,0:T(8,128)(2,1)S(1)} %convert_element_type.91), channel_id=1, source_target_pairs={{0,1},{3,2},{4,5},{7,6},{8,9},{11,10},{12,13},{15,14},{16,17},{19,... | collective-permute-start | bytes 1572872 | tf_op jit(solution)/shard_map/ppermute | solution.py:211
  12.7 5.8 %forward_rows.9 = f32[512,512]{1,0:T(8,128)} custom-call(s32[1]{0:T(128)} %constant.10.clone.1.base_ref, s32[16,16]{1,0:T(8,128)} %idx_ref.23, s32[16]{0:T(128)} %bitcast.8, bf16[16,16,128,128]{3,2,1,0:T(8,128)(2,1)} %t_ref.23, bf16[2048,512]{1,0:T(8,128)(2,1)} %x_ref.7), custom_call_target="tpu_custom_call" | custom-call | tf_op jit(solution)/shard_map/forward_rows/pallas_call | solution.py:42
  19.9 2.1 collective-permute-start.1
  21.9 3.0 collective-permute-done
  27.4 5.8 %forward_rows.10 = f32[512,512]{1,0:T(8,128)} custom-call(s32[1]{0:T(128)} %constant.11.clone.1.base_ref, s32[16,16]{1,0:T(8,128)} %idx_ref.23, s32[16]{0:T(128)} %bitcast.9, bf16[16,16,128,128]{3,2,1,0:T(8,128)(2,1)} %t_ref.23, bf16[2048,512]{1,0:T(8,128)(2,1)} %x_ref.7), custom_call_target="tpu_custom_call" | custom-call | tf_op jit(solution)/shard_map/forward_rows/pallas_call | solution.py:42
  33.2 2.2 collective-permute-done.1
  35.4 1.5 convert_add_fusion.5
  40.1 5.8 %forward_rows.11 = f32[512,512]{1,0:T(8,128)} custom-call(s32[1]{0:T(128)} %constant.12.clone.1.base_ref, s32[16,16]{1,0:T(8,128)} %idx_ref.23, s32[16]{0:T(128)} %bitcast.10, bf16[16,16,128,128]{3,2,1,0:T(8,128)(2,1)} %t_ref.23, bf16[2048,512]{1,0:T(8,128)(2,1)} %x_ref.7), custom_call_target="tpu_custom_call" | custom-call | tf_op jit(solution)/shard_map/forward_rows/pallas_call | solution.py:42
  45.9 6.4 %collective-permute-start.5 = (bf16[512,512]{1,0:T(8,128)(2,1)}, bf16[512,512]{1,0:T(8,128)(2,1)S(1)}, u32[]{:S(2)}, u32[]{:S(2)}) collective-permute-start(bf16[512,512]{1,0:T(8,128)(2,1)} %convert_element_type.100), channel_id=1, source_target_pairs={{0,1},{3,2},{4,5},{7,6},{8,9},{11,10},{12,13},{15,14},{16,17},{19,... | collective-permute-start | bytes 1572872 | tf_op jit(solution)/shard_map/ppermute | solution.py:211
  57.5 2.0 add_convert_fusion.3
  60.8 4.0 %collective-permute-done.5 = bf16[512,512]{1,0:T(8,128)(2,1)S(1)} collective-permute-done((bf16[512,512]{1,0:T(8,128)(2,1)}, bf16[512,512]{1,0:T(8,128)(2,1)S(1)}, u32[]{:S(2)}, u32[]{:S(2)}) %collective-permute-start.5) | collective-permute-done | bytes 524320 | tf_op jit(solution)/shard_map/ppermute | solution.py:211
  65.0 1.5 collective-permute-start.6
  66.4 7.3 %collective-permute-done.2 = bf16[512,512]{1,0:T(8,128)(2,1)S(1)} collective-permute-done((bf16[512,512]{1,0:T(8,128)(2,1)S(1)}, bf16[512,512]{1,0:T(8,128)(2,1)S(1)}, u32[]{:S(2)}, u32[]{:S(2)}) %collective-permute-start.2) | collective-permute-done | bytes 524320 | tf_op jit(solution)/shard_map/ppermute | solution.py:211
  77.8 6.4 %backward_rows.4.refs_0_ = f32[2048,512]{1,0:T(8,128)} custom-call(s32[16,16]{1,0:T(8,128)} %idx_ref.23, s32[16]{0:T(128)} %bitcast.11, bf16[16,16,128,128]{3,2,1,0:T(8,128)(2,1)} %t_ref.23, bf16[512,512]{1,0:T(8,128)(2,1)} %broadcast_select_fusion.5.f_ref), custom_call_target="tpu_custom_call" | custom-call | tf_op jit(solution)/shard_map/backward_rows/pallas_call | solution.py:92
  88.1 1.5 collective-permute-start.4
  89.6 1.9 broadcast_select_fusion.4.f_ref
  91.5 7.6 %backward_rows.5.refs_0_ = f32[2048,512]{1,0:T(8,128)} custom-call(s32[16,16]{1,0:T(8,128)} %idx_ref.23, s32[16]{0:T(128)} %bitcast.12, bf16[16,16,128,128]{3,2,1,0:T(8,128)(2,1)} %t_ref.23, bf16[512,512]{1,0:T(8,128)(2,1)} %broadcast_select_fusion.4.f_ref, f32[2048,512]{1,0:T(8,128)} %backward_rows.4.refs_0_), custom_call_target="tpu_custom_call" | custom-call | tf_op jit(solution)/shard_map/backward_rows/pallas_call | solution.py:92
  99.1 4.7 %collective-permute-done.7 = bf16[512,512]{1,0:T(8,128)(2,1)S(1)} collective-permute-done((bf16[512,512]{1,0:T(8,128)(2,1)S(1)}, bf16[512,512]{1,0:T(8,128)(2,1)S(1)}, u32[]{:S(2)}, u32[]{:S(2)}) %collective-permute-start.7) | collective-permute-done | bytes 524320 | tf_op jit(solution)/shard_map/ppermute | solution.py:226
  104.7 7.7 %backward_rows.6.refs_0_ = f32[2048,512]{1,0:T(8,128)} custom-call(s32[16,16]{1,0:T(8,128)} %idx_ref.23, s32[16]{0:T(128)} %bitcast.13, bf16[16,16,128,128]{3,2,1,0:T(8,128)(2,1)} %t_ref.23, bf16[512,512]{1,0:T(8,128)(2,1)} %broadcast_select_fusion.3.f_ref, f32[2048,512]{1,0:T(8,128)} %backward_rows.5.refs_0_), custom_call_target="tpu_custom_call" | custom-call | tf_op jit(solution)/shard_map/backward_rows/pallas_call | solution.py:92
  112.4 1.6 collective-permute-done.4
  114.1 1.8 fusion.5
  117.1 7.6 %backward_rows.7 = f32[2048,512]{1,0:T(8,128)} custom-call(s32[16,16]{1,0:T(8,128)} %idx_ref.23, s32[16]{0:T(128)} %bitcast.14, bf16[16,16,128,128]{3,2,1,0:T(8,128)(2,1)} %t_ref.23, bf16[512,512]{1,0:T(8,128)(2,1)} %copy-done.8, f32[2048,512]{1,0:T(8,128)} %backward_rows.6.refs_0_), custom_call_target="tpu_custom_call" | custom-call | tf_op jit(solution)/shard_map/backward_rows/pallas_call | solution.py:92
  124.7 1.8 constant_dynamic-slice_fusion.7
  126.4 1.5 collective-permute-start.12
  129.2 6.3 %collective-permute-done.16 = f32[128,512]{1,0:T(8,128)S(1)} collective-permute-done((f32[128,512]{1,0:T(8,128)S(1)}, f32[128,512]{1,0:T(8,128)S(1)}, u32[]{:S(2)}, u32[]{:S(2)}) %collective-permute-start.16) | collective-permute-done | bytes 262176 | tf_op jit(solution)/shard_map/ppermute | solution.py:259
  136.6 4.0 %collective-permute-done.17 = f32[64,512]{1,0:T(8,128)S(1)} collective-permute-done((f32[64,512]{1,0:T(8,128)S(1)}, f32[64,512]{1,0:T(8,128)S(1)}, u32[]{:S(2)}, u32[]{:S(2)}) %collective-permute-start.17) | collective-permute-done | bytes 131104 | tf_op jit(solution)/shard_map/ppermute | solution.py:259
  140.7 5.0 %collective-permute-done.18 = f32[64,512]{1,0:T(8,128)S(1)} collective-permute-done((f32[64,512]{1,0:T(8,128)S(1)}, f32[64,512]{1,0:T(8,128)S(1)}, u32[]{:S(2)}, u32[]{:S(2)}) %collective-permute-start.18) | collective-permute-done | bytes 131104 | tf_op jit(solution)/shard_map/ppermute | solution.py:236
  147.1 5.4 %collective-permute-done.19 = f32[64,512]{1,0:T(8,128)S(1)} collective-permute-done((f32[64,512]{1,0:T(8,128)S(1)}, f32[64,512]{1,0:T(8,128)S(1)}, u32[]{:S(2)}, u32[]{:S(2)}) %collective-permute-start.19) | collective-permute-done | bytes 131104 | tf_op jit(solution)/shard_map/ppermute | solution.py:236
  153.9 5.1 %collective-permute-done.20 = f32[64,512]{1,0:T(8,128)S(1)} collective-permute-done((f32[64,512]{1,0:T(8,128)S(1)}, f32[64,512]{1,0:T(8,128)S(1)}, u32[]{:S(2)}, u32[]{:S(2)}) %collective-permute-start.20) | collective-permute-done | bytes 131104 | tf_op jit(solution)/shard_map/ppermute | solution.py:268
  160.4 2.7 dynamic-slice_add_fusion
  163.9 1.6 collective-permute-done.21
  167.4 5.7 %collective-permute-done.13 = bf16[512,512]{1,0:T(8,128)(2,1)} collective-permute-done((bf16[512,512]{1,0:T(8,128)(2,1)S(1)}, bf16[512,512]{1,0:T(8,128)(2,1)}, u32[]{:S(2)}, u32[]{:S(2)}) %collective-permute-start.13) | collective-permute-done | bytes 524320 | tf_op jit(solution)/shard_map/ppermute | solution.py:259
  174.3 2.5 collective-permute-start.14
  179.1 30.2 %factorize.2 = (f32[512,512]{1,0:T(8,128)}, f32[512,512]{1,0:T(8,128)}) custom-call(f32[512,512]{1,0:T(8,128)} %pad_maximum_fusion.1.g_ref), custom_call_target="tpu_custom_call" | custom-call | tf_op jit(solution)/shard_map/factorize/pallas_call | solution.py:197
  209.3 2.3 convolution_convert_fusion
  211.7 9.2 %collective-permute-done.23 = bf16[256,512]{1,0:T(8,128)(2,1)S(1)} collective-permute-done((bf16[256,512]{1,0:T(8,128)(2,1)S(1)}, bf16[256,512]{1,0:T(8,128)(2,1)S(1)}, u32[]{:S(2)}, u32[]{:S(2)}) %collective-permute-start.23) | collective-permute-done | bytes 262176 | tf_op jit(solution)/shard_map/ppermute | solution.py:268
  221.0 9.2 %collective-permute-done.24 = bf16[512,512]{1,0:T(8,128)(2,1)S(1)} collective-permute-done((bf16[512,512]{1,0:T(8,128)(2,1)S(1)}, bf16[512,512]{1,0:T(8,128)(2,1)S(1)}, u32[]{:S(2)}, u32[]{:S(2)}) %collective-permute-start.24) | collective-permute-done | bytes 524320 | tf_op jit(solution)/shard_map/ppermute | solution.py:268
  230.6 2.6 collective-permute-done.25
  233.6 1.5 pad_maximum_fusion.x_ref
  235.0 5.8 %forward_rows.15 = f32[512,512]{1,0:T(8,128)} custom-call(s32[1]{0:T(128)} %bitcast.4.base_ref, s32[16,16]{1,0:T(8,128)} %idx_ref.23, s32[16]{0:T(128)} %bitcast.15, bf16[16,16,128,128]{3,2,1,0:T(8,128)(2,1)} %t_ref.23, bf16[2048,512]{1,0:T(8,128)(2,1)} %pad_maximum_fusion.x_ref), custom_call_target="tpu_custom_call" | custom-call | tf_op jit(solution)/shard_map/forward_rows/pallas_call | solution.py:42
  242.1 1.6 collective-permute-start.26
  244.5 5.9 %forward_rows.13 = f32[512,512]{1,0:T(8,128)} custom-call(s32[1]{0:T(128)} %bitcast.2.base_ref, s32[16,16]{1,0:T(8,128)} %idx_ref.23, s32[16]{0:T(128)} %bitcast.16, bf16[16,16,128,128]{3,2,1,0:T(8,128)(2,1)} %t_ref.23, bf16[2048,512]{1,0:T(8,128)(2,1)} %pad_maximum_fusion.x_ref), custom_call_target="tpu_custom_call" | custom-call | tf_op jit(solution)/shard_map/forward_rows/pallas_call | solution.py:42
  250.4 4.9 %collective-permute-done.26 = bf16[512,512]{1,0:T(8,128)(2,1)S(1)} collective-permute-done((bf16[512,512]{1,0:T(8,128)(2,1)S(1)}, bf16[512,512]{1,0:T(8,128)(2,1)S(1)}, u32[]{:S(2)}, u32[]{:S(2)}) %collective-permute-start.26) | collective-permute-done | bytes 524320 | tf_op jit(solution)/shard_map/ppermute | solution.py:307
  255.3 1.6 add_convert_fusion
  256.8 4.4 %collective-permute-start.28 = (bf16[512,512]{1,0:T(8,128)(2,1)S(1)}, bf16[512,512]{1,0:T(8,128)(2,1)S(1)}, u32[]{:S(2)}, u32[]{:S(2)}) collective-permute-start(bf16[512,512]{1,0:T(8,128)(2,1)S(1)} %get-tuple-element.55), channel_id=1, source_target_pairs={{0,1},{1,2},{4,5},{5,6},{8,9},{9,10},{12,13},{13,14},{16,17},{17,1... | collective-permute-start | bytes 1572872 | tf_op jit(solution)/shard_map/ppermute | solution.py:307
  262.0 5.9 %forward_rows.14 = f32[512,512]{1,0:T(8,128)} custom-call(s32[1]{0:T(128)} %bitcast.3.base_ref, s32[16,16]{1,0:T(8,128)} %idx_ref.23, s32[16]{0:T(128)} %bitcast.17, bf16[16,16,128,128]{3,2,1,0:T(8,128)(2,1)} %t_ref.23, bf16[2048,512]{1,0:T(8,128)(2,1)} %pad_maximum_fusion.x_ref), custom_call_target="tpu_custom_call" | custom-call | tf_op jit(solution)/shard_map/forward_rows/pallas_call | solution.py:42
  267.9 4.0 %collective-permute-done.28 = bf16[512,512]{1,0:T(8,128)(2,1)S(1)} collective-permute-done((bf16[512,512]{1,0:T(8,128)(2,1)S(1)}, bf16[512,512]{1,0:T(8,128)(2,1)S(1)}, u32[]{:S(2)}, u32[]{:S(2)}) %collective-permute-start.28) | collective-permute-done | bytes 524320 | tf_op jit(solution)/shard_map/ppermute | solution.py:307
  271.9 2.9 convert_add_fusion
  274.8 8.6 %collective-permute-start.30 = (f32[512,512]{1,0:T(8,128)}, f32[512,512]{1,0:T(8,128)S(1)}, u32[]{:S(2)}, u32[]{:S(2)}) collective-permute-start(f32[512,512]{1,0:T(8,128)} %get-tuple-element.53), channel_id=1, source_target_pairs={{0,1},{1,2},{2,3},{4,5},{5,6},{6,7},{8,9},{9,10},{10,11},{12,13},{... | collective-permute-start | bytes 3145736 | tf_op jit(solution)/shard_map/ppermute | solution.py:307
  284.7 5.8 %forward_rows.12 = f32[512,512]{1,0:T(8,128)} custom-call(s32[1]{0:T(128)} %bitcast.base_ref, s32[16,16]{1,0:T(8,128)} %idx_ref.23, s32[16]{0:T(128)} %bitcast.18, bf16[16,16,128,128]{3,2,1,0:T(8,128)(2,1)} %t_ref.23, bf16[2048,512]{1,0:T(8,128)(2,1)} %pad_maximum_fusion.x_ref), custom_call_target="tpu_custom_call" | custom-call | tf_op jit(solution)/shard_map/forward_rows/pallas_call | solution.py:42
  290.5 14.2 %collective-permute-done.30 = f32[512,512]{1,0:T(8,128)S(1)} collective-permute-done((f32[512,512]{1,0:T(8,128)}, f32[512,512]{1,0:T(8,128)S(1)}, u32[]{:S(2)}, u32[]{:S(2)}) %collective-permute-start.30) | collective-permute-done | bytes 1048608 | tf_op jit(solution)/shard_map/ppermute | solution.py:307
  304.7 4.1 %collective-permute-done.31 = f32[512,512]{1,0:T(8,128)S(1)} collective-permute-done((f32[512,512]{1,0:T(8,128)}, f32[512,512]{1,0:T(8,128)S(1)}, u32[]{:S(2)}, u32[]{:S(2)}) %collective-permute-start.31) | collective-permute-done | bytes 1048608 | tf_op jit(solution)/shard_map/ppermute | solution.py:308
  308.8 3.6 fusion.13
  312.5 1.9 collective-permute-done.32
  314.6 6.4 %collective-permute-done.33 = f32[128,512]{1,0:T(8,128)S(1)} collective-permute-done((f32[128,512]{1,0:T(8,128)S(1)}, f32[128,512]{1,0:T(8,128)S(1)}, u32[]{:S(2)}, u32[]{:S(2)}) %collective-permute-start.33) | collective-permute-done | bytes 262176 | tf_op jit(solution)/shard_map/ppermute | solution.py:259
  321.1 5.0 %collective-permute-done.34 = f32[64,512]{1,0:T(8,128)S(1)} collective-permute-done((f32[64,512]{1,0:T(8,128)S(1)}, f32[64,512]{1,0:T(8,128)S(1)}, u32[]{:S(2)}, u32[]{:S(2)}) %collective-permute-start.34) | collective-permute-done | bytes 131104 | tf_op jit(solution)/shard_map/ppermute | solution.py:259
  326.4 4.7 %collective-permute-done.35 = f32[64,512]{1,0:T(8,128)S(1)} collective-permute-done((f32[64,512]{1,0:T(8,128)S(1)}, f32[64,512]{1,0:T(8,128)S(1)}, u32[]{:S(2)}, u32[]{:S(2)}) %collective-permute-start.35) | collective-permute-done | bytes 131104 | tf_op jit(solution)/shard_map/ppermute | solution.py:236
  331.2 7.2 %collective-permute-done.36 = f32[64,512]{1,0:T(8,128)S(1)} collective-permute-done((f32[64,512]{1,0:T(8,128)S(1)}, f32[64,512]{1,0:T(8,128)S(1)}, u32[]{:S(2)}, u32[]{:S(2)}) %collective-permute-start.36) | collective-permute-done | bytes 131104 | tf_op jit(solution)/shard_map/ppermute | solution.py:236
  338.5 6.4 %collective-permute-done.37 = f32[64,512]{1,0:T(8,128)S(1)} collective-permute-done((f32[64,512]{1,0:T(8,128)S(1)}, f32[64,512]{1,0:T(8,128)S(1)}, u32[]{:S(2)}, u32[]{:S(2)}) %collective-permute-start.37) | collective-permute-done | bytes 131104 | tf_op jit(solution)/shard_map/ppermute | solution.py:268
  345.0 6.4 %collective-permute-done.38 = f32[128,512]{1,0:T(8,128)S(1)} collective-permute-done((f32[128,512]{1,0:T(8,128)S(1)}, f32[128,512]{1,0:T(8,128)S(1)}, u32[]{:S(2)}, u32[]{:S(2)}) %collective-permute-start.38) | collective-permute-done | bytes 262176 | tf_op jit(solution)/shard_map/ppermute | solution.py:268
  351.5 1.9 collective-permute-done.39
  354.6 30.2 %factorize.3 = (f32[512,512]{1,0:T(8,128)}, f32[512,512]{1,0:T(8,128)}) custom-call(f32[512,512]{1,0:T(8,128)} %pad_maximum_fusion.3.g_ref), custom_call_target="tpu_custom_call" | custom-call | tf_op jit(solution)/shard_map/factorize/pallas_call | solution.py:197
  384.8 4.1 %fusion.12 = f32[512,512]{1,0:T(8,128)} fusion(f32[512,512]{1,0:T(8,128)} %get-tuple-element.50, f32[512,512]{1,0:T(8,128)S(1)} %collective-permute-done.31, f32[512,512]{1,0:T(8,128)S(1)} %copy-done.3, f32[512,512]{1,0:T(8,128)S(1)} %collective-permute-done.30), kind=kOutput, calls=%fused_computation.77 | convolution fusion | flops 1611137024 | bytes 5242880 | tf_op jit(solution)/shard_map/dot_general | solution.py:359
  (126 shorter events, 45.0 us)
Async XLA Ops:
  7.7 17.3 %collective-permute-start = (bf16[512,512]{1,0:T(8,128)(2,1)S(1)}, bf16[512,512]{1,0:T(8,128)(2,1)S(1)}, u32[]{:S(2)}, u32[]{:S(2)}) collective-permute-start(bf16[512,512]{1,0:T(8,128)(2,1)S(1)} %convert_element_type.91), channel_id=1, source_target_pairs={{0,1},{3,2},{4,5},{7,6},{8,9},{11,10},{12,13},{15,14},{16,17},{19,... | collective-permute-start | bytes 1572872 | tf_op jit(solution)/shard_map/ppermute | solution.py:211
  18.5 6.5 %copy-start.5 = (f32[512,512]{1,0:T(8,128)S(1)}, f32[512,512]{1,0:T(8,128)}, u32[]{:S(2)}) copy-start(f32[512,512]{1,0:T(8,128)} %forward_rows.8) | copy-start | bytes 3145732
  19.9 15.5 %collective-permute-start.1 = (bf16[512,512]{1,0:T(8,128)(2,1)S(1)}, bf16[512,512]{1,0:T(8,128)(2,1)}, u32[]{:S(2)}, u32[]{:S(2)}) collective-permute-start(bf16[512,512]{1,0:T(8,128)(2,1)S(1)} %convert_element_type.93), channel_id=1, source_target_pairs={{0,1},{3,2},{4,5},{7,6},{8,9},{11,10},{12,13},{15,14},{16,17},{19,... | collective-permute-start | bytes 1572872 | tf_op jit(solution)/shard_map/ppermute | solution.py:211
  26.0 28.8 %collective-permute-start.10 = (bf16[512,512]{1,0:T(8,128)(2,1)}, bf16[512,512]{1,0:T(8,128)(2,1)}, u32[]{:S(2)}, u32[]{:S(2)}) collective-permute-start(bf16[512,512]{1,0:T(8,128)(2,1)} %convert_element_type.108), channel_id=1, source_target_pairs={{1,2},{2,1},{5,6},{6,5},{9,10},{10,9},{13,14},{14,13},{17,18},{18,... | collective-permute-start | bytes 1572872 | tf_op jit(solution)/shard_map/ppermute | solution.py:218
  33.2 6.0 %copy-start = (f32[512,512]{1,0:T(8,128)S(1)}, f32[512,512]{1,0:T(8,128)}, u32[]{:S(2)}) copy-start(f32[512,512]{1,0:T(8,128)} %forward_rows.10) | copy-start | bytes 3145732
  37.8 19.7 %collective-permute-start.8 = (bf16[512,512]{1,0:T(8,128)(2,1)}, bf16[512,512]{1,0:T(8,128)(2,1)}, u32[]{:S(2)}, u32[]{:S(2)}) collective-permute-start(bf16[512,512]{1,0:T(8,128)(2,1)} %convert_element_type.105), channel_id=1, source_target_pairs={{1,2},{2,1},{5,6},{6,5},{9,10},{10,9},{13,14},{14,13},{17,18},{18,... | collective-permute-start | bytes 1572872 | tf_op jit(solution)/shard_map/ppermute | solution.py:218
  45.9 18.9 %collective-permute-start.5 = (bf16[512,512]{1,0:T(8,128)(2,1)}, bf16[512,512]{1,0:T(8,128)(2,1)S(1)}, u32[]{:S(2)}, u32[]{:S(2)}) collective-permute-start(bf16[512,512]{1,0:T(8,128)(2,1)} %convert_element_type.100), channel_id=1, source_target_pairs={{0,1},{3,2},{4,5},{7,6},{8,9},{11,10},{12,13},{15,14},{16,17},{19,... | collective-permute-start | bytes 1572872 | tf_op jit(solution)/shard_map/ppermute | solution.py:211
  53.5 20.2 %collective-permute-start.2 = (bf16[512,512]{1,0:T(8,128)(2,1)S(1)}, bf16[512,512]{1,0:T(8,128)(2,1)S(1)}, u32[]{:S(2)}, u32[]{:S(2)}) collective-permute-start(bf16[512,512]{1,0:T(8,128)(2,1)S(1)} %convert_element_type.95), channel_id=1, source_target_pairs={{0,1},{3,2},{4,5},{7,6},{8,9},{11,10},{12,13},{15,14},{16,17},{19,... | collective-permute-start | bytes 1572872 | tf_op jit(solution)/shard_map/ppermute | solution.py:211
  56.1 18.5 %copy-start.1 = (f32[512,512]{1,0:T(8,128)S(1)}, f32[512,512]{1,0:T(8,128)}, u32[]{:S(2)}) copy-start(f32[512,512]{1,0:T(8,128)} %forward_rows.11) | copy-start | bytes 3145732
  56.1 20.9 %collective-permute-start.11 = (bf16[512,512]{1,0:T(8,128)(2,1)S(1)}, bf16[512,512]{1,0:T(8,128)(2,1)S(1)}, u32[]{:S(2)}, u32[]{:S(2)}) collective-permute-start(bf16[512,512]{1,0:T(8,128)(2,1)S(1)} %add_convert_fusion.2), channel_id=1, source_target_pairs={{1,0},{2,3},{5,4},{6,7},{9,8},{10,11},{13,12},{14,15},{17,16},{18,... | collective-permute-start | bytes 1572872 | tf_op jit(solution)/shard_map/ppermute | solution.py:226
  59.5 30.1 %collective-permute-start.9 = (bf16[512,512]{1,0:T(8,128)(2,1)}, bf16[512,512]{1,0:T(8,128)(2,1)}, u32[]{:S(2)}, u32[]{:S(2)}) collective-permute-start(bf16[512,512]{1,0:T(8,128)(2,1)} %add_convert_fusion.3), channel_id=1, source_target_pairs={{1,0},{2,3},{5,4},{6,7},{9,8},{10,11},{13,12},{14,15},{17,16},{18,... | collective-permute-start | bytes 1572872 | tf_op jit(solution)/shard_map/ppermute | solution.py:226
  64.8 10.8 %copy-start.13 = (bf16[512,512]{1,0:T(8,128)(2,1)}, bf16[512,512]{1,0:T(8,128)(2,1)S(1)}, u32[]{:S(2)}) copy-start(bf16[512,512]{1,0:T(8,128)(2,1)S(1)} %collective-permute-done.5) | copy-start | bytes 1572868
  65.0 19.3 %collective-permute-start.6 = (bf16[512,512]{1,0:T(8,128)(2,1)S(1)}, bf16[512,512]{1,0:T(8,128)(2,1)}, u32[]{:S(2)}, u32[]{:S(2)}) collective-permute-start(bf16[512,512]{1,0:T(8,128)(2,1)S(1)} %fusion.1), channel_id=1, source_target_pairs={{1,2},{2,1},{5,6},{6,5},{9,10},{10,9},{13,14},{14,13},{17,18},{18,... | collective-permute-start | bytes 1572872 | tf_op jit(solution)/shard_map/ppermute | solution.py:218
  73.8 0.8 copy-start.11
  75.6 11.3 %collective-permute-start.3 = (bf16[512,512]{1,0:T(8,128)(2,1)}, bf16[512,512]{1,0:T(8,128)(2,1)}, u32[]{:S(2)}, u32[]{:S(2)}) collective-permute-start(bf16[512,512]{1,0:T(8,128)(2,1)} %fusion), channel_id=1, source_target_pairs={{1,2},{2,1},{5,6},{6,5},{9,10},{10,9},{13,14},{14,13},{17,18},{18,... | collective-permute-start | bytes 1572872 | tf_op jit(solution)/shard_map/ppermute | solution.py:218
  77.8 6.4 %copy-start.14 = (bf16[512,512]{1,0:T(8,128)(2,1)S(1)}, bf16[512,512]{1,0:T(8,128)(2,1)}, u32[]{:S(2)}) copy-start(bf16[512,512]{1,0:T(8,128)(2,1)} %copy-done.13) | copy-start | bytes 1572868
  84.2 2.6 copy-start.12
  85.5 18.3 %collective-permute-start.7 = (bf16[512,512]{1,0:T(8,128)(2,1)S(1)}, bf16[512,512]{1,0:T(8,128)(2,1)S(1)}, u32[]{:S(2)}, u32[]{:S(2)}) collective-permute-start(bf16[512,512]{1,0:T(8,128)(2,1)S(1)} %add_convert_fusion.4), channel_id=1, source_target_pairs={{1,0},{2,3},{5,4},{6,7},{9,8},{10,11},{13,12},{14,15},{17,16},{18,... | collective-permute-start | bytes 1572872 | tf_op jit(solution)/shard_map/ppermute | solution.py:226
  88.1 25.9 %collective-permute-start.4 = (bf16[512,512]{1,0:T(8,128)(2,1)S(1)}, bf16[512,512]{1,0:T(8,128)(2,1)S(1)}, u32[]{:S(2)}, u32[]{:S(2)}) collective-permute-start(bf16[512,512]{1,0:T(8,128)(2,1)S(1)} %add_convert_fusion.5), channel_id=1, source_target_pairs={{1,0},{2,3},{5,4},{6,7},{9,8},{10,11},{13,12},{14,15},{17,16},{18,... | collective-permute-start | bytes 1572872 | tf_op jit(solution)/shard_map/ppermute | solution.py:226
  104.7 9.4 %copy-start.7 = (bf16[512,512]{1,0:T(8,128)(2,1)S(1)}, bf16[512,512]{1,0:T(8,128)(2,1)}, u32[]{:S(2)}) copy-start(bf16[512,512]{1,0:T(8,128)(2,1)} %broadcast_select_fusion.5.f_ref) | copy-start | bytes 1572868
  104.7 9.4 %copy-start.9 = (bf16[512,512]{1,0:T(8,128)(2,1)S(1)}, bf16[512,512]{1,0:T(8,128)(2,1)}, u32[]{:S(2)}) copy-start(bf16[512,512]{1,0:T(8,128)(2,1)} %broadcast_select_fusion.4.f_ref) | copy-start | bytes 1572868
  104.7 9.4 %copy-start.10 = (bf16[512,512]{1,0:T(8,128)(2,1)S(1)}, bf16[512,512]{1,0:T(8,128)(2,1)}, u32[]{:S(2)}) copy-start(bf16[512,512]{1,0:T(8,128)(2,1)} %broadcast_select_fusion.3.f_ref) | copy-start | bytes 1572868
  114.1 2.9 copy-start.8
  116.0 1.0 copy-start.15
  117.0 10.9 %collective-permute-start.15 = (f32[256,512]{1,0:T(8,128)S(1)}, f32[256,512]{1,0:T(8,128)S(1)}, u32[]{:S(2)}, u32[]{:S(2)}) collective-permute-start(f32[256,512]{1,0:T(8,128)S(1)} %constant_dynamic-slice_fusion.5), channel_id=1, source_target_pairs={{0,4},{4,0},{8,12},{12,8},{16,20},{20,16},{24,28},{28,24},{1,5},{5... | collective-permute-start | bytes 1572872 | tf_op jit(solution)/shard_map/ppermute | solution.py:259
  126.4 33.9 %collective-permute-start.12 = (f32[1024,512]{1,0:T(8,128)S(1)}, f32[1024,512]{1,0:T(8,128)}, u32[]{:S(2)}, u32[]{:S(2)}) collective-permute-start(f32[1024,512]{1,0:T(8,128)S(1)} %constant_dynamic-slice_fusion.7), channel_id=1, source_target_pairs={{0,4},{4,0},{8,12},{12,8},{16,20},{20,16},{24,28},{28,24},{1,5},{5... | collective-permute-start | bytes 6291464 | tf_op jit(solution)/shard_map/ppermute | solution.py:259
  129.1 6.4 %collective-permute-start.16 = (f32[128,512]{1,0:T(8,128)S(1)}, f32[128,512]{1,0:T(8,128)S(1)}, u32[]{:S(2)}, u32[]{:S(2)}) collective-permute-start(f32[128,512]{1,0:T(8,128)S(1)} %constant_dynamic-slice_fusion.4), channel_id=1, source_target_pairs={{0,8},{4,20},{8,0},{12,28},{16,24},{20,4},{24,16},{28,12},{1,9},{5... | collective-permute-start | bytes 786440 | tf_op jit(solution)/shard_map/ppermute | solution.py:259
  135.6 5.0 %collective-permute-start.17 = (f32[64,512]{1,0:T(8,128)S(1)}, f32[64,512]{1,0:T(8,128)S(1)}, u32[]{:S(2)}, u32[]{:S(2)}) collective-permute-start(f32[64,512]{1,0:T(8,128)S(1)} %constant_dynamic-slice_fusion.3), channel_id=1, source_target_pairs={{0,16},{4,12},{8,24},{12,4},{16,0},{20,28},{24,8},{28,20},{1,17},{... | collective-permute-start | bytes 393224 | tf_op jit(solution)/shard_map/ppermute | solution.py:259
  140.6 5.0 %collective-permute-start.18 = (f32[64,512]{1,0:T(8,128)S(1)}, f32[64,512]{1,0:T(8,128)S(1)}, u32[]{:S(2)}, u32[]{:S(2)}) collective-permute-start(f32[64,512]{1,0:T(8,128)S(1)} %dynamic-slice_add_fusion.6), channel_id=1, source_target_pairs={{0,1},{1,0},{2,3},{3,2},{4,5},{5,4},{6,7},{7,6},{8,9},{9,8},{10,11... | collective-permute-start | bytes 393224 | tf_op jit(solution)/shard_map/ppermute | solution.py:236
  145.7 6.8 %collective-permute-start.19 = (f32[64,512]{1,0:T(8,128)S(1)}, f32[64,512]{1,0:T(8,128)S(1)}, u32[]{:S(2)}, u32[]{:S(2)}) collective-permute-start(f32[64,512]{1,0:T(8,128)S(1)} %add.153), channel_id=1, source_target_pairs={{0,2},{1,3},{2,0},{3,1},{4,6},{5,7},{6,4},{7,5},{8,10},{9,11},{10,... | collective-permute-start | bytes 393224 | tf_op jit(solution)/shard_map/ppermute | solution.py:236
  152.5 6.4 %collective-permute-start.20 = (f32[64,512]{1,0:T(8,128)S(1)}, f32[64,512]{1,0:T(8,128)S(1)}, u32[]{:S(2)}, u32[]{:S(2)}) collective-permute-start(f32[64,512]{1,0:T(8,128)S(1)} %add.154), channel_id=1, source_target_pairs={{0,16},{4,12},{8,24},{12,4},{16,0},{20,28},{24,8},{28,20},{1,17},{... | collective-permute-start | bytes 393224 | tf_op jit(solution)/shard_map/ppermute | solution.py:268
  159.0 6.5 %collective-permute-start.21 = (f32[128,512]{1,0:T(8,128)S(1)}, f32[128,512]{1,0:T(8,128)}, u32[]{:S(2)}, u32[]{:S(2)}) collective-permute-start(f32[128,512]{1,0:T(8,128)S(1)} %pad_maximum_fusion.7), channel_id=1, source_target_pairs={{0,8},{4,20},{8,0},{12,28},{16,24},{20,4},{24,16},{28,12},{1,9},{5... | collective-permute-start | bytes 786440 | tf_op jit(solution)/shard_map/ppermute | solution.py:268
  163.2 9.9 %collective-permute-start.13 = (bf16[512,512]{1,0:T(8,128)(2,1)S(1)}, bf16[512,512]{1,0:T(8,128)(2,1)}, u32[]{:S(2)}, u32[]{:S(2)}) collective-permute-start(bf16[512,512]{1,0:T(8,128)(2,1)S(1)} %dynamic-slice_convert_fusion), channel_id=1, source_target_pairs={{0,8},{4,20},{8,0},{12,28},{16,24},{20,4},{24,16},{28,12},{1,9},{5... | collective-permute-start | bytes 1572872 | tf_op jit(solution)/shard_map/ppermute | solution.py:259
  166.5 0.9 copy-start.6
  167.4 9.4 %collective-permute-start.22 = (f32[256,512]{1,0:T(8,128)}, f32[256,512]{1,0:T(8,128)}, u32[]{:S(2)}, u32[]{:S(2)}) collective-permute-start(f32[256,512]{1,0:T(8,128)} %pad_maximum_fusion.4), channel_id=1, source_target_pairs={{0,4},{4,0},{8,12},{12,8},{16,20},{20,16},{24,28},{28,24},{1,5},{5... | collective-permute-start | bytes 1572872 | tf_op jit(solution)/shard_map/ppermute | solution.py:268
  174.3 35.0 %collective-permute-start.14 = (f32[256,512]{1,0:T(8,128)S(1)}, f32[256,512]{1,0:T(8,128)S(1)}, u32[]{:S(2)}, u32[]{:S(2)}) collective-permute-start(f32[256,512]{1,0:T(8,128)S(1)} %constant_dynamic-slice_fusion.6), channel_id=1, source_target_pairs={{0,16},{4,12},{8,24},{12,4},{16,0},{20,28},{24,8},{28,20},{1,17},{... | collective-permute-start | bytes 1572872 | tf_op jit(solution)/shard_map/ppermute | solution.py:259
  211.6 9.2 %collective-permute-start.23 = (bf16[256,512]{1,0:T(8,128)(2,1)S(1)}, bf16[256,512]{1,0:T(8,128)(2,1)S(1)}, u32[]{:S(2)}, u32[]{:S(2)}) collective-permute-start(bf16[256,512]{1,0:T(8,128)(2,1)S(1)} %convolution_convert_fusion), channel_id=1, source_target_pairs={{0,16},{4,12},{8,24},{12,4},{16,0},{20,28},{24,8},{28,20},{1,17},{... | collective-permute-start | bytes 786440 | tf_op jit(solution)/shard_map/ppermute | solution.py:268
  220.9 9.2 %collective-permute-start.24 = (bf16[512,512]{1,0:T(8,128)(2,1)S(1)}, bf16[512,512]{1,0:T(8,128)(2,1)S(1)}, u32[]{:S(2)}, u32[]{:S(2)}) collective-permute-start(bf16[512,512]{1,0:T(8,128)(2,1)S(1)} %pad_maximum_fusion.5), channel_id=1, source_target_pairs={{0,8},{4,20},{8,0},{12,28},{16,24},{20,4},{24,16},{28,12},{1,9},{5... | collective-permute-start | bytes 1572872 | tf_op jit(solution)/shard_map/ppermute | solution.py:268
  230.5 2.7 collective-permute-start.25
  242.1 13.1 %collective-permute-start.26 = (bf16[512,512]{1,0:T(8,128)(2,1)S(1)}, bf16[512,512]{1,0:T(8,128)(2,1)S(1)}, u32[]{:S(2)}, u32[]{:S(2)}) collective-permute-start(bf16[512,512]{1,0:T(8,128)(2,1)S(1)} %convert_element_type.114), channel_id=1, source_target_pairs={{0,1},{4,5},{8,9},{12,13},{16,17},{20,21},{24,25},{28,29}} | collective-permute-start | bytes 1572872 | tf_op jit(solution)/shard_map/ppermute | solution.py:307
  243.7 11.5 %collective-permute-start.27 = (bf16[512,512]{1,0:T(8,128)(2,1)S(1)}, bf16[512,512]{1,0:T(8,128)(2,1)S(1)}, u32[]{:S(2)}, u32[]{:S(2)}) collective-permute-start(bf16[512,512]{1,0:T(8,128)(2,1)S(1)} %convert_element_type.114), channel_id=1, source_target_pairs={{3,2},{7,6},{11,10},{15,14},{19,18},{23,22},{27,26},{31,30}} | collective-permute-start | bytes 1572872 | tf_op jit(solution)/shard_map/ppermute | solution.py:308
  244.5 10.8 %copy-start.2 = (f32[512,512]{1,0:T(8,128)S(1)}, f32[512,512]{1,0:T(8,128)}, u32[]{:S(2)}) copy-start(f32[512,512]{1,0:T(8,128)} %forward_rows.15) | copy-start | bytes 3145732
  256.8 15.1 %collective-permute-start.28 = (bf16[512,512]{1,0:T(8,128)(2,1)S(1)}, bf16[512,512]{1,0:T(8,128)(2,1)S(1)}, u32[]{:S(2)}, u32[]{:S(2)}) collective-permute-start(bf16[512,512]{1,0:T(8,128)(2,1)S(1)} %get-tuple-element.55), channel_id=1, source_target_pairs={{0,1},{1,2},{4,5},{5,6},{8,9},{9,10},{12,13},{13,14},{16,17},{17,1... | collective-permute-start | bytes 1572872 | tf_op jit(solution)/shard_map/ppermute | solution.py:307
  261.3 10.7 %collective-permute-start.29 = (bf16[512,512]{1,0:T(8,128)(2,1)S(1)}, bf16[512,512]{1,0:T(8,128)(2,1)S(1)}, u32[]{:S(2)}, u32[]{:S(2)}) collective-permute-start(bf16[512,512]{1,0:T(8,128)(2,1)S(1)} %get-tuple-element.54), channel_id=1, source_target_pairs={{3,2},{2,1},{7,6},{6,5},{11,10},{10,9},{15,14},{14,13},{19,18},{18... | collective-permute-start | bytes 1572872 | tf_op jit(solution)/shard_map/ppermute | solution.py:308
  262.0 9.9 %copy-start.4 = (f32[512,512]{1,0:T(8,128)S(1)}, f32[512,512]{1,0:T(8,128)}, u32[]{:S(2)}) copy-start(f32[512,512]{1,0:T(8,128)} %forward_rows.13) | copy-start | bytes 3145732
  274.8 29.9 %collective-permute-start.30 = (f32[512,512]{1,0:T(8,128)}, f32[512,512]{1,0:T(8,128)S(1)}, u32[]{:S(2)}, u32[]{:S(2)}) collective-permute-start(f32[512,512]{1,0:T(8,128)} %get-tuple-element.53), channel_id=1, source_target_pairs={{0,1},{1,2},{2,3},{4,5},{5,6},{6,7},{8,9},{9,10},{10,11},{12,13},{... | collective-permute-start | bytes 3145736 | tf_op jit(solution)/shard_map/ppermute | solution.py:307
  283.4 25.4 %collective-permute-start.31 = (f32[512,512]{1,0:T(8,128)}, f32[512,512]{1,0:T(8,128)S(1)}, u32[]{:S(2)}, u32[]{:S(2)}) collective-permute-start(f32[512,512]{1,0:T(8,128)} %get-tuple-element.52), channel_id=1, source_target_pairs={{3,2},{2,1},{1,0},{7,6},{6,5},{5,4},{11,10},{10,9},{9,8},{15,14},{... | collective-permute-start | bytes 3145736 | tf_op jit(solution)/shard_map/ppermute | solution.py:308
  312.4 2.0 collective-permute-start.32
  314.5 6.4 %collective-permute-start.33 = (f32[128,512]{1,0:T(8,128)S(1)}, f32[128,512]{1,0:T(8,128)S(1)}, u32[]{:S(2)}, u32[]{:S(2)}) collective-permute-start(f32[128,512]{1,0:T(8,128)S(1)} %constant_dynamic-slice_fusion.1), channel_id=1, source_target_pairs={{0,8},{4,20},{8,0},{12,28},{16,24},{20,4},{24,16},{28,12},{1,9},{5... | collective-permute-start | bytes 786440 | tf_op jit(solution)/shard_map/ppermute | solution.py:259
  321.0 5.0 %collective-permute-start.34 = (f32[64,512]{1,0:T(8,128)S(1)}, f32[64,512]{1,0:T(8,128)S(1)}, u32[]{:S(2)}, u32[]{:S(2)}) collective-permute-start(f32[64,512]{1,0:T(8,128)S(1)} %constant_dynamic-slice_fusion), channel_id=1, source_target_pairs={{0,16},{4,12},{8,24},{12,4},{16,0},{20,28},{24,8},{28,20},{1,17},{... | collective-permute-start | bytes 393224 | tf_op jit(solution)/shard_map/ppermute | solution.py:259
  326.1 5.0 %collective-permute-start.35 = (f32[64,512]{1,0:T(8,128)S(1)}, f32[64,512]{1,0:T(8,128)S(1)}, u32[]{:S(2)}, u32[]{:S(2)}) collective-permute-start(f32[64,512]{1,0:T(8,128)S(1)} %dynamic-slice_add_fusion.5), channel_id=1, source_target_pairs={{0,1},{1,0},{2,3},{3,2},{4,5},{5,4},{6,7},{7,6},{8,9},{9,8},{10,11... | collective-permute-start | bytes 393224 | tf_op jit(solution)/shard_map/ppermute | solution.py:236
  331.1 7.3 %collective-permute-start.36 = (f32[64,512]{1,0:T(8,128)S(1)}, f32[64,512]{1,0:T(8,128)S(1)}, u32[]{:S(2)}, u32[]{:S(2)}) collective-permute-start(f32[64,512]{1,0:T(8,128)S(1)} %add.164), channel_id=1, source_target_pairs={{0,2},{1,3},{2,0},{3,1},{4,6},{5,7},{6,4},{7,5},{8,10},{9,11},{10,... | collective-permute-start | bytes 393224 | tf_op jit(solution)/shard_map/ppermute | solution.py:236
  338.5 6.4 %collective-permute-start.37 = (f32[64,512]{1,0:T(8,128)S(1)}, f32[64,512]{1,0:T(8,128)S(1)}, u32[]{:S(2)}, u32[]{:S(2)}) collective-permute-start(f32[64,512]{1,0:T(8,128)S(1)} %add.165), channel_id=1, source_target_pairs={{0,16},{4,12},{8,24},{12,4},{16,0},{20,28},{24,8},{28,20},{1,17},{... | collective-permute-start | bytes 393224 | tf_op jit(solution)/shard_map/ppermute | solution.py:268
  344.9 6.4 %collective-permute-start.38 = (f32[128,512]{1,0:T(8,128)S(1)}, f32[128,512]{1,0:T(8,128)S(1)}, u32[]{:S(2)}, u32[]{:S(2)}) collective-permute-start(f32[128,512]{1,0:T(8,128)S(1)} %pad_maximum_fusion.8), channel_id=1, source_target_pairs={{0,8},{4,20},{8,0},{12,28},{16,24},{20,4},{24,16},{28,12},{1,9},{5... | collective-permute-start | bytes 786440 | tf_op jit(solution)/shard_map/ppermute | solution.py:268
  351.5 2.0 collective-permute-start.39
  353.6 31.3 %copy-start.3 = (f32[512,512]{1,0:T(8,128)S(1)}, f32[512,512]{1,0:T(8,128)}, u32[]{:S(2)}) copy-start(f32[512,512]{1,0:T(8,128)} %forward_rows.12) | copy-start | bytes 3145732

commit v3 on v2

--- a/solution.py
+++ b/solution.py
@@ -56,15 +56,20 @@
     )(jnp.full((1,), base, jnp.int32), col_index, counts, tiles, x)
 
 
-def backward_body(group, base, first, idx_ref, cnt_ref, t_ref, f_ref, *refs):
+def backward_body(group, base, panels, idx_ref, cnt_ref, t_ref, *refs):
     z_ref = refs[-1]
     tile = t_ref.shape[2]
-    row = pl.program_id(0) + base
+    at = pl.program_id(0)
+    each = pl.num_programs(0) // panels
+    row = at + base
     count = cnt_ref[row]
-
-    @pl.when(pl.program_id(0) == 0)
+    f = refs[0][...]
+    for k in range(1, panels):
+        f = jnp.where(at >= k * each, refs[k][...], f)
+
+    @pl.when(at == 0)
     def _():
-        z_ref[...] = jnp.zeros_like(z_ref) if first else refs[0][...]
+        z_ref[...] = refs[panels][...] if len(refs) > panels + 1 else jnp.zeros_like(z_ref)
 
     def step(p, carry):
         lhs = []
@@ -73,7 +78,7 @@
             t = t_ref[0, s]
             lhs.append(t if q == 0 else jnp.where(s < count, t, jnp.zeros_like(t)))
         out = lax.dot_general(
-            jnp.concatenate(lhs, 1), f_ref[...], TN, preferred_element_type=jnp.float32
+            jnp.concatenate(lhs, 1), f, TN, preferred_element_type=jnp.float32
         )
         for q in range(group):
             c = pl.multiple_of(idx_ref[row, p * group + q] * tile, tile)
@@ -83,26 +88,30 @@
     lax.fori_loop(0, (count + group - 1) // group, step, 0)
 
 
-def backward(tiles, col_index, counts, panel, col_rows, base, total):
+def backward(tiles, col_index, counts, panels, col_rows, base, total):
     slots, tile = tiles.shape[1], tiles.shape[2]
-    width = panel.shape[1]
+    width = panels[0].shape[1]
+    each = panels[0].shape[0] // tile
     group = next(g for g in (4, 2, 1) if slots % g == 0)
     whole = pl.BlockSpec((col_rows, width), lambda r, *_: (0, 0), pipeline_mode=pl.Buffered(1))
     more = () if total is None else (total,)
+
+    def panel_map(k):
+        return lambda r, *_: (jnp.clip(r - k * each, 0, each - 1), 0)
+
     return pl.pallas_call(
-        functools.partial(backward_body, group, base, total is None),
+        functools.partial(backward_body, group, base, len(panels)),
         out_shape=jax.ShapeDtypeStruct((col_rows, width), jnp.float32),
         grid_spec=pltpu.PrefetchScalarGridSpec(
             num_scalar_prefetch=2,
-            grid=(panel.shape[0] // tile,),
-            in_specs=[
-                pl.BlockSpec((1, slots, tile, tile), lambda r, *_: (r + base, 0, 0, 0)),
-                pl.BlockSpec((tile, width), lambda r, *_: (r, 0)),
-            ] + [whole] * len(more),
+            grid=(each * len(panels),),
+            in_specs=[pl.BlockSpec((1, slots, tile, tile), lambda r, *_: (r + base, 0, 0, 0))]
+            + [pl.BlockSpec((tile, width), panel_map(k)) for k in range(len(panels))]
+            + [whole] * len(more),
             out_specs=pl.BlockSpec((col_rows, width), lambda r, *_: (0, 0)),
         ),
         name="backward_rows",
-    )(col_index, counts, tiles, panel, *more)
+    )(col_index, counts, tiles, *panels, *more)
 
 
 def factor_block(read, r_ref, t_ref, group):
@@ -161,33 +170,44 @@
             e[v] = e[v] - ue
 
 
-def chol_body(scale, group, g_ref, r_ref, t_ref, a_ref, rk_ref, tk_ref):
+def chol_body(scale, group, g_ref, r_ref, t_ref, w_ref, rk_ref, tk_ref):
     n = g_ref.shape[0]
     b = 128
-    a_ref[...] = g_ref[...] * scale
-    rows = lax.broadcasted_iota(jnp.int32, (n, n), 0)
-    cols = lax.broadcasted_iota(jnp.int32, (n, n), 1)
-    t_ref[...] = jnp.where(rows == cols, 1.0, 0.0).astype(jnp.float32)
+    w_ref[...] = g_ref[...] * scale
 
     def block(k, carry):
         at = pl.multiple_of(k * b, b)
-        factor_block(lambda v: a_ref[pl.ds(pl.multiple_of(at + 8 * v, 8), 8), pl.ds(at, b)], rk_ref, tk_ref, group)
+
+        def read(v):
+            return w_ref[pl.ds(pl.multiple_of(at + 8 * v, 8), 8), pl.ds(at, b)]
+
+        factor_block(read, rk_ref, tk_ref, group)
         inv = tk_ref[...]
-        rp = jnp.dot(inv, a_ref[pl.ds(at, b), :], precision=HI, preferred_element_type=jnp.float32)
-        ep = jnp.dot(inv, t_ref[pl.ds(at, b), :], precision=HI, preferred_element_type=jnp.float32)
-        row = lax.broadcasted_iota(jnp.int32, rp.shape, 0) + at
-        col = lax.broadcasted_iota(jnp.int32, rp.shape, 1)
-        r_ref[pl.ds(at, b), :] = jnp.where(col >= row, rp, 0.0)
-        t_ref[pl.ds(at, b), :] = jnp.where(col <= row, ep, 0.0)
+        x = jnp.dot(inv, w_ref[pl.ds(at, b), :], precision=HI, preferred_element_type=jnp.float32)
+        row = lax.broadcasted_iota(jnp.int32, x.shape, 0) + at
+        col = lax.broadcasted_iota(jnp.int32, x.shape, 1)
+        r_ref[pl.ds(at, b), :] = jnp.where(col >= at + b, x, 0.0)
+        r_ref[pl.ds(at, b), pl.ds(at, b)] = jnp.where(
+            col[:, :b] >= row[:, :b] - at, rk_ref[...], 0.0
+        )
+        inv = jnp.where(col[:, :b] <= row[:, :b] - at, inv, 0.0)
+        t_ref[pl.ds(at, b), :] = jnp.where(col < at, x, 0.0)
+        t_ref[pl.ds(at, b), pl.ds(at, b)] = inv
+        w_ref[pl.ds(at, b), :] = x
+        w_ref[pl.ds(at, b), pl.ds(at, b)] = inv
 
         def below(i, carry):
             to = pl.multiple_of(i * b, b)
             l = r_ref[pl.ds(at, b), pl.ds(to, b)]
-            a_ref[pl.ds(to, b), :] -= lax.dot_general(l, r_ref[pl.ds(at, b), :], TN, precision=HI, preferred_element_type=jnp.float32)
-            t_ref[pl.ds(to, b), :] -= lax.dot_general(l, t_ref[pl.ds(at, b), :], TN, precision=HI, preferred_element_type=jnp.float32)
+            w_ref[pl.ds(to, b), pl.ds(at, b)] = jnp.zeros((b, b), jnp.float32)
+            w_ref[pl.ds(to, b), :] -= lax.dot_general(
+                l, w_ref[pl.ds(at, b), :], TN, precision=HI, preferred_element_type=jnp.float32
+            )
             return carry
+
         lax.fori_loop(k + 1, n // b, below, 0)
         return carry
+
     lax.fori_loop(0, n // b, block, 0)
 
 
@@ -197,7 +217,11 @@
     return pl.pallas_call(
         functools.partial(chol_body, scale, group),
         out_shape=(s, s),
-        scratch_shapes=[pltpu.VMEM((n, n), jnp.float32), pltpu.VMEM((128, 128), jnp.float32), pltpu.VMEM((128, 128), jnp.float32)],
+        scratch_shapes=[
+            pltpu.VMEM((n, n), jnp.float32),
+            pltpu.VMEM((128, 128), jnp.float32),
+            pltpu.VMEM((128, 128), jnp.float32),
+        ],
         name="factorize",
     )(gram)
 
@@ -218,16 +242,14 @@
     return (value + lax.ppermute(value.astype(wire), "col", pairs).astype(value.dtype)).astype(wire)
 
 
-def line_outward(value, beside=None):
+def line_outward(value):
     n = lax.axis_size("col")
     z = lax.axis_index("col")
     for s in reversed(range(n // 2 - 1)):
         pairs = [(s + 1, s), (n - 2 - s, n - 1 - s)]
         got = lax.ppermute(value, "col", pairs)
-        if beside is not None:
-            value, beside = lax.optimization_barrier((value, beside))
         value = jnp.where((z == s) | (z == n - 1 - s), got, value)
-    return value, beside
+    return value
 
 
 def col_sum(value):
@@ -249,19 +271,16 @@
         yield pairs, own
 
 
-def row_scatter(value, wires):
+def row_step(value, step, wire):
     bits = lax.axis_size("row").bit_length() - 1
-    offset = jnp.int32(0)
-    for step, (pairs, own) in enumerate(halving(bits)):
-        half = value.shape[0] // 2
-        give = lax.dynamic_slice_in_dim(value, (1 - own) * half, half, 0).astype(wires[min(step, len(wires) - 1)])
-        keep = lax.dynamic_slice_in_dim(value, own * half, half, 0)
-        value = keep + lax.ppermute(give, "row", pairs).astype(value.dtype)
-        offset = offset + own * half
-    return value, offset
-
-
-def row_gather(part, offset, total):
+    pairs, own = list(halving(bits))[step]
+    half = value.shape[0] // 2
+    give = lax.dynamic_slice_in_dim(value, (1 - own) * half, half, 0).astype(wire)
+    keep = lax.dynamic_slice_in_dim(value, own * half, half, 0)
+    return keep + lax.ppermute(give, "row", pairs).astype(value.dtype)
+
+
+def row_gather(part):
     bits = lax.axis_size("row").bit_length() - 1
     steps = list(halving(bits))
     for pairs, own in reversed(steps):
@@ -273,9 +292,9 @@
 
 
 def gram_sum(gram):
-    part, offset = row_scatter(gram, (jnp.float32,))
-    part = col_sum(part)
-    return row_gather(part, offset, gram.shape[0])
+    for step in range(lax.axis_size("row").bit_length() - 1):
+        gram = row_step(gram, step, jnp.float32)
+    return row_gather(col_sum(gram))
 
 
 def share_order(k):
@@ -318,37 +337,56 @@
     z = lax.axis_index("col")
 
     chunk = tile_rows // n_col
-    halves, sums, sent = [], [], []
+    halves, crossed, sent = [], [], []
     for j in range(n_col):
         live = counts
-        if j >= 2:
-            live, halves[j - 2] = lax.optimization_barrier((counts, halves[j - 2]))
+        if j == 2:
+            live, halves[0] = lax.optimization_barrier((counts, halves[0]))
+        elif j > 2:
+            live, crossed[j - 3] = lax.optimization_barrier((counts, crossed[j - 3]))
         part = forward(tiles, col_index, live, sketch, j * chunk, chunk)
         if j >= 1:
             value, got = sent[j - 1]
             value, part = lax.optimization_barrier((value, part))
             halves.append(value + got.astype(value.dtype))
+            if j >= 2:
+                crossed.append(line_across(halves[j - 2], jnp.bfloat16))
         sent.append(line_inward(part, jnp.bfloat16))
     value, got = sent[-1]
     halves.append(value + got.astype(value.dtype))
-    crossed = [line_across(half, jnp.bfloat16) for half in halves]
-    back = None
-    for j in range(n_col):
-        total, back = line_outward(crossed[j], back)
-        sums.append(total)
-        if j < n_col - 1:
-            back = backward(tiles, col_index, counts, total, sketch.shape[0], j * chunk, back)
+    for half in halves[len(crossed):]:
+        crossed.append(line_across(half, jnp.bfloat16))
+    sums = [line_outward(value) for value in crossed]
+    middle = n_col // 2
+    back = backward(tiles, col_index, counts, sums[:middle], sketch.shape[0], 0, None)
+    sums[-1], back = lax.optimization_barrier((sums[-1], back))
     first = jnp.concatenate(sums, 0)
 
     share = first.shape[0] // n_col
     mine = lax.dynamic_slice_in_dim(first, z * share, share, 0)
     gram = lax.dot_general(mine, mine, TN, preferred_element_type=jnp.float32)
-    unused, inverse = cholesky(gram_sum(gram), 1.0 / total_rows)
-
-    back = backward(tiles, col_index, counts, sums[-1], sketch.shape[0], (n_col - 1) * chunk, back)
-    part, offset = row_scatter(back, (jnp.float32, jnp.bfloat16, jnp.float32))
+    wires = (jnp.float32, jnp.bfloat16, jnp.float32)
+    bits = lax.axis_size("row").bit_length() - 1
+    for j in range(middle, n_col):
+        live, gram = lax.optimization_barrier((counts, gram))
+        back = backward(tiles, col_index, live, sums[j:j + 1], sketch.shape[0], j * chunk, back)
+        if j - middle < bits:
+            gram = row_step(gram, j - middle, jnp.float32)
+        gram, back = lax.optimization_barrier((gram, back))
+    part = row_step(back, 0, wires[0])
+    for k in range(min(n_col - middle, bits), bits):
+        gram = row_step(gram, k, jnp.float32)
+    gram = col_sum(gram)
+    gram, part = lax.optimization_barrier((gram, part))
+    if bits > 1:
+        part = row_step(part, 1, wires[1])
+    gram = row_gather(gram)
+    gram, part = lax.optimization_barrier((gram, part))
+    for k in range(2, bits):
+        part = row_step(part, k, wires[2])
+    unused, inverse = cholesky(gram, 1.0 / total_rows)
     part = lax.dot_general(part, inverse, NT, precision=HI, preferred_element_type=jnp.float32)
-    back = row_gather(part.astype(jnp.bfloat16), offset, sketch.shape[0])
+    back = row_gather(part.astype(jnp.bfloat16))
 
     parts = [
         forward(tiles, col_index, counts, back, share_order(k) * chunk, chunk) for k in range(n_col)

time: 392 us -> 370 us (0.944)
  waiting for transfers between devices: 144 us -> 131 us
  Pallas kernels: 136 us -> 126 us
  starting transfers between devices: 54.5 us -> 60.9 us
  other arithmetic: 37.4 us -> 33.4 us
    ppermute x9, waiting for transfers between devices: 29.2 us -> 19.5 us  [row_step(): return keep + lax.ppermute(give, 'row', pairs).astype(value.dtype)]
    ppermute x4, waiting for transfers between devices: 16.5 us -> 7.85 us  [line_inward(): lax.ppermute(value.astype(wire), 'col', [(s, s + 1), (n - 1 - s, n - 2 -...]
    ppermute x4, waiting for transfers between devices: 6.33 us -> 12.5 us  [line_outward(): got = lax.ppermute(value, 'col', pairs)]
    ppermute x9, starting transfers between devices: 6.16 us -> 11.8 us  [row_step(): return keep + lax.ppermute(give, 'row', pairs).astype(value.dtype)]
    pallas_call x2, Pallas kernels: 60.4 us -> 54.8 us  [cholesky(): pl.pallas_call(functools.partial(chol_body, scale, group), out_shape=(s,...]
    pallas_call x4 -> x3, Pallas kernels: 29.3 us -> 24.6 us  [backward(): pl.pallas_call(functools.partial(backward_body, group, base, len(panels))...]
  transfers between devices with their start and end apart: 40 -> 40, of which waited for: 28 -> 26; matrix products, arithmetic and copies ran while one was open for 7% -> 5% of each run, Pallas kernels for 24% -> 24%
where the time goes in v3:
time: 370 us; the launch traced here: 367 us
  waiting for transfers between devices  131 us (35%)
  Pallas kernels  126 us (34%)
  starting transfers between devices  60.9 us (16%)
  other arithmetic  33.4 us (9%)
  matrix products  11.8 us (3%)
    pallas_call x2, Pallas kernels, cholesky(): pl.pallas_call(functools.partial(chol_body, scale, group), out_shape=(s,...  54.8 us
    pallas_call x8, Pallas kernels, forward(): pl.pallas_call(functools.partial(forward_body, group), out_shape=jax.Shap...  46.5 us
    ppermute x9, waiting for transfers between devices, row_gather(): got = lax.ppermute(part, 'row', pairs)  41.2 us
    pallas_call x3, Pallas kernels, backward(): pl.pallas_call(functools.partial(backward_body, group, base, len(panels))...  24.6 us
    ppermute x3, waiting for transfers between devices, line_scatter(): right = lax.ppermute(up.astype(wire), 'col', [(i, i + 1) for i in range(t)])  23.2 us
    ppermute x4, waiting for transfers between devices, col_sum(): lax.ppermute(value, 'col', [(i, i ^ 1 << bit) for i in range(n)])  23.1 us
    ppermute x9, waiting for transfers between devices, row_step(): return keep + lax.ppermute(give, 'row', pairs).astype(value.dtype)  19.5 us
    ppermute x4, starting transfers between devices, line_inward(): lax.ppermute(value.astype(wire), 'col', [(s, s + 1), (n - 1 - s, n - 2 -...  18.2 us
  transfers between devices with their start and end apart: 40, of which 26 were waited for; matrix products, arithmetic and copies ran while one was open for 5% of the time, Pallas kernels for 24%

profile of v3, /device:TPU:0, one launch (start us, length us, event | category | flops | bytes accessed | tf_op | source)
XLA Modules:
  0.0 366.8 jit_solution(14929998725576980394)
XLA Ops:
  0.6 5.8 %forward_rows.8 = f32[512,512]{1,0:T(8,128)} custom-call(s32[1]{0:T(128)} %constant.9.clone.1.base_ref, s32[16,16]{1,0:T(8,128)} %idx_ref.21, s32[16]{0:T(128)} %bitcast.7, bf16[16,16,128,128]{3,2,1,0:T(8,128)(2,1)} %t_ref.21, bf16[2048,512]{1,0:T(8,128)(2,1)} %x_ref.7), custom_call_target="tpu_custom_call" | custom-call | tf_op jit(solution)/shard_map/forward_rows/pallas_call | solution.py:42
  7.7 5.0 %collective-permute-start = (bf16[512,512]{1,0:T(8,128)(2,1)S(1)}, bf16[512,512]{1,0:T(8,128)(2,1)S(1)}, u32[]{:S(2)}, u32[]{:S(2)}) collective-permute-start(bf16[512,512]{1,0:T(8,128)(2,1)S(1)} %convert_element_type.91), channel_id=1, source_target_pairs={{0,1},{3,2},{4,5},{7,6},{8,9},{11,10},{12,13},{15,14},{16,17},{19,... | collective-permute-start | bytes 1572872 | tf_op jit(solution)/shard_map/ppermute | solution.py:235
  12.7 5.8 %forward_rows.9 = f32[512,512]{1,0:T(8,128)} custom-call(s32[1]{0:T(128)} %constant.10.clone.1.base_ref, s32[16,16]{1,0:T(8,128)} %idx_ref.21, s32[16]{0:T(128)} %bitcast.8, bf16[16,16,128,128]{3,2,1,0:T(8,128)(2,1)} %t_ref.21, bf16[2048,512]{1,0:T(8,128)(2,1)} %x_ref.7), custom_call_target="tpu_custom_call" | custom-call | tf_op jit(solution)/shard_map/forward_rows/pallas_call | solution.py:42
  18.5 2.2 convert_element_type.96
  22.0 3.0 collective-permute-done
  26.0 1.5 collective-permute-start.1
  27.4 5.8 %forward_rows.10 = f32[512,512]{1,0:T(8,128)} custom-call(s32[1]{0:T(128)} %constant.11.clone.1.base_ref, s32[16,16]{1,0:T(8,128)} %idx_ref.21, s32[16]{0:T(128)} %bitcast.9, bf16[16,16,128,128]{3,2,1,0:T(8,128)(2,1)} %t_ref.21, bf16[2048,512]{1,0:T(8,128)(2,1)} %x_ref.7), custom_call_target="tpu_custom_call" | custom-call | tf_op jit(solution)/shard_map/forward_rows/pallas_call | solution.py:42
  33.2 2.2 convert_element_type.101
  35.4 6.5 %collective-permute-start.6 = (bf16[512,512]{1,0:T(8,128)(2,1)}, bf16[512,512]{1,0:T(8,128)(2,1)S(1)}, u32[]{:S(2)}, u32[]{:S(2)}) collective-permute-start(bf16[512,512]{1,0:T(8,128)(2,1)} %convert_element_type.101), channel_id=1, source_target_pairs={{0,1},{3,2},{4,5},{7,6},{8,9},{11,10},{12,13},{15,14},{16,17},{19,... | collective-permute-start | bytes 1572872 | tf_op jit(solution)/shard_map/ppermute | solution.py:235
  42.8 1.5 collective-permute-start.4
  44.3 2.0 add_convert_fusion.5
  47.6 5.8 %forward_rows.11 = f32[512,512]{1,0:T(8,128)} custom-call(s32[1]{0:T(128)} %constant.12.clone.1.base_ref, s32[16,16]{1,0:T(8,128)} %idx_ref.21, s32[16]{0:T(128)} %bitcast.10, bf16[16,16,128,128]{3,2,1,0:T(8,128)(2,1)} %t_ref.21, bf16[2048,512]{1,0:T(8,128)(2,1)} %x_ref.7), custom_call_target="tpu_custom_call" | custom-call | tf_op jit(solution)/shard_map/forward_rows/pallas_call | solution.py:42
  54.8 5.5 %collective-permute-start.9 = (bf16[512,512]{1,0:T(8,128)(2,1)S(1)}, bf16[512,512]{1,0:T(8,128)(2,1)S(1)}, u32[]{:S(2)}, u32[]{:S(2)}) collective-permute-start(bf16[512,512]{1,0:T(8,128)(2,1)S(1)} %convert_element_type.106), channel_id=1, source_target_pairs={{0,1},{3,2},{4,5},{7,6},{8,9},{11,10},{12,13},{15,14},{16,17},{19,... | collective-permute-start | bytes 1572872 | tf_op jit(solution)/shard_map/ppermute | solution.py:235
  63.7 4.9 %collective-permute-done.9 = bf16[512,512]{1,0:T(8,128)(2,1)S(1)} collective-permute-done((bf16[512,512]{1,0:T(8,128)(2,1)S(1)}, bf16[512,512]{1,0:T(8,128)(2,1)S(1)}, u32[]{:S(2)}, u32[]{:S(2)}) %collective-permute-start.9) | collective-permute-done | bytes 524320 | tf_op jit(solution)/shard_map/ppermute | solution.py:235
  71.0 1.9 broadcast_select_fusion.5.refs_0_
  73.1 1.5 collective-permute-start.11
  74.6 3.3 collective-permute-done.5
  78.8 9.3 %backward_rows.3.refs_1_ = f32[2048,512]{1,0:T(8,128)} custom-call(s32[16,16]{1,0:T(8,128)} %idx_ref.21, s32[16]{0:T(128)} %bitcast.11, bf16[16,16,128,128]{3,2,1,0:T(8,128)(2,1)} %t_ref.21, bf16[512,512]{1,0:T(8,128)(2,1)} %broadcast_select_fusion.5.refs_0_, bf16[512,512]{1,0:T(8,128)(2,1)} %broadcast_select_fusion.4.refs_1_), custom_call_target="tpu_custom_call" | custom-call | tf_op jit(solution)/shard_map/backward_rows/pallas_call | solution.py:102
  89.2 8.1 %collective-permute-done.11 = bf16[512,512]{1,0:T(8,128)(2,1)S(1)} collective-permute-done((bf16[512,512]{1,0:T(8,128)(2,1)S(1)}, bf16[512,512]{1,0:T(8,128)(2,1)S(1)}, u32[]{:S(2)}, u32[]{:S(2)}) %collective-permute-start.11) | collective-permute-done | bytes 524320 | tf_op jit(solution)/shard_map/ppermute | solution.py:250
  97.4 1.8 fusion.6
  99.5 7.6 %backward_rows.4.refs_1_ = f32[2048,512]{1,0:T(8,128)} custom-call(s32[16,16]{1,0:T(8,128)} %idx_ref.21, s32[16]{0:T(128)} %bitcast.12, bf16[16,16,128,128]{3,2,1,0:T(8,128)(2,1)} %t_ref.21, bf16[512,512]{1,0:T(8,128)(2,1)} %copy-done.10, f32[2048,512]{1,0:T(8,128)} %backward_rows.3.refs_1_), custom_call_target="tpu_custom_call" | custom-call | tf_op jit(solution)/shard_map/backward_rows/pallas_call | solution.py:102
  107.2 2.1 collective-permute-start.13
  109.3 7.6 %backward_rows.5 = f32[2048,512]{1,0:T(8,128)} custom-call(s32[16,16]{1,0:T(8,128)} %idx_ref.21, s32[16]{0:T(128)} %bitcast.13, bf16[16,16,128,128]{3,2,1,0:T(8,128)(2,1)} %t_ref.21, bf16[512,512]{1,0:T(8,128)(2,1)} %copy-done.9, f32[2048,512]{1,0:T(8,128)} %backward_rows.4.refs_1_), custom_call_target="tpu_custom_call" | custom-call | tf_op jit(solution)/shard_map/backward_rows/pallas_call | solution.py:102
  117.0 1.8 constant_dynamic-slice_fusion.4
  119.0 5.1 %collective-permute-start.14 = (f32[64,512]{1,0:T(8,128)S(1)}, f32[64,512]{1,0:T(8,128)S(1)}, u32[]{:S(2)}, u32[]{:S(2)}) collective-permute-start(f32[64,512]{1,0:T(8,128)S(1)} %constant_dynamic-slice_fusion.5), channel_id=1, source_target_pairs={{0,16},{4,12},{8,24},{12,4},{16,0},{20,28},{24,8},{28,20},{1,17},{... | collective-permute-start | bytes 393224 | tf_op jit(solution)/shard_map/ppermute | solution.py:280
  124.1 2.9 collective-permute-done.14
  128.0 4.2 %collective-permute-done.15 = f32[64,512]{1,0:T(8,128)S(1)} collective-permute-done((f32[64,512]{1,0:T(8,128)S(1)}, f32[64,512]{1,0:T(8,128)S(1)}, u32[]{:S(2)}, u32[]{:S(2)}) %collective-permute-start.15) | collective-permute-done | bytes 131104 | tf_op jit(solution)/shard_map/ppermute | solution.py:258
  132.4 7.1 %collective-permute-done.16 = f32[64,512]{1,0:T(8,128)S(1)} collective-permute-done((f32[64,512]{1,0:T(8,128)S(1)}, f32[64,512]{1,0:T(8,128)S(1)}, u32[]{:S(2)}, u32[]{:S(2)}) %collective-permute-start.16) | collective-permute-done | bytes 131104 | tf_op jit(solution)/shard_map/ppermute | solution.py:258
  139.5 2.7 dynamic-slice_add_fusion
  142.2 2.7 collective-permute-start.18
  145.0 2.9 collective-permute-done.18
  148.6 1.6 collective-permute-start.21
  150.2 4.3 %collective-permute-done.19 = f32[128,512]{1,0:T(8,128)} collective-permute-done((f32[128,512]{1,0:T(8,128)S(1)}, f32[128,512]{1,0:T(8,128)}, u32[]{:S(2)}, u32[]{:S(2)}) %collective-permute-start.19) | collective-permute-done | bytes 262176 | tf_op jit(solution)/shard_map/ppermute | solution.py:287
  156.4 3.7 %collective-permute-done.21 = bf16[512,512]{1,0:T(8,128)(2,1)} collective-permute-done((bf16[512,512]{1,0:T(8,128)(2,1)S(1)}, bf16[512,512]{1,0:T(8,128)(2,1)}, u32[]{:S(2)}, u32[]{:S(2)}) %collective-permute-start.21) | collective-permute-done | bytes 524320 | tf_op jit(solution)/shard_map/ppermute | solution.py:280
  163.6 2.1 collective-permute-start.22
  165.7 27.4 %factorize.2 = (f32[512,512]{1,0:T(8,128)}, f32[512,512]{1,0:T(8,128)}) custom-call(f32[512,512]{1,0:T(8,128)} %pad_maximum_fusion.1.g_ref), custom_call_target="tpu_custom_call" | custom-call | tf_op jit(solution)/shard_map/factorize/pallas_call | solution.py:217
  193.1 2.3 convolution_convert_fusion
  195.5 8.0 %collective-permute-done.23 = bf16[256,512]{1,0:T(8,128)(2,1)S(1)} collective-permute-done((bf16[256,512]{1,0:T(8,128)(2,1)S(1)}, bf16[256,512]{1,0:T(8,128)(2,1)S(1)}, u32[]{:S(2)}, u32[]{:S(2)}) %collective-permute-start.23) | collective-permute-done | bytes 262176 | tf_op jit(solution)/shard_map/ppermute | solution.py:287
  203.7 9.0 %collective-permute-done.24 = bf16[512,512]{1,0:T(8,128)(2,1)S(1)} collective-permute-done((bf16[512,512]{1,0:T(8,128)(2,1)S(1)}, bf16[512,512]{1,0:T(8,128)(2,1)S(1)}, u32[]{:S(2)}, u32[]{:S(2)}) %collective-permute-start.24) | collective-permute-done | bytes 524320 | tf_op jit(solution)/shard_map/ppermute | solution.py:287
  213.2 2.6 collective-permute-done.25
  216.2 1.5 pad_maximum_fusion.x_ref
  217.6 5.8 %forward_rows.15 = f32[512,512]{1,0:T(8,128)} custom-call(s32[1]{0:T(128)} %bitcast.4.base_ref, s32[16,16]{1,0:T(8,128)} %idx_ref.21, s32[16]{0:T(128)} %bitcast.14, bf16[16,16,128,128]{3,2,1,0:T(8,128)(2,1)} %t_ref.21, bf16[2048,512]{1,0:T(8,128)(2,1)} %pad_maximum_fusion.x_ref), custom_call_target="tpu_custom_call" | custom-call | tf_op jit(solution)/shard_map/forward_rows/pallas_call | solution.py:42
  226.8 5.9 %forward_rows.13 = f32[512,512]{1,0:T(8,128)} custom-call(s32[1]{0:T(128)} %bitcast.2.base_ref, s32[16,16]{1,0:T(8,128)} %idx_ref.21, s32[16]{0:T(128)} %bitcast.15, bf16[16,16,128,128]{3,2,1,0:T(8,128)(2,1)} %t_ref.21, bf16[2048,512]{1,0:T(8,128)(2,1)} %pad_maximum_fusion.x_ref), custom_call_target="tpu_custom_call" | custom-call | tf_op jit(solution)/shard_map/forward_rows/pallas_call | solution.py:42
  232.7 5.1 %collective-permute-done.26 = bf16[512,512]{1,0:T(8,128)(2,1)S(1)} collective-permute-done((bf16[512,512]{1,0:T(8,128)(2,1)S(1)}, bf16[512,512]{1,0:T(8,128)(2,1)S(1)}, u32[]{:S(2)}, u32[]{:S(2)}) %collective-permute-start.26) | collective-permute-done | bytes 524320 | tf_op jit(solution)/shard_map/ppermute | solution.py:326
  237.8 1.6 add_convert_fusion
  239.4 4.4 %collective-permute-start.28 = (bf16[512,512]{1,0:T(8,128)(2,1)S(1)}, bf16[512,512]{1,0:T(8,128)(2,1)S(1)}, u32[]{:S(2)}, u32[]{:S(2)}) collective-permute-start(bf16[512,512]{1,0:T(8,128)(2,1)S(1)} %get-tuple-element.71), channel_id=1, source_target_pairs={{0,1},{1,2},{4,5},{5,6},{8,9},{9,10},{12,13},{13,14},{16,17},{17,1... | collective-permute-start | bytes 1572872 | tf_op jit(solution)/shard_map/ppermute | solution.py:326
  244.5 5.9 %forward_rows.14 = f32[512,512]{1,0:T(8,128)} custom-call(s32[1]{0:T(128)} %bitcast.3.base_ref, s32[16,16]{1,0:T(8,128)} %idx_ref.21, s32[16]{0:T(128)} %bitcast.16, bf16[16,16,128,128]{3,2,1,0:T(8,128)(2,1)} %t_ref.21, bf16[2048,512]{1,0:T(8,128)(2,1)} %pad_maximum_fusion.x_ref), custom_call_target="tpu_custom_call" | custom-call | tf_op jit(solution)/shard_map/forward_rows/pallas_call | solution.py:42
  250.4 4.2 %collective-permute-done.28 = bf16[512,512]{1,0:T(8,128)(2,1)S(1)} collective-permute-done((bf16[512,512]{1,0:T(8,128)(2,1)S(1)}, bf16[512,512]{1,0:T(8,128)(2,1)S(1)}, u32[]{:S(2)}, u32[]{:S(2)}) %collective-permute-start.28) | collective-permute-done | bytes 524320 | tf_op jit(solution)/shard_map/ppermute | solution.py:326
  254.6 2.9 convert_add_fusion
  257.5 6.9 %collective-permute-start.30 = (f32[512,512]{1,0:T(8,128)}, f32[512,512]{1,0:T(8,128)S(1)}, u32[]{:S(2)}, u32[]{:S(2)}) collective-permute-start(f32[512,512]{1,0:T(8,128)} %get-tuple-element.69), channel_id=1, source_target_pairs={{0,1},{1,2},{2,3},{4,5},{5,6},{6,7},{8,9},{9,10},{10,11},{12,13},{... | collective-permute-start | bytes 3145736 | tf_op jit(solution)/shard_map/ppermute | solution.py:326
  265.8 5.8 %forward_rows.12 = f32[512,512]{1,0:T(8,128)} custom-call(s32[1]{0:T(128)} %bitcast.base_ref, s32[16,16]{1,0:T(8,128)} %idx_ref.21, s32[16]{0:T(128)} %bitcast.17, bf16[16,16,128,128]{3,2,1,0:T(8,128)(2,1)} %t_ref.21, bf16[2048,512]{1,0:T(8,128)(2,1)} %pad_maximum_fusion.x_ref), custom_call_target="tpu_custom_call" | custom-call | tf_op jit(solution)/shard_map/forward_rows/pallas_call | solution.py:42
  271.5 13.9 %collective-permute-done.30 = f32[512,512]{1,0:T(8,128)S(1)} collective-permute-done((f32[512,512]{1,0:T(8,128)}, f32[512,512]{1,0:T(8,128)S(1)}, u32[]{:S(2)}, u32[]{:S(2)}) %collective-permute-start.30) | collective-permute-done | bytes 1048608 | tf_op jit(solution)/shard_map/ppermute | solution.py:326
  285.4 4.1 %collective-permute-done.31 = f32[512,512]{1,0:T(8,128)S(1)} collective-permute-done((f32[512,512]{1,0:T(8,128)}, f32[512,512]{1,0:T(8,128)S(1)}, u32[]{:S(2)}, u32[]{:S(2)}) %collective-permute-start.31) | collective-permute-done | bytes 1048608 | tf_op jit(solution)/shard_map/ppermute | solution.py:327
  289.5 3.6 fusion.14
  293.2 1.9 collective-permute-done.32
  295.4 6.2 %collective-permute-done.33 = f32[128,512]{1,0:T(8,128)S(1)} collective-permute-done((f32[128,512]{1,0:T(8,128)S(1)}, f32[128,512]{1,0:T(8,128)S(1)}, u32[]{:S(2)}, u32[]{:S(2)}) %collective-permute-start.33) | collective-permute-done | bytes 262176 | tf_op jit(solution)/shard_map/ppermute | solution.py:280
  302.1 4.6 %collective-permute-done.34 = f32[64,512]{1,0:T(8,128)S(1)} collective-permute-done((f32[64,512]{1,0:T(8,128)S(1)}, f32[64,512]{1,0:T(8,128)S(1)}, u32[]{:S(2)}, u32[]{:S(2)}) %collective-permute-start.34) | collective-permute-done | bytes 131104 | tf_op jit(solution)/shard_map/ppermute | solution.py:280
  307.1 4.7 %collective-permute-done.35 = f32[64,512]{1,0:T(8,128)S(1)} collective-permute-done((f32[64,512]{1,0:T(8,128)S(1)}, f32[64,512]{1,0:T(8,128)S(1)}, u32[]{:S(2)}, u32[]{:S(2)}) %collective-permute-start.35) | collective-permute-done | bytes 131104 | tf_op jit(solution)/shard_map/ppermute | solution.py:258
  311.9 7.2 %collective-permute-done.36 = f32[64,512]{1,0:T(8,128)S(1)} collective-permute-done((f32[64,512]{1,0:T(8,128)S(1)}, f32[64,512]{1,0:T(8,128)S(1)}, u32[]{:S(2)}, u32[]{:S(2)}) %collective-permute-start.36) | collective-permute-done | bytes 131104 | tf_op jit(solution)/shard_map/ppermute | solution.py:258
  319.2 6.3 %collective-permute-done.37 = f32[64,512]{1,0:T(8,128)S(1)} collective-permute-done((f32[64,512]{1,0:T(8,128)S(1)}, f32[64,512]{1,0:T(8,128)S(1)}, u32[]{:S(2)}, u32[]{:S(2)}) %collective-permute-start.37) | collective-permute-done | bytes 131104 | tf_op jit(solution)/shard_map/ppermute | solution.py:287
  326.0 6.1 %collective-permute-done.38 = f32[128,512]{1,0:T(8,128)S(1)} collective-permute-done((f32[128,512]{1,0:T(8,128)S(1)}, f32[128,512]{1,0:T(8,128)S(1)}, u32[]{:S(2)}, u32[]{:S(2)}) %collective-permute-start.38) | collective-permute-done | bytes 262176 | tf_op jit(solution)/shard_map/ppermute | solution.py:287
  332.2 1.9 collective-permute-done.39
  335.3 27.4 %factorize.3 = (f32[512,512]{1,0:T(8,128)}, f32[512,512]{1,0:T(8,128)}) custom-call(f32[512,512]{1,0:T(8,128)} %pad_maximum_fusion.3.g_ref), custom_call_target="tpu_custom_call" | custom-call | tf_op jit(solution)/shard_map/factorize/pallas_call | solution.py:217
  362.7 4.1 %fusion.13 = f32[512,512]{1,0:T(8,128)} fusion(f32[512,512]{1,0:T(8,128)} %get-tuple-element.66, f32[512,512]{1,0:T(8,128)S(1)} %collective-permute-done.31, f32[512,512]{1,0:T(8,128)S(1)} %copy-done.4, f32[512,512]{1,0:T(8,128)S(1)} %collective-permute-done.30), kind=kOutput, calls=%fused_computation.78 | convolution fusion | flops 1611137024 | bytes 5242880 | tf_op jit(solution)/shard_map/dot_general | solution.py:397
  (118 shorter events, 32.5 us)
Async XLA Ops:
  7.7 17.3 %collective-permute-start = (bf16[512,512]{1,0:T(8,128)(2,1)S(1)}, bf16[512,512]{1,0:T(8,128)(2,1)S(1)}, u32[]{:S(2)}, u32[]{:S(2)}) collective-permute-start(bf16[512,512]{1,0:T(8,128)(2,1)S(1)} %convert_element_type.91), channel_id=1, source_target_pairs={{0,1},{3,2},{4,5},{7,6},{8,9},{11,10},{12,13},{15,14},{16,17},{19,... | collective-permute-start | bytes 1572872 | tf_op jit(solution)/shard_map/ppermute | solution.py:235
  18.5 6.5 %copy-start.6 = (f32[512,512]{1,0:T(8,128)S(1)}, f32[512,512]{1,0:T(8,128)}, u32[]{:S(2)}) copy-start(f32[512,512]{1,0:T(8,128)} %forward_rows.8) | copy-start | bytes 3145732
  20.6 21.2 %collective-permute-start.3 = (bf16[512,512]{1,0:T(8,128)(2,1)}, bf16[512,512]{1,0:T(8,128)(2,1)S(1)}, u32[]{:S(2)}, u32[]{:S(2)}) collective-permute-start(bf16[512,512]{1,0:T(8,128)(2,1)} %convert_element_type.96), channel_id=1, source_target_pairs={{0,1},{3,2},{4,5},{7,6},{8,9},{11,10},{12,13},{15,14},{16,17},{19,... | collective-permute-start | bytes 1572872 | tf_op jit(solution)/shard_map/ppermute | solution.py:235
  26.0 18.3 %collective-permute-start.1 = (bf16[512,512]{1,0:T(8,128)(2,1)}, bf16[512,512]{1,0:T(8,128)(2,1)}, u32[]{:S(2)}, u32[]{:S(2)}) collective-permute-start(bf16[512,512]{1,0:T(8,128)(2,1)} %convert_element_type.93), channel_id=1, source_target_pairs={{1,2},{2,1},{5,6},{6,5},{9,10},{10,9},{13,14},{14,13},{17,18},{18,... | collective-permute-start | bytes 1572872 | tf_op jit(solution)/shard_map/ppermute | solution.py:242
  33.2 8.7 %copy-start = (f32[512,512]{1,0:T(8,128)S(1)}, f32[512,512]{1,0:T(8,128)}, u32[]{:S(2)}) copy-start(f32[512,512]{1,0:T(8,128)} %forward_rows.9) | copy-start | bytes 3145732
  35.4 24.9 %collective-permute-start.6 = (bf16[512,512]{1,0:T(8,128)(2,1)}, bf16[512,512]{1,0:T(8,128)(2,1)S(1)}, u32[]{:S(2)}, u32[]{:S(2)}) collective-permute-start(bf16[512,512]{1,0:T(8,128)(2,1)} %convert_element_type.101), channel_id=1, source_target_pairs={{0,1},{3,2},{4,5},{7,6},{8,9},{11,10},{12,13},{15,14},{16,17},{19,... | collective-permute-start | bytes 1572872 | tf_op jit(solution)/shard_map/ppermute | solution.py:235
  42.8 18.3 %collective-permute-start.4 = (bf16[512,512]{1,0:T(8,128)(2,1)}, bf16[512,512]{1,0:T(8,128)(2,1)}, u32[]{:S(2)}, u32[]{:S(2)}) collective-permute-start(bf16[512,512]{1,0:T(8,128)(2,1)} %fusion), channel_id=1, source_target_pairs={{1,2},{2,1},{5,6},{6,5},{9,10},{10,9},{13,14},{14,13},{17,18},{18,... | collective-permute-start | bytes 1572872 | tf_op jit(solution)/shard_map/ppermute | solution.py:242
  46.3 24.7 %collective-permute-start.2 = (bf16[512,512]{1,0:T(8,128)(2,1)}, bf16[512,512]{1,0:T(8,128)(2,1)}, u32[]{:S(2)}, u32[]{:S(2)}) collective-permute-start(bf16[512,512]{1,0:T(8,128)(2,1)} %add_convert_fusion.5), channel_id=1, source_target_pairs={{1,0},{2,3},{5,4},{6,7},{9,8},{10,11},{13,12},{14,15},{17,16},{18,... | collective-permute-start | bytes 1572872 | tf_op jit(solution)/shard_map/ppermute | solution.py:250
  53.4 6.9 %copy-start.1 = (f32[512,512]{1,0:T(8,128)S(1)}, f32[512,512]{1,0:T(8,128)}, u32[]{:S(2)}) copy-start(f32[512,512]{1,0:T(8,128)} %forward_rows.10) | copy-start | bytes 3145732
  54.7 13.8 %copy-start.2 = (f32[512,512]{1,0:T(8,128)S(1)}, f32[512,512]{1,0:T(8,128)}, u32[]{:S(2)}) copy-start(f32[512,512]{1,0:T(8,128)} %forward_rows.11) | copy-start | bytes 3145732
  54.8 13.8 %collective-permute-start.9 = (bf16[512,512]{1,0:T(8,128)(2,1)S(1)}, bf16[512,512]{1,0:T(8,128)(2,1)S(1)}, u32[]{:S(2)}, u32[]{:S(2)}) collective-permute-start(bf16[512,512]{1,0:T(8,128)(2,1)S(1)} %convert_element_type.106), channel_id=1, source_target_pairs={{0,1},{3,2},{4,5},{7,6},{8,9},{11,10},{12,13},{15,14},{16,17},{19,... | collective-permute-start | bytes 1572872 | tf_op jit(solution)/shard_map/ppermute | solution.py:235
  60.5 9.0 %collective-permute-start.7 = (bf16[512,512]{1,0:T(8,128)(2,1)S(1)}, bf16[512,512]{1,0:T(8,128)(2,1)S(1)}, u32[]{:S(2)}, u32[]{:S(2)}) collective-permute-start(bf16[512,512]{1,0:T(8,128)(2,1)S(1)} %fusion.1), channel_id=1, source_target_pairs={{1,2},{2,1},{5,6},{6,5},{9,10},{10,9},{13,14},{14,13},{17,18},{18,... | collective-permute-start | bytes 1572872 | tf_op jit(solution)/shard_map/ppermute | solution.py:242
  62.4 15.5 %collective-permute-start.5 = (bf16[512,512]{1,0:T(8,128)(2,1)S(1)}, bf16[512,512]{1,0:T(8,128)(2,1)S(1)}, u32[]{:S(2)}, u32[]{:S(2)}) collective-permute-start(bf16[512,512]{1,0:T(8,128)(2,1)S(1)} %add_convert_fusion.4), channel_id=1, source_target_pairs={{1,0},{2,3},{5,4},{6,7},{9,8},{10,11},{13,12},{14,15},{17,16},{18,... | collective-permute-start | bytes 1572872 | tf_op jit(solution)/shard_map/ppermute | solution.py:250
  68.7 4.2 %collective-permute-start.10 = (bf16[512,512]{1,0:T(8,128)(2,1)S(1)}, bf16[512,512]{1,0:T(8,128)(2,1)S(1)}, u32[]{:S(2)}, u32[]{:S(2)}) collective-permute-start(bf16[512,512]{1,0:T(8,128)(2,1)S(1)} %fusion.2), channel_id=1, source_target_pairs={{1,2},{2,1},{5,6},{6,5},{9,10},{10,9},{13,14},{14,13},{17,18},{18,... | collective-permute-start | bytes 1572872 | tf_op jit(solution)/shard_map/ppermute | solution.py:242
  69.7 19.5 %collective-permute-start.8 = (bf16[512,512]{1,0:T(8,128)(2,1)S(1)}, bf16[512,512]{1,0:T(8,128)(2,1)S(1)}, u32[]{:S(2)}, u32[]{:S(2)}) collective-permute-start(bf16[512,512]{1,0:T(8,128)(2,1)S(1)} %add_convert_fusion.3), channel_id=1, source_target_pairs={{1,0},{2,3},{5,4},{6,7},{9,8},{10,11},{13,12},{14,15},{17,16},{18,... | collective-permute-start | bytes 1572872 | tf_op jit(solution)/shard_map/ppermute | solution.py:250
  73.1 24.2 %collective-permute-start.11 = (bf16[512,512]{1,0:T(8,128)(2,1)S(1)}, bf16[512,512]{1,0:T(8,128)(2,1)S(1)}, u32[]{:S(2)}, u32[]{:S(2)}) collective-permute-start(bf16[512,512]{1,0:T(8,128)(2,1)S(1)} %add_convert_fusion.2), channel_id=1, source_target_pairs={{1,0},{2,3},{5,4},{6,7},{9,8},{10,11},{13,12},{14,15},{17,16},{18,... | collective-permute-start | bytes 1572872 | tf_op jit(solution)/shard_map/ppermute | solution.py:250
  88.1 9.3 %copy-start.11 = (bf16[512,512]{1,0:T(8,128)(2,1)S(1)}, bf16[512,512]{1,0:T(8,128)(2,1)}, u32[]{:S(2)}) copy-start(bf16[512,512]{1,0:T(8,128)(2,1)} %broadcast_select_fusion.5.refs_0_) | copy-start | bytes 1572868
  88.1 9.3 %copy-start.12 = (bf16[512,512]{1,0:T(8,128)(2,1)S(1)}, bf16[512,512]{1,0:T(8,128)(2,1)}, u32[]{:S(2)}) copy-start(bf16[512,512]{1,0:T(8,128)(2,1)} %broadcast_select_fusion.4.refs_1_) | copy-start | bytes 1572868
  89.2 10.1 %copy-start.10 = (bf16[512,512]{1,0:T(8,128)(2,1)}, bf16[512,512]{1,0:T(8,128)(2,1)S(1)}, u32[]{:S(2)}) copy-start(bf16[512,512]{1,0:T(8,128)(2,1)S(1)} %broadcast_select_fusion.3.refs_0_) | copy-start | bytes 1572868
  97.4 1.9 copy-start.9
  99.4 7.7 %collective-permute-start.12 = (f32[256,512]{1,0:T(8,128)S(1)}, f32[256,512]{1,0:T(8,128)S(1)}, u32[]{:S(2)}, u32[]{:S(2)}) collective-permute-start(f32[256,512]{1,0:T(8,128)S(1)} %constant_dynamic-slice_fusion.7), channel_id=1, source_target_pairs={{0,4},{4,0},{8,12},{12,8},{16,20},{20,16},{24,28},{28,24},{1,5},{5... | collective-permute-start | bytes 1572872 | tf_op jit(solution)/shard_map/ppermute | solution.py:280
  107.2 9.8 %collective-permute-start.13 = (f32[128,512]{1,0:T(8,128)S(1)}, f32[128,512]{1,0:T(8,128)S(1)}, u32[]{:S(2)}, u32[]{:S(2)}) collective-permute-start(f32[128,512]{1,0:T(8,128)S(1)} %constant_dynamic-slice_fusion.6), channel_id=1, source_target_pairs={{0,8},{4,20},{8,0},{12,28},{16,24},{20,4},{24,16},{28,12},{1,9},{5... | collective-permute-start | bytes 786440 | tf_op jit(solution)/shard_map/ppermute | solution.py:280
  118.8 20.7 %collective-permute-start.17 = (f32[1024,512]{1,0:T(8,128)S(1)}, f32[1024,512]{1,0:T(8,128)}, u32[]{:S(2)}, u32[]{:S(2)}) collective-permute-start(f32[1024,512]{1,0:T(8,128)S(1)} %constant_dynamic-slice_fusion.4), channel_id=1, source_target_pairs={{0,4},{4,0},{8,12},{12,8},{16,20},{20,16},{24,28},{28,24},{1,5},{5... | collective-permute-start | bytes 6291464 | tf_op jit(solution)/shard_map/ppermute | solution.py:280
  119.0 8.0 %collective-permute-start.14 = (f32[64,512]{1,0:T(8,128)S(1)}, f32[64,512]{1,0:T(8,128)S(1)}, u32[]{:S(2)}, u32[]{:S(2)}) collective-permute-start(f32[64,512]{1,0:T(8,128)S(1)} %constant_dynamic-slice_fusion.5), channel_id=1, source_target_pairs={{0,16},{4,12},{8,24},{12,4},{16,0},{20,28},{24,8},{28,20},{1,17},{... | collective-permute-start | bytes 393224 | tf_op jit(solution)/shard_map/ppermute | solution.py:280
  127.1 5.0 %collective-permute-start.15 = (f32[64,512]{1,0:T(8,128)S(1)}, f32[64,512]{1,0:T(8,128)S(1)}, u32[]{:S(2)}, u32[]{:S(2)}) collective-permute-start(f32[64,512]{1,0:T(8,128)S(1)} %dynamic-slice_add_fusion.6), channel_id=1, source_target_pairs={{0,1},{1,0},{2,3},{3,2},{4,5},{5,4},{6,7},{7,6},{8,9},{9,8},{10,11... | collective-permute-start | bytes 393224 | tf_op jit(solution)/shard_map/ppermute | solution.py:258
  132.1 7.3 %collective-permute-start.16 = (f32[64,512]{1,0:T(8,128)S(1)}, f32[64,512]{1,0:T(8,128)S(1)}, u32[]{:S(2)}, u32[]{:S(2)}) collective-permute-start(f32[64,512]{1,0:T(8,128)S(1)} %add.144), channel_id=1, source_target_pairs={{0,2},{1,3},{2,0},{3,1},{4,6},{5,7},{6,4},{7,5},{8,10},{9,11},{10,... | collective-permute-start | bytes 393224 | tf_op jit(solution)/shard_map/ppermute | solution.py:258
  142.2 5.7 %collective-permute-start.18 = (f32[64,512]{1,0:T(8,128)S(1)}, f32[64,512]{1,0:T(8,128)S(1)}, u32[]{:S(2)}, u32[]{:S(2)}) collective-permute-start(f32[64,512]{1,0:T(8,128)S(1)} %add.145), channel_id=1, source_target_pairs={{0,16},{4,12},{8,24},{12,4},{16,0},{20,28},{24,8},{28,20},{1,17},{... | collective-permute-start | bytes 393224 | tf_op jit(solution)/shard_map/ppermute | solution.py:287
  148.0 6.5 %collective-permute-start.19 = (f32[128,512]{1,0:T(8,128)S(1)}, f32[128,512]{1,0:T(8,128)}, u32[]{:S(2)}, u32[]{:S(2)}) collective-permute-start(f32[128,512]{1,0:T(8,128)S(1)} %pad_maximum_fusion.7), channel_id=1, source_target_pairs={{0,8},{4,20},{8,0},{12,28},{16,24},{20,4},{24,16},{28,12},{1,9},{5... | collective-permute-start | bytes 786440 | tf_op jit(solution)/shard_map/ppermute | solution.py:287
  148.6 11.5 %collective-permute-start.21 = (bf16[512,512]{1,0:T(8,128)(2,1)S(1)}, bf16[512,512]{1,0:T(8,128)(2,1)}, u32[]{:S(2)}, u32[]{:S(2)}) collective-permute-start(bf16[512,512]{1,0:T(8,128)(2,1)S(1)} %dynamic-slice_convert_fusion), channel_id=1, source_target_pairs={{0,8},{4,20},{8,0},{12,28},{16,24},{20,4},{24,16},{28,12},{1,9},{5... | collective-permute-start | bytes 1572872 | tf_op jit(solution)/shard_map/ppermute | solution.py:280
  155.5 0.9 copy-start.7
  156.4 5.0 %collective-permute-start.20 = (f32[256,512]{1,0:T(8,128)}, f32[256,512]{1,0:T(8,128)}, u32[]{:S(2)}, u32[]{:S(2)}) collective-permute-start(f32[256,512]{1,0:T(8,128)} %pad_maximum_fusion.4), channel_id=1, source_target_pairs={{0,4},{4,0},{8,12},{12,8},{16,20},{20,16},{24,28},{28,24},{1,5},{5... | collective-permute-start | bytes 1572872 | tf_op jit(solution)/shard_map/ppermute | solution.py:287
  160.1 1.3 copy-start.8
  163.6 29.5 %collective-permute-start.22 = (f32[256,512]{1,0:T(8,128)S(1)}, f32[256,512]{1,0:T(8,128)S(1)}, u32[]{:S(2)}, u32[]{:S(2)}) collective-permute-start(f32[256,512]{1,0:T(8,128)S(1)} %constant_dynamic-slice_fusion.3), channel_id=1, source_target_pairs={{0,16},{4,12},{8,24},{12,4},{16,0},{20,28},{24,8},{28,20},{1,17},{... | collective-permute-start | bytes 1572872 | tf_op jit(solution)/shard_map/ppermute | solution.py:280
  195.4 8.1 %collective-permute-start.23 = (bf16[256,512]{1,0:T(8,128)(2,1)S(1)}, bf16[256,512]{1,0:T(8,128)(2,1)S(1)}, u32[]{:S(2)}, u32[]{:S(2)}) collective-permute-start(bf16[256,512]{1,0:T(8,128)(2,1)S(1)} %convolution_convert_fusion), channel_id=1, source_target_pairs={{0,16},{4,12},{8,24},{12,4},{16,0},{20,28},{24,8},{28,20},{1,17},{... | collective-permute-start | bytes 786440 | tf_op jit(solution)/shard_map/ppermute | solution.py:287
  203.5 9.2 %collective-permute-start.24 = (bf16[512,512]{1,0:T(8,128)(2,1)S(1)}, bf16[512,512]{1,0:T(8,128)(2,1)S(1)}, u32[]{:S(2)}, u32[]{:S(2)}) collective-permute-start(bf16[512,512]{1,0:T(8,128)(2,1)S(1)} %pad_maximum_fusion.5), channel_id=1, source_target_pairs={{0,8},{4,20},{8,0},{12,28},{16,24},{20,4},{24,16},{28,12},{1,9},{5... | collective-permute-start | bytes 1572872 | tf_op jit(solution)/shard_map/ppermute | solution.py:287
  213.1 2.7 collective-permute-start.25
  224.7 13.1 %collective-permute-start.26 = (bf16[512,512]{1,0:T(8,128)(2,1)S(1)}, bf16[512,512]{1,0:T(8,128)(2,1)S(1)}, u32[]{:S(2)}, u32[]{:S(2)}) collective-permute-start(bf16[512,512]{1,0:T(8,128)(2,1)S(1)} %convert_element_type.114), channel_id=1, source_target_pairs={{0,1},{4,5},{8,9},{12,13},{16,17},{20,21},{24,25},{28,29}} | collective-permute-start | bytes 1572872 | tf_op jit(solution)/shard_map/ppermute | solution.py:326
  226.0 11.7 %collective-permute-start.27 = (bf16[512,512]{1,0:T(8,128)(2,1)S(1)}, bf16[512,512]{1,0:T(8,128)(2,1)S(1)}, u32[]{:S(2)}, u32[]{:S(2)}) collective-permute-start(bf16[512,512]{1,0:T(8,128)(2,1)S(1)} %convert_element_type.114), channel_id=1, source_target_pairs={{3,2},{7,6},{11,10},{15,14},{19,18},{23,22},{27,26},{31,30}} | collective-permute-start | bytes 1572872 | tf_op jit(solution)/shard_map/ppermute | solution.py:327
  226.8 11.0 %copy-start.3 = (f32[512,512]{1,0:T(8,128)S(1)}, f32[512,512]{1,0:T(8,128)}, u32[]{:S(2)}) copy-start(f32[512,512]{1,0:T(8,128)} %forward_rows.15) | copy-start | bytes 3145732
  239.4 15.3 %collective-permute-start.28 = (bf16[512,512]{1,0:T(8,128)(2,1)S(1)}, bf16[512,512]{1,0:T(8,128)(2,1)S(1)}, u32[]{:S(2)}, u32[]{:S(2)}) collective-permute-start(bf16[512,512]{1,0:T(8,128)(2,1)S(1)} %get-tuple-element.71), channel_id=1, source_target_pairs={{0,1},{1,2},{4,5},{5,6},{8,9},{9,10},{12,13},{13,14},{16,17},{17,1... | collective-permute-start | bytes 1572872 | tf_op jit(solution)/shard_map/ppermute | solution.py:326
  243.8 10.9 %collective-permute-start.29 = (bf16[512,512]{1,0:T(8,128)(2,1)S(1)}, bf16[512,512]{1,0:T(8,128)(2,1)S(1)}, u32[]{:S(2)}, u32[]{:S(2)}) collective-permute-start(bf16[512,512]{1,0:T(8,128)(2,1)S(1)} %get-tuple-element.70), channel_id=1, source_target_pairs={{3,2},{2,1},{7,6},{6,5},{11,10},{10,9},{15,14},{14,13},{19,18},{18... | collective-permute-start | bytes 1572872 | tf_op jit(solution)/shard_map/ppermute | solution.py:327
  244.5 10.1 %copy-start.5 = (f32[512,512]{1,0:T(8,128)S(1)}, f32[512,512]{1,0:T(8,128)}, u32[]{:S(2)}) copy-start(f32[512,512]{1,0:T(8,128)} %forward_rows.13) | copy-start | bytes 3145732
  257.5 27.9 %collective-permute-start.30 = (f32[512,512]{1,0:T(8,128)}, f32[512,512]{1,0:T(8,128)S(1)}, u32[]{:S(2)}, u32[]{:S(2)}) collective-permute-start(f32[512,512]{1,0:T(8,128)} %get-tuple-element.69), channel_id=1, source_target_pairs={{0,1},{1,2},{2,3},{4,5},{5,6},{6,7},{8,9},{9,10},{10,11},{12,13},{... | collective-permute-start | bytes 3145736 | tf_op jit(solution)/shard_map/ppermute | solution.py:326
  264.5 25.0 %collective-permute-start.31 = (f32[512,512]{1,0:T(8,128)}, f32[512,512]{1,0:T(8,128)S(1)}, u32[]{:S(2)}, u32[]{:S(2)}) collective-permute-start(f32[512,512]{1,0:T(8,128)} %get-tuple-element.68), channel_id=1, source_target_pairs={{3,2},{2,1},{1,0},{7,6},{6,5},{5,4},{11,10},{10,9},{9,8},{15,14},{... | collective-permute-start | bytes 3145736 | tf_op jit(solution)/shard_map/ppermute | solution.py:327
  293.1 2.0 collective-permute-start.32
  295.2 6.4 %collective-permute-start.33 = (f32[128,512]{1,0:T(8,128)S(1)}, f32[128,512]{1,0:T(8,128)S(1)}, u32[]{:S(2)}, u32[]{:S(2)}) collective-permute-start(f32[128,512]{1,0:T(8,128)S(1)} %constant_dynamic-slice_fusion.1), channel_id=1, source_target_pairs={{0,8},{4,20},{8,0},{12,28},{16,24},{20,4},{24,16},{28,12},{1,9},{5... | collective-permute-start | bytes 786440 | tf_op jit(solution)/shard_map/ppermute | solution.py:280
  301.7 5.0 %collective-permute-start.34 = (f32[64,512]{1,0:T(8,128)S(1)}, f32[64,512]{1,0:T(8,128)S(1)}, u32[]{:S(2)}, u32[]{:S(2)}) collective-permute-start(f32[64,512]{1,0:T(8,128)S(1)} %constant_dynamic-slice_fusion), channel_id=1, source_target_pairs={{0,16},{4,12},{8,24},{12,4},{16,0},{20,28},{24,8},{28,20},{1,17},{... | collective-permute-start | bytes 393224 | tf_op jit(solution)/shard_map/ppermute | solution.py:280
  306.8 5.0 %collective-permute-start.35 = (f32[64,512]{1,0:T(8,128)S(1)}, f32[64,512]{1,0:T(8,128)S(1)}, u32[]{:S(2)}, u32[]{:S(2)}) collective-permute-start(f32[64,512]{1,0:T(8,128)S(1)} %dynamic-slice_add_fusion.5), channel_id=1, source_target_pairs={{0,1},{1,0},{2,3},{3,2},{4,5},{5,4},{6,7},{7,6},{8,9},{9,8},{10,11... | collective-permute-start | bytes 393224 | tf_op jit(solution)/shard_map/ppermute | solution.py:258
  311.8 7.3 %collective-permute-start.36 = (f32[64,512]{1,0:T(8,128)S(1)}, f32[64,512]{1,0:T(8,128)S(1)}, u32[]{:S(2)}, u32[]{:S(2)}) collective-permute-start(f32[64,512]{1,0:T(8,128)S(1)} %add.164), channel_id=1, source_target_pairs={{0,2},{1,3},{2,0},{3,1},{4,6},{5,7},{6,4},{7,5},{8,10},{9,11},{10,... | collective-permute-start | bytes 393224 | tf_op jit(solution)/shard_map/ppermute | solution.py:258
  319.1 6.4 %collective-permute-start.37 = (f32[64,512]{1,0:T(8,128)S(1)}, f32[64,512]{1,0:T(8,128)S(1)}, u32[]{:S(2)}, u32[]{:S(2)}) collective-permute-start(f32[64,512]{1,0:T(8,128)S(1)} %add.165), channel_id=1, source_target_pairs={{0,16},{4,12},{8,24},{12,4},{16,0},{20,28},{24,8},{28,20},{1,17},{... | collective-permute-start | bytes 393224 | tf_op jit(solution)/shard_map/ppermute | solution.py:287
  325.6 6.4 %collective-permute-start.38 = (f32[128,512]{1,0:T(8,128)S(1)}, f32[128,512]{1,0:T(8,128)S(1)}, u32[]{:S(2)}, u32[]{:S(2)}) collective-permute-start(f32[128,512]{1,0:T(8,128)S(1)} %pad_maximum_fusion.8), channel_id=1, source_target_pairs={{0,8},{4,20},{8,0},{12,28},{16,24},{20,4},{24,16},{28,12},{1,9},{5... | collective-permute-start | bytes 786440 | tf_op jit(solution)/shard_map/ppermute | solution.py:287
  332.2 2.0 collective-permute-start.39
  334.2 28.4 %copy-start.4 = (f32[512,512]{1,0:T(8,128)S(1)}, f32[512,512]{1,0:T(8,128)}, u32[]{:S(2)}) copy-start(f32[512,512]{1,0:T(8,128)} %forward_rows.12) | copy-start | bytes 3145732

commit v4 on v3

--- a/solution.py
+++ b/solution.py
@@ -12,7 +12,7 @@
 TN = (((0,), (0,)), ((), ()))
 
 
-def forward_body(group, base_ref, idx_ref, cnt_ref, t_ref, x_ref, o_ref, acc_ref):
+def forward_body(group, base_ref, idx_ref, cnt_ref, t_ref, x_ref, o_ref, h_ref, acc_ref):
     tile = t_ref.shape[2]
     row = pl.program_id(0) + base_ref[0]
     count = cnt_ref[row]
@@ -33,6 +33,7 @@
 
     lax.fori_loop(0, (count + group - 1) // group, step, 0)
     o_ref[...] = acc_ref[...]
+    h_ref[...] = acc_ref[...].astype(h_ref.dtype)
 
 
 def forward(tiles, col_index, counts, x, base, rows):
@@ -41,15 +42,18 @@
     group = next(g for g in (8, 4, 2, 1) if slots % g == 0)
     return pl.pallas_call(
         functools.partial(forward_body, group),
-        out_shape=jax.ShapeDtypeStruct((rows * tile, width), jnp.float32),
+        out_shape=[
+            jax.ShapeDtypeStruct((rows * tile, width), jnp.float32),
+            jax.ShapeDtypeStruct((rows * tile, width), jnp.bfloat16),
+        ],
         grid_spec=pltpu.PrefetchScalarGridSpec(
             num_scalar_prefetch=3,
             grid=(rows,),
             in_specs=[
                 pl.BlockSpec((1, slots, tile, tile), lambda r, at, *_: (r + at[0], 0, 0, 0)),
-                pl.BlockSpec(x.shape, lambda r, *_: (0, 0)),
+                pl.BlockSpec(memory_space=pltpu.VMEM),
             ],
-            out_specs=pl.BlockSpec((tile, width), lambda r, *_: (r, 0)),
+            out_specs=[pl.BlockSpec((tile, width), lambda r, *_: (r, 0))] * 2,
             scratch_shapes=[pltpu.VMEM((tile, width), jnp.float32)],
         ),
         name="forward_rows",
@@ -93,7 +97,7 @@
     width = panels[0].shape[1]
     each = panels[0].shape[0] // tile
     group = next(g for g in (4, 2, 1) if slots % g == 0)
-    whole = pl.BlockSpec((col_rows, width), lambda r, *_: (0, 0), pipeline_mode=pl.Buffered(1))
+    whole = pl.BlockSpec(memory_space=pltpu.VMEM)
     more = () if total is None else (total,)
 
     def panel_map(k):
@@ -108,7 +112,7 @@
             in_specs=[pl.BlockSpec((1, slots, tile, tile), lambda r, *_: (r + base, 0, 0, 0))]
             + [pl.BlockSpec((tile, width), panel_map(k)) for k in range(len(panels))]
             + [whole] * len(more),
-            out_specs=pl.BlockSpec((col_rows, width), lambda r, *_: (0, 0)),
+            out_specs=whole,
         ),
         name="backward_rows",
     )(col_index, counts, tiles, *panels, *more)
@@ -226,13 +230,14 @@
     )(gram)
 
 
-def line_inward(value, wire):
-    n = lax.axis_size("col")
-    got = jnp.zeros_like(value).astype(wire)
+def line_inward(value, rounded):
+    n = lax.axis_size("col")
+    got = jnp.zeros_like(rounded)
     for s in range(n // 2 - 1):
         if s:
             value = value + got.astype(value.dtype)
-        got = lax.ppermute(value.astype(wire), "col", [(s, s + 1), (n - 1 - s, n - 2 - s)])
+            rounded = value.astype(rounded.dtype)
+        got = lax.ppermute(rounded, "col", [(s, s + 1), (n - 1 - s, n - 2 - s)])
     return value, got
 
 
@@ -305,7 +310,7 @@
     return jnp.where(k == n - 1, z, jnp.where(z < n // 2, low, high))
 
 
-def line_scatter(parts):
+def line_scatter(parts, rounded):
     n = lax.axis_size("col")
     z = lax.axis_index("col")
 
@@ -317,9 +322,11 @@
 
     right = left = None
     for t in range(1, n):
-        up = pick(t, jnp.where(z < n // 2, z, 0))
-        down = pick(t, jnp.where(z < n // 2, 0, n - 1 - z))
-        if right is not None:
+        if t == 1:
+            up = down = rounded
+        else:
+            up = pick(t, jnp.where(z < n // 2, z, 0))
+            down = pick(t, jnp.where(z < n // 2, 0, n - 1 - z))
             up = up + right.astype(up.dtype)
             down = down + left.astype(down.dtype)
         wire = jnp.float32 if t == n - 1 else jnp.bfloat16
@@ -337,6 +344,7 @@
     z = lax.axis_index("col")
 
     chunk = tile_rows // n_col
+    near = pltpu.with_memory_space_constraint(sketch, pltpu.VMEM)
     halves, crossed, sent = [], [], []
     for j in range(n_col):
         live = counts
@@ -344,14 +352,14 @@
             live, halves[0] = lax.optimization_barrier((counts, halves[0]))
         elif j > 2:
             live, crossed[j - 3] = lax.optimization_barrier((counts, crossed[j - 3]))
-        part = forward(tiles, col_index, live, sketch, j * chunk, chunk)
+        part, rounded = forward(tiles, col_index, live, near, j * chunk, chunk)
         if j >= 1:
             value, got = sent[j - 1]
             value, part = lax.optimization_barrier((value, part))
             halves.append(value + got.astype(value.dtype))
             if j >= 2:
                 crossed.append(line_across(halves[j - 2], jnp.bfloat16))
-        sent.append(line_inward(part, jnp.bfloat16))
+        sent.append(line_inward(part, rounded))
     value, got = sent[-1]
     halves.append(value + got.astype(value.dtype))
     for half in halves[len(crossed):]:
@@ -387,11 +395,12 @@
     unused, inverse = cholesky(gram, 1.0 / total_rows)
     part = lax.dot_general(part, inverse, NT, precision=HI, preferred_element_type=jnp.float32)
     back = row_gather(part.astype(jnp.bfloat16))
+    back = pltpu.with_memory_space_constraint(back, pltpu.VMEM)
 
     parts = [
         forward(tiles, col_index, counts, back, share_order(k) * chunk, chunk) for k in range(n_col)
     ]
-    second = line_scatter(parts)
+    second = line_scatter([part for part, _ in parts], parts[0][1])
     gram = lax.dot_general(second, second, TN, precision=HI, preferred_element_type=jnp.float32)
     factor, inverse = cholesky(gram_sum(gram), 1.0 / total_rows)
     basis = lax.dot_general(second, inverse, NT, precision=HI, preferred_element_type=jnp.float32)

time: 370 us -> 370 us (level)
  starting transfers between devices: 60.9 us -> 67.5 us
    convert_element_type x5 -> x0, other arithmetic: 8.31 us -> none  [the longest x4 7.02 us: line_inward(): value.astype(wire)]
where the time goes in v4:
time: 370 us; the launch traced here: 369 us
  waiting for transfers between devices  128 us (35%)
  Pallas kernels  125 us (34%)
  starting transfers between devices  67.5 us (18%)
  other arithmetic  30.4 us (8%)
  matrix products  12.7 us (3%)
    pallas_call x2, Pallas kernels, cholesky(): pl.pallas_call(functools.partial(chol_body, scale, group), out_shape=(s,...  54.7 us
    pallas_call x8, Pallas kernels, forward(): pl.pallas_call(functools.partial(forward_body, group), out_shape=[jax.Sha...  42.9 us
    ppermute x9, waiting for transfers between devices, row_gather(): got = lax.ppermute(part, 'row', pairs)  41.6 us
    pallas_call x3, Pallas kernels, backward(): pl.pallas_call(functools.partial(backward_body, group, base, len(panels))...  27.7 us
    ppermute x4, waiting for transfers between devices, col_sum(): lax.ppermute(value, 'col', [(i, i ^ 1 << bit) for i in range(n)])  21.8 us
    ppermute x3, waiting for transfers between devices, line_scatter(): right = lax.ppermute(up.astype(wire), 'col', [(i, i + 1) for i in range(t)])  21.5 us
    ppermute x4, starting transfers between devices, line_inward(): got = lax.ppermute(rounded, 'col', [(s, s + 1), (n - 1 - s, n - 2 - s)])  19.9 us
    ppermute x9, waiting for transfers between devices, row_step(): return keep + lax.ppermute(give, 'row', pairs).astype(value.dtype)  18.8 us
  transfers between devices with their start and end apart: 40, of which 26 were waited for; matrix products, arithmetic and copies ran while one was open for 5% of the time, Pallas kernels for 24%

profile of v4, /device:TPU:0, one launch (start us, length us, event | category | flops | bytes accessed | tf_op | source)
XLA Modules:
  0.0 368.9 jit_solution(10539849125039591730)
XLA Ops:
  0.6 1.6 copy-done
  2.2 5.1 %forward_rows.8 = (f32[512,512]{1,0:T(8,128)}, bf16[512,512]{1,0:T(8,128)(2,1)}) custom-call(s32[1]{0:T(128)} %constant.9.clone.1.base_ref, s32[16,16]{1,0:T(8,128)} %idx_ref.21, s32[16]{0:T(128)} %bitcast.7, bf16[16,16,128,128]{3,2,1,0:T(8,128)(2,1)} %t_ref.21, bf16[2048,512]{1,0:T(8,128)(2,1)S(1)} %copy-done), custom_call_target="tpu_custom_call" | custom-call | tf_op jit(solution)/shard_map/forward_rows/pallas_call | solution.py:43
  7.4 5.9 %collective-permute-start = (bf16[512,512]{1,0:T(8,128)(2,1)}, bf16[512,512]{1,0:T(8,128)(2,1)}, u32[]{:S(2)}, u32[]{:S(2)}) collective-permute-start(bf16[512,512]{1,0:T(8,128)(2,1)} %get-tuple-element.51), channel_id=1, source_target_pairs={{0,1},{3,2},{4,5},{7,6},{8,9},{11,10},{12,13},{15,14},{16,17},{19,... | collective-permute-start | bytes 1572872 | tf_op jit(solution)/shard_map/ppermute | solution.py:240
  13.3 5.1 %forward_rows.9 = (f32[512,512]{1,0:T(8,128)}, bf16[512,512]{1,0:T(8,128)(2,1)}) custom-call(s32[1]{0:T(128)} %constant.10.clone.1.base_ref, s32[16,16]{1,0:T(8,128)} %idx_ref.21, s32[16]{0:T(128)} %bitcast.8, bf16[16,16,128,128]{3,2,1,0:T(8,128)(2,1)} %t_ref.21, bf16[2048,512]{1,0:T(8,128)(2,1)S(1)} %copy-done), custom_call_target="tpu_custom_call" | custom-call | tf_op jit(solution)/shard_map/forward_rows/pallas_call | solution.py:43
  18.4 2.1 collective-permute-start.3
  20.5 4.6 %collective-permute-done = bf16[512,512]{1,0:T(8,128)(2,1)} collective-permute-done((bf16[512,512]{1,0:T(8,128)(2,1)}, bf16[512,512]{1,0:T(8,128)(2,1)}, u32[]{:S(2)}, u32[]{:S(2)}) %collective-permute-start) | collective-permute-done | bytes 524320 | tf_op jit(solution)/shard_map/ppermute | solution.py:240
  25.1 1.5 convert_add_fusion.6
  28.9 5.6 %forward_rows.10 = (f32[512,512]{1,0:T(8,128)}, bf16[512,512]{1,0:T(8,128)(2,1)}) custom-call(s32[1]{0:T(128)} %constant.11.clone.1.base_ref, s32[16,16]{1,0:T(8,128)} %idx_ref.21, s32[16]{0:T(128)} %bitcast.9, bf16[16,16,128,128]{3,2,1,0:T(8,128)(2,1)} %t_ref.21, bf16[2048,512]{1,0:T(8,128)(2,1)S(1)} %copy-done), custom_call_target="tpu_custom_call" | custom-call | tf_op jit(solution)/shard_map/forward_rows/pallas_call | solution.py:43
  34.5 6.8 %collective-permute-start.6 = (bf16[512,512]{1,0:T(8,128)(2,1)}, bf16[512,512]{1,0:T(8,128)(2,1)}, u32[]{:S(2)}, u32[]{:S(2)}) collective-permute-start(bf16[512,512]{1,0:T(8,128)(2,1)} %get-tuple-element.63), channel_id=1, source_target_pairs={{0,1},{3,2},{4,5},{7,6},{8,9},{11,10},{12,13},{15,14},{16,17},{19,... | collective-permute-start | bytes 1572872 | tf_op jit(solution)/shard_map/ppermute | solution.py:240
  41.3 2.3 fusion
  45.1 2.0 add_convert_fusion.5
  48.5 5.5 %forward_rows.11 = (f32[512,512]{1,0:T(8,128)}, bf16[512,512]{1,0:T(8,128)(2,1)}) custom-call(s32[1]{0:T(128)} %constant.12.clone.1.base_ref, s32[16,16]{1,0:T(8,128)} %idx_ref.21, s32[16]{0:T(128)} %bitcast.10, bf16[16,16,128,128]{3,2,1,0:T(8,128)(2,1)} %t_ref.21, bf16[2048,512]{1,0:T(8,128)(2,1)S(1)} %copy-done), custom_call_target="tpu_custom_call" | custom-call | tf_op jit(solution)/shard_map/forward_rows/pallas_call | solution.py:43
  53.9 5.2 %collective-permute-start.9 = (bf16[512,512]{1,0:T(8,128)(2,1)}, bf16[512,512]{1,0:T(8,128)(2,1)S(1)}, u32[]{:S(2)}, u32[]{:S(2)}) collective-permute-start(bf16[512,512]{1,0:T(8,128)(2,1)} %get-tuple-element.65), channel_id=1, source_target_pairs={{0,1},{3,2},{4,5},{7,6},{8,9},{11,10},{12,13},{15,14},{16,17},{19,... | collective-permute-start | bytes 1572872 | tf_op jit(solution)/shard_map/ppermute | solution.py:240
  63.8 3.7 %collective-permute-done.9 = bf16[512,512]{1,0:T(8,128)(2,1)S(1)} collective-permute-done((bf16[512,512]{1,0:T(8,128)(2,1)}, bf16[512,512]{1,0:T(8,128)(2,1)S(1)}, u32[]{:S(2)}, u32[]{:S(2)}) %collective-permute-start.9) | collective-permute-done | bytes 524320 | tf_op jit(solution)/shard_map/ppermute | solution.py:240
  70.9 1.9 broadcast_select_fusion.5.refs_0_
  73.1 1.5 collective-permute-start.11
  74.5 3.4 collective-permute-done.5
  78.8 9.9 %backward_rows.3.refs_1_ = f32[2048,512]{1,0:T(8,128)} custom-call(s32[16,16]{1,0:T(8,128)} %idx_ref.21, s32[16]{0:T(128)} %bitcast.11, bf16[16,16,128,128]{3,2,1,0:T(8,128)(2,1)} %t_ref.21, bf16[512,512]{1,0:T(8,128)(2,1)} %broadcast_select_fusion.5.refs_0_, bf16[512,512]{1,0:T(8,128)(2,1)} %broadcast_select_fusion.4.refs_1_), custom_call_target="tpu_custom_call" | custom-call | tf_op jit(solution)/shard_map/backward_rows/pallas_call | solution.py:106
  89.3 7.8 %collective-permute-done.11 = bf16[512,512]{1,0:T(8,128)(2,1)S(1)} collective-permute-done((bf16[512,512]{1,0:T(8,128)(2,1)S(1)}, bf16[512,512]{1,0:T(8,128)(2,1)S(1)}, u32[]{:S(2)}, u32[]{:S(2)}) %collective-permute-start.11) | collective-permute-done | bytes 524320 | tf_op jit(solution)/shard_map/ppermute | solution.py:255
  97.3 1.8 fusion.6
  99.3 8.9 %backward_rows.4.refs_1_ = f32[2048,512]{1,0:T(8,128)} custom-call(s32[16,16]{1,0:T(8,128)} %idx_ref.21, s32[16]{0:T(128)} %bitcast.12, bf16[16,16,128,128]{3,2,1,0:T(8,128)(2,1)} %t_ref.21, bf16[512,512]{1,0:T(8,128)(2,1)} %copy-done.9, f32[2048,512]{1,0:T(8,128)} %backward_rows.3.refs_1_), custom_call_target="tpu_custom_call" | custom-call | tf_op jit(solution)/shard_map/backward_rows/pallas_call | solution.py:106
  108.7 8.9 %backward_rows.5 = f32[2048,512]{1,0:T(8,128)} custom-call(s32[16,16]{1,0:T(8,128)} %idx_ref.21, s32[16]{0:T(128)} %bitcast.13, bf16[16,16,128,128]{3,2,1,0:T(8,128)(2,1)} %t_ref.21, bf16[512,512]{1,0:T(8,128)(2,1)} %copy-done.8, f32[2048,512]{1,0:T(8,128)} %backward_rows.4.refs_1_), custom_call_target="tpu_custom_call" | custom-call | tf_op jit(solution)/shard_map/backward_rows/pallas_call | solution.py:106
  117.6 1.8 constant_dynamic-slice_fusion.4
  119.5 5.4 %collective-permute-start.14 = (f32[64,512]{1,0:T(8,128)S(1)}, f32[64,512]{1,0:T(8,128)S(1)}, u32[]{:S(2)}, u32[]{:S(2)}) collective-permute-start(f32[64,512]{1,0:T(8,128)S(1)} %constant_dynamic-slice_fusion.5), channel_id=1, source_target_pairs={{0,16},{4,12},{8,24},{12,4},{16,0},{20,28},{24,8},{28,20},{1,17},{... | collective-permute-start | bytes 393224 | tf_op jit(solution)/shard_map/ppermute | solution.py:285
  124.8 2.9 collective-permute-done.14
  129.2 3.6 collective-permute-done.15
  133.9 6.3 %collective-permute-done.16 = f32[64,512]{1,0:T(8,128)S(1)} collective-permute-done((f32[64,512]{1,0:T(8,128)S(1)}, f32[64,512]{1,0:T(8,128)S(1)}, u32[]{:S(2)}, u32[]{:S(2)}) %collective-permute-start.16) | collective-permute-done | bytes 131104 | tf_op jit(solution)/shard_map/ppermute | solution.py:263
  140.2 2.7 dynamic-slice_add_fusion
  142.9 2.7 collective-permute-start.18
  145.7 2.9 collective-permute-done.18
  148.8 2.1 collective-permute-start.21
  150.9 4.3 %collective-permute-done.19 = f32[128,512]{1,0:T(8,128)} collective-permute-done((f32[128,512]{1,0:T(8,128)S(1)}, f32[128,512]{1,0:T(8,128)}, u32[]{:S(2)}, u32[]{:S(2)}) %collective-permute-start.19) | collective-permute-done | bytes 262176 | tf_op jit(solution)/shard_map/ppermute | solution.py:292
  157.1 3.7 %collective-permute-done.21 = bf16[512,512]{1,0:T(8,128)(2,1)} collective-permute-done((bf16[512,512]{1,0:T(8,128)(2,1)S(1)}, bf16[512,512]{1,0:T(8,128)(2,1)}, u32[]{:S(2)}, u32[]{:S(2)}) %collective-permute-start.21) | collective-permute-done | bytes 524320 | tf_op jit(solution)/shard_map/ppermute | solution.py:285
  164.3 2.1 collective-permute-start.22
  166.4 27.4 %factorize.2 = (f32[512,512]{1,0:T(8,128)}, f32[512,512]{1,0:T(8,128)}) custom-call(f32[512,512]{1,0:T(8,128)} %pad_maximum_fusion.1.g_ref), custom_call_target="tpu_custom_call" | custom-call | tf_op jit(solution)/shard_map/factorize/pallas_call | solution.py:221
  193.8 2.3 convolution_convert_fusion
  196.2 9.1 %collective-permute-done.23 = bf16[256,512]{1,0:T(8,128)(2,1)S(1)} collective-permute-done((bf16[256,512]{1,0:T(8,128)(2,1)S(1)}, bf16[256,512]{1,0:T(8,128)(2,1)S(1)}, u32[]{:S(2)}, u32[]{:S(2)}) %collective-permute-start.23) | collective-permute-done | bytes 262176 | tf_op jit(solution)/shard_map/ppermute | solution.py:292
  205.4 9.2 %collective-permute-done.24 = bf16[512,512]{1,0:T(8,128)(2,1)S(1)} collective-permute-done((bf16[512,512]{1,0:T(8,128)(2,1)S(1)}, bf16[512,512]{1,0:T(8,128)(2,1)S(1)}, u32[]{:S(2)}, u32[]{:S(2)}) %collective-permute-start.24) | collective-permute-done | bytes 524320 | tf_op jit(solution)/shard_map/ppermute | solution.py:292
  215.0 2.6 collective-permute-done.25
  218.1 5.5 %forward_rows.15 = (f32[512,512]{1,0:T(8,128)}, bf16[512,512]{1,0:T(8,128)(2,1)}) custom-call(s32[1]{0:T(128)} %bitcast.4.base_ref, s32[16,16]{1,0:T(8,128)} %idx_ref.21, s32[16]{0:T(128)} %bitcast.14, bf16[16,16,128,128]{3,2,1,0:T(8,128)(2,1)} %t_ref.21, bf16[2048,512]{1,0:T(8,128)(2,1)S(1)} %pad_maximum_fusion.x_ref), custom_call_target="tpu_custom_call" | custom-call | tf_op jit(solution)/shard_map/forward_rows/pallas_call | solution.py:43
  223.6 2.1 collective-permute-start.26
  225.7 1.5 collective-permute-start.27
  227.2 5.7 %forward_rows.13 = (f32[512,512]{1,0:T(8,128)}, bf16[512,512]{1,0:T(8,128)(2,1)}) custom-call(s32[1]{0:T(128)} %bitcast.2.base_ref, s32[16,16]{1,0:T(8,128)} %idx_ref.21, s32[16]{0:T(128)} %bitcast.15, bf16[16,16,128,128]{3,2,1,0:T(8,128)(2,1)} %t_ref.21, bf16[2048,512]{1,0:T(8,128)(2,1)S(1)} %pad_maximum_fusion.x_ref), custom_call_target="tpu_custom_call" | custom-call | tf_op jit(solution)/shard_map/forward_rows/pallas_call | solution.py:43
  232.9 3.8 %collective-permute-done.26 = bf16[512,512]{1,0:T(8,128)(2,1)} collective-permute-done((bf16[512,512]{1,0:T(8,128)(2,1)}, bf16[512,512]{1,0:T(8,128)(2,1)}, u32[]{:S(2)}, u32[]{:S(2)}) %collective-permute-start.26) | collective-permute-done | bytes 524320 | tf_op jit(solution)/shard_map/ppermute | solution.py:333
  236.7 2.9 add_convert_fusion
  239.6 5.2 %collective-permute-start.28 = (bf16[512,512]{1,0:T(8,128)(2,1)}, bf16[512,512]{1,0:T(8,128)(2,1)}, u32[]{:S(2)}, u32[]{:S(2)}) collective-permute-start(bf16[512,512]{1,0:T(8,128)(2,1)} %get-tuple-element.97), channel_id=1, source_target_pairs={{0,1},{1,2},{4,5},{5,6},{8,9},{9,10},{12,13},{13,14},{16,17},{17,1... | collective-permute-start | bytes 1572872 | tf_op jit(solution)/shard_map/ppermute | solution.py:333
  246.2 5.2 %forward_rows.14 = (f32[512,512]{1,0:T(8,128)}, bf16[512,512]{1,0:T(8,128)(2,1)}) custom-call(s32[1]{0:T(128)} %bitcast.3.base_ref, s32[16,16]{1,0:T(8,128)} %idx_ref.21, s32[16]{0:T(128)} %bitcast.16, bf16[16,16,128,128]{3,2,1,0:T(8,128)(2,1)} %t_ref.21, bf16[2048,512]{1,0:T(8,128)(2,1)S(1)} %pad_maximum_fusion.x_ref), custom_call_target="tpu_custom_call" | custom-call | tf_op jit(solution)/shard_map/forward_rows/pallas_call | solution.py:43
  251.5 3.4 collective-permute-done.28
  254.9 3.2 convert_add_fusion
  258.0 7.7 %collective-permute-start.30 = (f32[512,512]{1,0:T(8,128)}, f32[512,512]{1,0:T(8,128)S(1)}, u32[]{:S(2)}, u32[]{:S(2)}) collective-permute-start(f32[512,512]{1,0:T(8,128)} %get-tuple-element.95), channel_id=1, source_target_pairs={{0,1},{1,2},{2,3},{4,5},{5,6},{6,7},{8,9},{9,10},{10,11},{12,13},{... | collective-permute-start | bytes 3145736 | tf_op jit(solution)/shard_map/ppermute | solution.py:333
  267.0 5.2 %forward_rows.12 = (f32[512,512]{1,0:T(8,128)}, bf16[512,512]{1,0:T(8,128)(2,1)}) custom-call(s32[1]{0:T(128)} %bitcast.base_ref, s32[16,16]{1,0:T(8,128)} %idx_ref.21, s32[16]{0:T(128)} %bitcast.17, bf16[16,16,128,128]{3,2,1,0:T(8,128)(2,1)} %t_ref.21, bf16[2048,512]{1,0:T(8,128)(2,1)S(1)} %pad_maximum_fusion.x_ref), custom_call_target="tpu_custom_call" | custom-call | tf_op jit(solution)/shard_map/forward_rows/pallas_call | solution.py:43
  272.2 14.3 %collective-permute-done.30 = f32[512,512]{1,0:T(8,128)S(1)} collective-permute-done((f32[512,512]{1,0:T(8,128)}, f32[512,512]{1,0:T(8,128)S(1)}, u32[]{:S(2)}, u32[]{:S(2)}) %collective-permute-start.30) | collective-permute-done | bytes 1048608 | tf_op jit(solution)/shard_map/ppermute | solution.py:333
  286.5 4.2 %collective-permute-done.31 = f32[512,512]{1,0:T(8,128)} collective-permute-done((f32[512,512]{1,0:T(8,128)}, f32[512,512]{1,0:T(8,128)}, u32[]{:S(2)}, u32[]{:S(2)}) %collective-permute-start.31) | collective-permute-done | bytes 1048608 | tf_op jit(solution)/shard_map/ppermute | solution.py:334
  290.7 4.2 %fusion.14 = f32[512,512]{1,0:T(8,128)S(1)} fusion(f32[512,512]{1,0:T(8,128)} %collective-permute-done.31, f32[512,512]{1,0:T(8,128)} %get-tuple-element.81, f32[512,512]{1,0:T(8,128)S(1)} %collective-permute-done.30), kind=kOutput, calls=%fused_computation.79 | convolution fusion | flops 1611137024 | bytes 4194304 | tf_op jit(solution)/shard_map/dot_general | solution.py:404
  295.1 1.9 collective-permute-done.32
  298.3 5.2 %collective-permute-done.33 = f32[128,512]{1,0:T(8,128)S(1)} collective-permute-done((f32[128,512]{1,0:T(8,128)S(1)}, f32[128,512]{1,0:T(8,128)S(1)}, u32[]{:S(2)}, u32[]{:S(2)}) %collective-permute-start.33) | collective-permute-done | bytes 262176 | tf_op jit(solution)/shard_map/ppermute | solution.py:285
  303.7 5.0 %collective-permute-done.34 = f32[64,512]{1,0:T(8,128)S(1)} collective-permute-done((f32[64,512]{1,0:T(8,128)S(1)}, f32[64,512]{1,0:T(8,128)S(1)}, u32[]{:S(2)}, u32[]{:S(2)}) %collective-permute-start.34) | collective-permute-done | bytes 131104 | tf_op jit(solution)/shard_map/ppermute | solution.py:285
  308.9 4.7 %collective-permute-done.35 = f32[64,512]{1,0:T(8,128)S(1)} collective-permute-done((f32[64,512]{1,0:T(8,128)S(1)}, f32[64,512]{1,0:T(8,128)S(1)}, u32[]{:S(2)}, u32[]{:S(2)}) %collective-permute-start.35) | collective-permute-done | bytes 131104 | tf_op jit(solution)/shard_map/ppermute | solution.py:263
  313.8 7.2 %collective-permute-done.36 = f32[64,512]{1,0:T(8,128)S(1)} collective-permute-done((f32[64,512]{1,0:T(8,128)S(1)}, f32[64,512]{1,0:T(8,128)S(1)}, u32[]{:S(2)}, u32[]{:S(2)}) %collective-permute-start.36) | collective-permute-done | bytes 131104 | tf_op jit(solution)/shard_map/ppermute | solution.py:263
  321.1 6.4 %collective-permute-done.37 = f32[64,512]{1,0:T(8,128)S(1)} collective-permute-done((f32[64,512]{1,0:T(8,128)S(1)}, f32[64,512]{1,0:T(8,128)S(1)}, u32[]{:S(2)}, u32[]{:S(2)}) %collective-permute-start.37) | collective-permute-done | bytes 131104 | tf_op jit(solution)/shard_map/ppermute | solution.py:292
  328.7 5.2 %collective-permute-done.38 = f32[128,512]{1,0:T(8,128)S(1)} collective-permute-done((f32[128,512]{1,0:T(8,128)S(1)}, f32[128,512]{1,0:T(8,128)S(1)}, u32[]{:S(2)}, u32[]{:S(2)}) %collective-permute-start.38) | collective-permute-done | bytes 262176 | tf_op jit(solution)/shard_map/ppermute | solution.py:292
  334.1 1.9 collective-permute-done.39
  337.1 27.4 %factorize.3 = (f32[512,512]{1,0:T(8,128)}, f32[512,512]{1,0:T(8,128)}) custom-call(f32[512,512]{1,0:T(8,128)} %pad_maximum_fusion.3.g_ref), custom_call_target="tpu_custom_call" | custom-call | tf_op jit(solution)/shard_map/factorize/pallas_call | solution.py:221
  364.5 4.4 %fusion.13 = f32[512,512]{1,0:T(8,128)} fusion(f32[512,512]{1,0:T(8,128)} %get-tuple-element.92, f32[512,512]{1,0:T(8,128)} %collective-permute-done.31, f32[512,512]{1,0:T(8,128)S(1)} %copy-done.1, f32[512,512]{1,0:T(8,128)S(1)} %collective-permute-done.30), kind=kOutput, calls=%fused_computation.78 | convolution fusion | flops 1611137024 | bytes 5242880 | tf_op jit(solution)/shard_map/dot_general | solution.py:406
  (113 shorter events, 32.3 us)
Async XLA Ops:
  0.6 1.6 copy-start
  7.4 17.7 %collective-permute-start = (bf16[512,512]{1,0:T(8,128)(2,1)}, bf16[512,512]{1,0:T(8,128)(2,1)}, u32[]{:S(2)}, u32[]{:S(2)}) collective-permute-start(bf16[512,512]{1,0:T(8,128)(2,1)} %get-tuple-element.51), channel_id=1, source_target_pairs={{0,1},{3,2},{4,5},{7,6},{8,9},{11,10},{12,13},{15,14},{16,17},{19,... | collective-permute-start | bytes 1572872 | tf_op jit(solution)/shard_map/ppermute | solution.py:240
  18.4 22.9 %collective-permute-start.3 = (bf16[512,512]{1,0:T(8,128)(2,1)}, bf16[512,512]{1,0:T(8,128)(2,1)}, u32[]{:S(2)}, u32[]{:S(2)}) collective-permute-start(bf16[512,512]{1,0:T(8,128)(2,1)} %get-tuple-element.58), channel_id=1, source_target_pairs={{0,1},{3,2},{4,5},{7,6},{8,9},{11,10},{12,13},{15,14},{16,17},{19,... | collective-permute-start | bytes 1572872 | tf_op jit(solution)/shard_map/ppermute | solution.py:240
  27.5 17.6 %collective-permute-start.1 = (bf16[512,512]{1,0:T(8,128)(2,1)}, bf16[512,512]{1,0:T(8,128)(2,1)}, u32[]{:S(2)}, u32[]{:S(2)}) collective-permute-start(bf16[512,512]{1,0:T(8,128)(2,1)} %convert_element_type.76), channel_id=1, source_target_pairs={{1,2},{2,1},{5,6},{6,5},{9,10},{10,9},{13,14},{14,13},{17,18},{18,... | collective-permute-start | bytes 1572872 | tf_op jit(solution)/shard_map/ppermute | solution.py:247
  34.5 24.6 %collective-permute-start.6 = (bf16[512,512]{1,0:T(8,128)(2,1)}, bf16[512,512]{1,0:T(8,128)(2,1)}, u32[]{:S(2)}, u32[]{:S(2)}) collective-permute-start(bf16[512,512]{1,0:T(8,128)(2,1)} %get-tuple-element.63), channel_id=1, source_target_pairs={{0,1},{3,2},{4,5},{7,6},{8,9},{11,10},{12,13},{15,14},{16,17},{19,... | collective-permute-start | bytes 1572872 | tf_op jit(solution)/shard_map/ppermute | solution.py:240
  43.6 17.4 %collective-permute-start.4 = (bf16[512,512]{1,0:T(8,128)(2,1)}, bf16[512,512]{1,0:T(8,128)(2,1)}, u32[]{:S(2)}, u32[]{:S(2)}) collective-permute-start(bf16[512,512]{1,0:T(8,128)(2,1)} %fusion), channel_id=1, source_target_pairs={{1,2},{2,1},{5,6},{6,5},{9,10},{10,9},{13,14},{14,13},{17,18},{18,... | collective-permute-start | bytes 1572872 | tf_op jit(solution)/shard_map/ppermute | solution.py:247
  47.1 12.1 %copy-start.3 = (f32[512,512]{1,0:T(8,128)S(1)}, f32[512,512]{1,0:T(8,128)}, u32[]{:S(2)}) copy-start(f32[512,512]{1,0:T(8,128)} %get-tuple-element.62) | copy-start | bytes 3145732
  47.1 23.9 %collective-permute-start.2 = (bf16[512,512]{1,0:T(8,128)(2,1)}, bf16[512,512]{1,0:T(8,128)(2,1)}, u32[]{:S(2)}, u32[]{:S(2)}) collective-permute-start(bf16[512,512]{1,0:T(8,128)(2,1)} %add_convert_fusion.5), channel_id=1, source_target_pairs={{1,0},{2,3},{5,4},{6,7},{9,8},{10,11},{13,12},{14,15},{17,16},{18,... | collective-permute-start | bytes 1572872 | tf_op jit(solution)/shard_map/ppermute | solution.py:255
  53.9 7.1 %copy-start.2 = (f32[512,512]{1,0:T(8,128)S(1)}, f32[512,512]{1,0:T(8,128)}, u32[]{:S(2)}) copy-start(f32[512,512]{1,0:T(8,128)} %get-tuple-element.57) | copy-start | bytes 3145732
  53.9 13.5 %copy-start.5 = (f32[512,512]{1,0:T(8,128)S(1)}, f32[512,512]{1,0:T(8,128)}, u32[]{:S(2)}) copy-start(f32[512,512]{1,0:T(8,128)} %get-tuple-element.64) | copy-start | bytes 3145732
  53.9 13.5 %collective-permute-start.9 = (bf16[512,512]{1,0:T(8,128)(2,1)}, bf16[512,512]{1,0:T(8,128)(2,1)S(1)}, u32[]{:S(2)}, u32[]{:S(2)}) collective-permute-start(bf16[512,512]{1,0:T(8,128)(2,1)} %get-tuple-element.65), channel_id=1, source_target_pairs={{0,1},{3,2},{4,5},{7,6},{8,9},{11,10},{12,13},{15,14},{16,17},{19,... | collective-permute-start | bytes 1572872 | tf_op jit(solution)/shard_map/ppermute | solution.py:240
  60.3 8.0 %collective-permute-start.7 = (bf16[512,512]{1,0:T(8,128)(2,1)S(1)}, bf16[512,512]{1,0:T(8,128)(2,1)S(1)}, u32[]{:S(2)}, u32[]{:S(2)}) collective-permute-start(bf16[512,512]{1,0:T(8,128)(2,1)S(1)} %fusion.1), channel_id=1, source_target_pairs={{1,2},{2,1},{5,6},{6,5},{9,10},{10,9},{13,14},{14,13},{17,18},{18,... | collective-permute-start | bytes 1572872 | tf_op jit(solution)/shard_map/ppermute | solution.py:247
  62.5 15.4 %collective-permute-start.5 = (bf16[512,512]{1,0:T(8,128)(2,1)S(1)}, bf16[512,512]{1,0:T(8,128)(2,1)S(1)}, u32[]{:S(2)}, u32[]{:S(2)}) collective-permute-start(bf16[512,512]{1,0:T(8,128)(2,1)S(1)} %add_convert_fusion.4), channel_id=1, source_target_pairs={{1,0},{2,3},{5,4},{6,7},{9,8},{10,11},{13,12},{14,15},{17,16},{18,... | collective-permute-start | bytes 1572872 | tf_op jit(solution)/shard_map/ppermute | solution.py:255
  67.7 5.2 %collective-permute-start.10 = (bf16[512,512]{1,0:T(8,128)(2,1)S(1)}, bf16[512,512]{1,0:T(8,128)(2,1)S(1)}, u32[]{:S(2)}, u32[]{:S(2)}) collective-permute-start(bf16[512,512]{1,0:T(8,128)(2,1)S(1)} %fusion.2), channel_id=1, source_target_pairs={{1,2},{2,1},{5,6},{6,5},{9,10},{10,9},{13,14},{14,13},{17,18},{18,... | collective-permute-start | bytes 1572872 | tf_op jit(solution)/shard_map/ppermute | solution.py:247
  69.6 19.6 %collective-permute-start.8 = (bf16[512,512]{1,0:T(8,128)(2,1)S(1)}, bf16[512,512]{1,0:T(8,128)(2,1)S(1)}, u32[]{:S(2)}, u32[]{:S(2)}) collective-permute-start(bf16[512,512]{1,0:T(8,128)(2,1)S(1)} %add_convert_fusion.3), channel_id=1, source_target_pairs={{1,0},{2,3},{5,4},{6,7},{9,8},{10,11},{13,12},{14,15},{17,16},{18,... | collective-permute-start | bytes 1572872 | tf_op jit(solution)/shard_map/ppermute | solution.py:255
  73.1 24.1 %collective-permute-start.11 = (bf16[512,512]{1,0:T(8,128)(2,1)S(1)}, bf16[512,512]{1,0:T(8,128)(2,1)S(1)}, u32[]{:S(2)}, u32[]{:S(2)}) collective-permute-start(bf16[512,512]{1,0:T(8,128)(2,1)S(1)} %add_convert_fusion.2), channel_id=1, source_target_pairs={{1,0},{2,3},{5,4},{6,7},{9,8},{10,11},{13,12},{14,15},{17,16},{18,... | collective-permute-start | bytes 1572872 | tf_op jit(solution)/shard_map/ppermute | solution.py:255
  88.7 8.5 %copy-start.10 = (bf16[512,512]{1,0:T(8,128)(2,1)S(1)}, bf16[512,512]{1,0:T(8,128)(2,1)}, u32[]{:S(2)}) copy-start(bf16[512,512]{1,0:T(8,128)(2,1)} %broadcast_select_fusion.5.refs_0_) | copy-start | bytes 1572868
  88.7 8.5 %copy-start.11 = (bf16[512,512]{1,0:T(8,128)(2,1)S(1)}, bf16[512,512]{1,0:T(8,128)(2,1)}, u32[]{:S(2)}) copy-start(bf16[512,512]{1,0:T(8,128)(2,1)} %broadcast_select_fusion.4.refs_1_) | copy-start | bytes 1572868
  89.3 9.8 %copy-start.9 = (bf16[512,512]{1,0:T(8,128)(2,1)}, bf16[512,512]{1,0:T(8,128)(2,1)S(1)}, u32[]{:S(2)}) copy-start(bf16[512,512]{1,0:T(8,128)(2,1)S(1)} %broadcast_select_fusion.3.refs_0_) | copy-start | bytes 1572868
  97.2 1.9 copy-start.8
  99.2 8.9 %collective-permute-start.12 = (f32[256,512]{1,0:T(8,128)S(1)}, f32[256,512]{1,0:T(8,128)S(1)}, u32[]{:S(2)}, u32[]{:S(2)}) collective-permute-start(f32[256,512]{1,0:T(8,128)S(1)} %constant_dynamic-slice_fusion.7), channel_id=1, source_target_pairs={{0,4},{4,0},{8,12},{12,8},{16,20},{20,16},{24,28},{28,24},{1,5},{5... | collective-permute-start | bytes 1572872 | tf_op jit(solution)/shard_map/ppermute | solution.py:285
  108.2 9.3 %collective-permute-start.13 = (f32[128,512]{1,0:T(8,128)S(1)}, f32[128,512]{1,0:T(8,128)S(1)}, u32[]{:S(2)}, u32[]{:S(2)}) collective-permute-start(f32[128,512]{1,0:T(8,128)S(1)} %constant_dynamic-slice_fusion.6), channel_id=1, source_target_pairs={{0,8},{4,20},{8,0},{12,28},{16,24},{20,4},{24,16},{28,12},{1,9},{5... | collective-permute-start | bytes 786440 | tf_op jit(solution)/shard_map/ppermute | solution.py:285
  119.3 20.9 %collective-permute-start.17 = (f32[1024,512]{1,0:T(8,128)S(1)}, f32[1024,512]{1,0:T(8,128)}, u32[]{:S(2)}, u32[]{:S(2)}) collective-permute-start(f32[1024,512]{1,0:T(8,128)S(1)} %constant_dynamic-slice_fusion.4), channel_id=1, source_target_pairs={{0,4},{4,0},{8,12},{12,8},{16,20},{20,16},{24,28},{28,24},{1,5},{5... | collective-permute-start | bytes 6291464 | tf_op jit(solution)/shard_map/ppermute | solution.py:285
  119.5 8.3 %collective-permute-start.14 = (f32[64,512]{1,0:T(8,128)S(1)}, f32[64,512]{1,0:T(8,128)S(1)}, u32[]{:S(2)}, u32[]{:S(2)}) collective-permute-start(f32[64,512]{1,0:T(8,128)S(1)} %constant_dynamic-slice_fusion.5), channel_id=1, source_target_pairs={{0,16},{4,12},{8,24},{12,4},{16,0},{20,28},{24,8},{28,20},{1,17},{... | collective-permute-start | bytes 393224 | tf_op jit(solution)/shard_map/ppermute | solution.py:285
  127.8 5.0 %collective-permute-start.15 = (f32[64,512]{1,0:T(8,128)S(1)}, f32[64,512]{1,0:T(8,128)S(1)}, u32[]{:S(2)}, u32[]{:S(2)}) collective-permute-start(f32[64,512]{1,0:T(8,128)S(1)} %dynamic-slice_add_fusion.6), channel_id=1, source_target_pairs={{0,1},{1,0},{2,3},{3,2},{4,5},{5,4},{6,7},{7,6},{8,9},{9,8},{10,11... | collective-permute-start | bytes 393224 | tf_op jit(solution)/shard_map/ppermute | solution.py:263
  132.8 7.3 %collective-permute-start.16 = (f32[64,512]{1,0:T(8,128)S(1)}, f32[64,512]{1,0:T(8,128)S(1)}, u32[]{:S(2)}, u32[]{:S(2)}) collective-permute-start(f32[64,512]{1,0:T(8,128)S(1)} %add.144), channel_id=1, source_target_pairs={{0,2},{1,3},{2,0},{3,1},{4,6},{5,7},{6,4},{7,5},{8,10},{9,11},{10,... | collective-permute-start | bytes 393224 | tf_op jit(solution)/shard_map/ppermute | solution.py:263
  142.9 5.7 %collective-permute-start.18 = (f32[64,512]{1,0:T(8,128)S(1)}, f32[64,512]{1,0:T(8,128)S(1)}, u32[]{:S(2)}, u32[]{:S(2)}) collective-permute-start(f32[64,512]{1,0:T(8,128)S(1)} %add.145), channel_id=1, source_target_pairs={{0,16},{4,12},{8,24},{12,4},{16,0},{20,28},{24,8},{28,20},{1,17},{... | collective-permute-start | bytes 393224 | tf_op jit(solution)/shard_map/ppermute | solution.py:292
  148.7 6.5 %collective-permute-start.19 = (f32[128,512]{1,0:T(8,128)S(1)}, f32[128,512]{1,0:T(8,128)}, u32[]{:S(2)}, u32[]{:S(2)}) collective-permute-start(f32[128,512]{1,0:T(8,128)S(1)} %pad_maximum_fusion.7), channel_id=1, source_target_pairs={{0,8},{4,20},{8,0},{12,28},{16,24},{20,4},{24,16},{28,12},{1,9},{5... | collective-permute-start | bytes 786440 | tf_op jit(solution)/shard_map/ppermute | solution.py:292
  148.8 12.0 %collective-permute-start.21 = (bf16[512,512]{1,0:T(8,128)(2,1)S(1)}, bf16[512,512]{1,0:T(8,128)(2,1)}, u32[]{:S(2)}, u32[]{:S(2)}) collective-permute-start(bf16[512,512]{1,0:T(8,128)(2,1)S(1)} %dynamic-slice_convert_fusion), channel_id=1, source_target_pairs={{0,8},{4,20},{8,0},{12,28},{16,24},{20,4},{24,16},{28,12},{1,9},{5... | collective-permute-start | bytes 1572872 | tf_op jit(solution)/shard_map/ppermute | solution.py:285
  156.2 0.9 copy-start.6
  157.1 5.0 %collective-permute-start.20 = (f32[256,512]{1,0:T(8,128)}, f32[256,512]{1,0:T(8,128)}, u32[]{:S(2)}, u32[]{:S(2)}) collective-permute-start(f32[256,512]{1,0:T(8,128)} %pad_maximum_fusion.4), channel_id=1, source_target_pairs={{0,4},{4,0},{8,12},{12,8},{16,20},{20,16},{24,28},{28,24},{1,5},{5... | collective-permute-start | bytes 1572872 | tf_op jit(solution)/shard_map/ppermute | solution.py:292
  160.8 1.3 copy-start.7
  164.3 29.5 %collective-permute-start.22 = (f32[256,512]{1,0:T(8,128)S(1)}, f32[256,512]{1,0:T(8,128)S(1)}, u32[]{:S(2)}, u32[]{:S(2)}) collective-permute-start(f32[256,512]{1,0:T(8,128)S(1)} %constant_dynamic-slice_fusion.3), channel_id=1, source_target_pairs={{0,16},{4,12},{8,24},{12,4},{16,0},{20,28},{24,8},{28,20},{1,17},{... | collective-permute-start | bytes 1572872 | tf_op jit(solution)/shard_map/ppermute | solution.py:285
  196.1 9.2 %collective-permute-start.23 = (bf16[256,512]{1,0:T(8,128)(2,1)S(1)}, bf16[256,512]{1,0:T(8,128)(2,1)S(1)}, u32[]{:S(2)}, u32[]{:S(2)}) collective-permute-start(bf16[256,512]{1,0:T(8,128)(2,1)S(1)} %convolution_convert_fusion), channel_id=1, source_target_pairs={{0,16},{4,12},{8,24},{12,4},{16,0},{20,28},{24,8},{28,20},{1,17},{... | collective-permute-start | bytes 786440 | tf_op jit(solution)/shard_map/ppermute | solution.py:292
  205.4 9.2 %collective-permute-start.24 = (bf16[512,512]{1,0:T(8,128)(2,1)S(1)}, bf16[512,512]{1,0:T(8,128)(2,1)S(1)}, u32[]{:S(2)}, u32[]{:S(2)}) collective-permute-start(bf16[512,512]{1,0:T(8,128)(2,1)S(1)} %pad_maximum_fusion.5), channel_id=1, source_target_pairs={{0,8},{4,20},{8,0},{12,28},{16,24},{20,4},{24,16},{28,12},{1,9},{5... | collective-permute-start | bytes 1572872 | tf_op jit(solution)/shard_map/ppermute | solution.py:292
  214.9 2.7 collective-permute-start.25
  223.6 13.1 %collective-permute-start.26 = (bf16[512,512]{1,0:T(8,128)(2,1)}, bf16[512,512]{1,0:T(8,128)(2,1)}, u32[]{:S(2)}, u32[]{:S(2)}) collective-permute-start(bf16[512,512]{1,0:T(8,128)(2,1)} %get-tuple-element.85), channel_id=1, source_target_pairs={{0,1},{4,5},{8,9},{12,13},{16,17},{20,21},{24,25},{28,29}} | collective-permute-start | bytes 1572872 | tf_op jit(solution)/shard_map/ppermute | solution.py:333
  225.7 11.0 %collective-permute-start.27 = (bf16[512,512]{1,0:T(8,128)(2,1)}, bf16[512,512]{1,0:T(8,128)(2,1)}, u32[]{:S(2)}, u32[]{:S(2)}) collective-permute-start(bf16[512,512]{1,0:T(8,128)(2,1)} %get-tuple-element.85), channel_id=1, source_target_pairs={{3,2},{7,6},{11,10},{15,14},{19,18},{23,22},{27,26},{31,30}} | collective-permute-start | bytes 1572872 | tf_op jit(solution)/shard_map/ppermute | solution.py:334
  227.2 9.5 %copy-start.12 = (f32[512,512]{1,0:T(8,128)S(1)}, f32[512,512]{1,0:T(8,128)}, u32[]{:S(2)}) copy-start(f32[512,512]{1,0:T(8,128)} %get-tuple-element.84) | copy-start | bytes 3145732
  239.6 15.3 %collective-permute-start.28 = (bf16[512,512]{1,0:T(8,128)(2,1)}, bf16[512,512]{1,0:T(8,128)(2,1)}, u32[]{:S(2)}, u32[]{:S(2)}) collective-permute-start(bf16[512,512]{1,0:T(8,128)(2,1)} %get-tuple-element.97), channel_id=1, source_target_pairs={{0,1},{1,2},{4,5},{5,6},{8,9},{9,10},{12,13},{13,14},{16,17},{17,1... | collective-permute-start | bytes 1572872 | tf_op jit(solution)/shard_map/ppermute | solution.py:333
  244.7 10.1 %collective-permute-start.29 = (bf16[512,512]{1,0:T(8,128)(2,1)}, bf16[512,512]{1,0:T(8,128)(2,1)}, u32[]{:S(2)}, u32[]{:S(2)}) collective-permute-start(bf16[512,512]{1,0:T(8,128)(2,1)} %get-tuple-element.96), channel_id=1, source_target_pairs={{3,2},{2,1},{7,6},{6,5},{11,10},{10,9},{15,14},{14,13},{19,18},{18... | collective-permute-start | bytes 1572872 | tf_op jit(solution)/shard_map/ppermute | solution.py:334
  246.2 8.7 %copy-start.4 = (f32[512,512]{1,0:T(8,128)S(1)}, f32[512,512]{1,0:T(8,128)}, u32[]{:S(2)}) copy-start(f32[512,512]{1,0:T(8,128)} %get-tuple-element.82) | copy-start | bytes 3145732
  258.0 28.5 %collective-permute-start.30 = (f32[512,512]{1,0:T(8,128)}, f32[512,512]{1,0:T(8,128)S(1)}, u32[]{:S(2)}, u32[]{:S(2)}) collective-permute-start(f32[512,512]{1,0:T(8,128)} %get-tuple-element.95), channel_id=1, source_target_pairs={{0,1},{1,2},{2,3},{4,5},{5,6},{6,7},{8,9},{9,10},{10,11},{12,13},{... | collective-permute-start | bytes 3145736 | tf_op jit(solution)/shard_map/ppermute | solution.py:333
  265.7 25.0 %collective-permute-start.31 = (f32[512,512]{1,0:T(8,128)}, f32[512,512]{1,0:T(8,128)}, u32[]{:S(2)}, u32[]{:S(2)}) collective-permute-start(f32[512,512]{1,0:T(8,128)} %get-tuple-element.94), channel_id=1, source_target_pairs={{3,2},{2,1},{1,0},{7,6},{6,5},{5,4},{11,10},{10,9},{9,8},{15,14},{... | collective-permute-start | bytes 3145736 | tf_op jit(solution)/shard_map/ppermute | solution.py:334
  295.0 2.0 collective-permute-start.32
  297.1 6.4 %collective-permute-start.33 = (f32[128,512]{1,0:T(8,128)S(1)}, f32[128,512]{1,0:T(8,128)S(1)}, u32[]{:S(2)}, u32[]{:S(2)}) collective-permute-start(f32[128,512]{1,0:T(8,128)S(1)} %constant_dynamic-slice_fusion.1), channel_id=1, source_target_pairs={{0,8},{4,20},{8,0},{12,28},{16,24},{20,4},{24,16},{28,12},{1,9},{5... | collective-permute-start | bytes 786440 | tf_op jit(solution)/shard_map/ppermute | solution.py:285
  303.6 5.0 %collective-permute-start.34 = (f32[64,512]{1,0:T(8,128)S(1)}, f32[64,512]{1,0:T(8,128)S(1)}, u32[]{:S(2)}, u32[]{:S(2)}) collective-permute-start(f32[64,512]{1,0:T(8,128)S(1)} %constant_dynamic-slice_fusion), channel_id=1, source_target_pairs={{0,16},{4,12},{8,24},{12,4},{16,0},{20,28},{24,8},{28,20},{1,17},{... | collective-permute-start | bytes 393224 | tf_op jit(solution)/shard_map/ppermute | solution.py:285
  308.6 5.0 %collective-permute-start.35 = (f32[64,512]{1,0:T(8,128)S(1)}, f32[64,512]{1,0:T(8,128)S(1)}, u32[]{:S(2)}, u32[]{:S(2)}) collective-permute-start(f32[64,512]{1,0:T(8,128)S(1)} %dynamic-slice_add_fusion.5), channel_id=1, source_target_pairs={{0,1},{1,0},{2,3},{3,2},{4,5},{5,4},{6,7},{7,6},{8,9},{9,8},{10,11... | collective-permute-start | bytes 393224 | tf_op jit(solution)/shard_map/ppermute | solution.py:263
  313.7 7.3 %collective-permute-start.36 = (f32[64,512]{1,0:T(8,128)S(1)}, f32[64,512]{1,0:T(8,128)S(1)}, u32[]{:S(2)}, u32[]{:S(2)}) collective-permute-start(f32[64,512]{1,0:T(8,128)S(1)} %add.164), channel_id=1, source_target_pairs={{0,2},{1,3},{2,0},{3,1},{4,6},{5,7},{6,4},{7,5},{8,10},{9,11},{10,... | collective-permute-start | bytes 393224 | tf_op jit(solution)/shard_map/ppermute | solution.py:263
  321.0 6.4 %collective-permute-start.37 = (f32[64,512]{1,0:T(8,128)S(1)}, f32[64,512]{1,0:T(8,128)S(1)}, u32[]{:S(2)}, u32[]{:S(2)}) collective-permute-start(f32[64,512]{1,0:T(8,128)S(1)} %add.165), channel_id=1, source_target_pairs={{0,16},{4,12},{8,24},{12,4},{16,0},{20,28},{24,8},{28,20},{1,17},{... | collective-permute-start | bytes 393224 | tf_op jit(solution)/shard_map/ppermute | solution.py:292
  327.5 6.4 %collective-permute-start.38 = (f32[128,512]{1,0:T(8,128)S(1)}, f32[128,512]{1,0:T(8,128)S(1)}, u32[]{:S(2)}, u32[]{:S(2)}) collective-permute-start(f32[128,512]{1,0:T(8,128)S(1)} %pad_maximum_fusion.8), channel_id=1, source_target_pairs={{0,8},{4,20},{8,0},{12,28},{16,24},{20,4},{24,16},{28,12},{1,9},{5... | collective-permute-start | bytes 786440 | tf_op jit(solution)/shard_map/ppermute | solution.py:292
  334.0 2.0 collective-permute-start.39
  336.1 28.4 %copy-start.1 = (f32[512,512]{1,0:T(8,128)S(1)}, f32[512,512]{1,0:T(8,128)}, u32[]{:S(2)}) copy-start(f32[512,512]{1,0:T(8,128)} %get-tuple-element.81) | copy-start | bytes 3145732

commit v5 on v4

--- a/solution.py
+++ b/solution.py
@@ -12,10 +12,10 @@
 TN = (((0,), (0,)), ((), ()))
 
 
-def forward_body(group, base_ref, idx_ref, cnt_ref, t_ref, x_ref, o_ref, h_ref, acc_ref):
-    tile = t_ref.shape[2]
-    row = pl.program_id(0) + base_ref[0]
-    count = cnt_ref[row]
+def forward_body(group, base, meta_ref, t_ref, x_ref, o_ref, h_ref, acc_ref):
+    slots, tile = t_ref.shape[1], t_ref.shape[2]
+    row = pl.program_id(0) + (meta_ref[0, slots + 1] if base is None else base)
+    count = meta_ref[row, slots]
     acc_ref[...] = jnp.zeros_like(acc_ref)
 
     def step(p, carry):
@@ -24,7 +24,7 @@
             s = p * group + q
             t = t_ref[0, s]
             lhs.append(t if q == 0 else jnp.where(s < count, t, jnp.zeros_like(t)))
-            c = pl.multiple_of(idx_ref[row, s] * tile, tile)
+            c = pl.multiple_of(meta_ref[row, s] * tile, tile)
             rhs.append(x_ref[pl.ds(c, tile), :])
         acc_ref[...] += jnp.dot(
             jnp.concatenate(lhs, 1), jnp.concatenate(rhs, 0), preferred_element_type=jnp.float32
@@ -36,37 +36,41 @@
     h_ref[...] = acc_ref[...].astype(h_ref.dtype)
 
 
-def forward(tiles, col_index, counts, x, base, rows):
+def forward(tiles, meta, x, base, rows):
     slots, tile = tiles.shape[1], tiles.shape[2]
     width = x.shape[1]
     group = next(g for g in (8, 4, 2, 1) if slots % g == 0)
+
+    def tile_map(r, meta_ref):
+        return (r + (meta_ref[0, slots + 1] if base is None else base), 0, 0, 0)
+
     return pl.pallas_call(
-        functools.partial(forward_body, group),
+        functools.partial(forward_body, group, base),
         out_shape=[
             jax.ShapeDtypeStruct((rows * tile, width), jnp.float32),
             jax.ShapeDtypeStruct((rows * tile, width), jnp.bfloat16),
         ],
         grid_spec=pltpu.PrefetchScalarGridSpec(
-            num_scalar_prefetch=3,
+            num_scalar_prefetch=1,
             grid=(rows,),
             in_specs=[
-                pl.BlockSpec((1, slots, tile, tile), lambda r, at, *_: (r + at[0], 0, 0, 0)),
+                pl.BlockSpec((1, slots, tile, tile), tile_map),
                 pl.BlockSpec(memory_space=pltpu.VMEM),
             ],
             out_specs=[pl.BlockSpec((tile, width), lambda r, *_: (r, 0))] * 2,
             scratch_shapes=[pltpu.VMEM((tile, width), jnp.float32)],
         ),
         name="forward_rows",
-    )(jnp.full((1,), base, jnp.int32), col_index, counts, tiles, x)
-
-
-def backward_body(group, base, panels, idx_ref, cnt_ref, t_ref, *refs):
+    )(meta, tiles, x)
+
+
+def backward_body(group, base, panels, meta_ref, t_ref, *refs):
     z_ref = refs[-1]
-    tile = t_ref.shape[2]
+    slots, tile = t_ref.shape[1], t_ref.shape[2]
     at = pl.program_id(0)
     each = pl.num_programs(0) // panels
     row = at + base
-    count = cnt_ref[row]
+    count = meta_ref[row, slots]
     f = refs[0][...]
     for k in range(1, panels):
         f = jnp.where(at >= k * each, refs[k][...], f)
@@ -85,14 +89,14 @@
             jnp.concatenate(lhs, 1), f, TN, preferred_element_type=jnp.float32
         )
         for q in range(group):
-            c = pl.multiple_of(idx_ref[row, p * group + q] * tile, tile)
+            c = pl.multiple_of(meta_ref[row, p * group + q] * tile, tile)
             z_ref[pl.ds(c, tile), :] += out[q * tile:(q + 1) * tile]
         return carry
 
     lax.fori_loop(0, (count + group - 1) // group, step, 0)
 
 
-def backward(tiles, col_index, counts, panels, col_rows, base, total):
+def backward(tiles, meta, panels, col_rows, base, total):
     slots, tile = tiles.shape[1], tiles.shape[2]
     width = panels[0].shape[1]
     each = panels[0].shape[0] // tile
@@ -107,7 +111,7 @@
         functools.partial(backward_body, group, base, len(panels)),
         out_shape=jax.ShapeDtypeStruct((col_rows, width), jnp.float32),
         grid_spec=pltpu.PrefetchScalarGridSpec(
-            num_scalar_prefetch=2,
+            num_scalar_prefetch=1,
             grid=(each * len(panels),),
             in_specs=[pl.BlockSpec((1, slots, tile, tile), lambda r, *_: (r + base, 0, 0, 0))]
             + [pl.BlockSpec((tile, width), panel_map(k)) for k in range(len(panels))]
@@ -115,7 +119,7 @@
             out_specs=whole,
         ),
         name="backward_rows",
-    )(col_index, counts, tiles, *panels, *more)
+    )(meta, tiles, *panels, *more)
 
 
 def factor_block(read, r_ref, t_ref, group):
@@ -340,19 +344,24 @@
     tile_rows, slots, tile = tiles.shape[:3]
     n_col = lax.axis_size("col")
     total_rows = tile_rows * tile * lax.axis_size("row")
-    counts = counts.reshape(-1)
     z = lax.axis_index("col")
+
+    def table(base):
+        start = jnp.broadcast_to(base, (tile_rows, 1)).astype(jnp.int32)
+        return jnp.concatenate([col_index, counts.reshape(-1, 1), start], 1)
+
+    meta = table(0)
 
     chunk = tile_rows // n_col
     near = pltpu.with_memory_space_constraint(sketch, pltpu.VMEM)
     halves, crossed, sent = [], [], []
     for j in range(n_col):
-        live = counts
+        live = meta
         if j == 2:
-            live, halves[0] = lax.optimization_barrier((counts, halves[0]))
+            live, halves[0] = lax.optimization_barrier((meta, halves[0]))
         elif j > 2:
-            live, crossed[j - 3] = lax.optimization_barrier((counts, crossed[j - 3]))
-        part, rounded = forward(tiles, col_index, live, near, j * chunk, chunk)
+            live, crossed[j - 3] = lax.optimization_barrier((meta, crossed[j - 3]))
+        part, rounded = forward(tiles, live, near, j * chunk, chunk)
         if j >= 1:
             value, got = sent[j - 1]
             value, part = lax.optimization_barrier((value, part))
@@ -366,7 +375,7 @@
         crossed.append(line_across(half, jnp.bfloat16))
     sums = [line_outward(value) for value in crossed]
     middle = n_col // 2
-    back = backward(tiles, col_index, counts, sums[:middle], sketch.shape[0], 0, None)
+    back = backward(tiles, meta, sums[:middle], sketch.shape[0], 0, None)
     sums[-1], back = lax.optimization_barrier((sums[-1], back))
     first = jnp.concatenate(sums, 0)
 
@@ -376,8 +385,8 @@
     wires = (jnp.float32, jnp.bfloat16, jnp.float32)
     bits = lax.axis_size("row").bit_length() - 1
     for j in range(middle, n_col):
-        live, gram = lax.optimization_barrier((counts, gram))
-        back = backward(tiles, col_index, live, sums[j:j + 1], sketch.shape[0], j * chunk, back)
+        live, gram = lax.optimization_barrier((meta, gram))
+        back = backward(tiles, live, sums[j:j + 1], sketch.shape[0], j * chunk, back)
         if j - middle < bits:
             gram = row_step(gram, j - middle, jnp.float32)
         gram, back = lax.optimization_barrier((gram, back))
@@ -398,7 +407,7 @@
     back = pltpu.with_memory_space_constraint(back, pltpu.VMEM)
 
     parts = [
-        forward(tiles, col_index, counts, back, share_order(k) * chunk, chunk) for k in range(n_col)
+        forward(tiles, table(share_order(k) * chunk), back, None, chunk) for k in range(n_col)
     ]
     second = line_scatter([part for part, _ in parts], parts[0][1])
     gram = lax.dot_general(second, second, TN, precision=HI, preferred_element_type=jnp.float32)

time: 370 us -> 374 us (1.011)
  Pallas kernels: 125 us -> 134 us
  waiting for transfers between devices: 128 us -> 120 us
    ppermute x9, starting transfers between devices: 11.4 us -> 4.47 us  [row_step(): return keep + lax.ppermute(give, 'row', pairs).astype(value.dtype)]
    pallas_call x3, Pallas kernels: 27.7 us -> 33 us  [backward(): pl.pallas_call(functools.partial(backward_body, group, base, len(panels))...]
    ppermute x9, waiting for transfers between devices: 41.6 us -> 37.1 us  [row_gather(): got = lax.ppermute(part, 'row', pairs)]
  transfers between devices with their start and end apart: 40 -> 40, of which waited for: 26 -> 25; matrix products, arithmetic and copies ran while one was open for 5% -> 5% of each run, Pallas kernels for 24% -> 25%
where the time goes in v5:
time: 374 us; the launch traced here: 373 us
  Pallas kernels  134 us (36%)
  waiting for transfers between devices  120 us (32%)
  starting transfers between devices  68.3 us (18%)
  other arithmetic  32.4 us (9%)
  matrix products  12.7 us (3%)
  local copies, waits for them, and re-layouts  4.79 us (1%)
    pallas_call x2, Pallas kernels, cholesky(): pl.pallas_call(functools.partial(chol_body, scale, group), out_shape=(s,...  54.7 us
    pallas_call x8, Pallas kernels, forward(): pl.pallas_call(functools.partial(forward_body, group, base), out_shape=[j...  45.9 us
    ppermute x9, waiting for transfers between devices, row_gather(): got = lax.ppermute(part, 'row', pairs)  37.1 us
    pallas_call x3, Pallas kernels, backward(): pl.pallas_call(functools.partial(backward_body, group, base, len(panels))...  33 us
    ppermute x4, waiting for transfers between devices, col_sum(): lax.ppermute(value, 'col', [(i, i ^ 1 << bit) for i in range(n)])  21 us
    ppermute x3, waiting for transfers between devices, line_scatter(): right = lax.ppermute(up.astype(wire), 'col', [(i, i + 1) for i in range(t)])  20.6 us
    ppermute x9, waiting for transfers between devices, row_step(): return keep + lax.ppermute(give, 'row', pairs).astype(value.dtype)  20.6 us
    ppermute x4, starting transfers between devices, line_inward(): got = lax.ppermute(rounded, 'col', [(s, s + 1), (n - 1 - s, n - 2 - s)])  20.2 us
  transfers between devices with their start and end apart: 40, of which 25 were waited for; matrix products, arithmetic and copies ran while one was open for 5% of the time, Pallas kernels for 25%

profile of v5, /device:TPU:0, one launch (start us, length us, event | category | flops | bytes accessed | tf_op | source)
XLA Modules:
  0.0 372.8 jit_solution(15551372709565240524)
XLA Ops:
  3.8 1.6 copy-done
  5.3 5.9 %forward_rows.8 = (f32[512,512]{1,0:T(8,128)}, bf16[512,512]{1,0:T(8,128)(2,1)}) custom-call(s32[16,18]{1,0:T(8,128)} %get-tuple-element.72.meta_ref, bf16[16,16,128,128]{3,2,1,0:T(8,128)(2,1)} %t_ref.21, bf16[2048,512]{1,0:T(8,128)(2,1)S(1)} %copy-done), custom_call_target="tpu_custom_call" | custom-call | tf_op jit(solution)/shard_map/forward_rows/pallas_call | solution.py:47
  11.2 5.1 %collective-permute-start = (bf16[512,512]{1,0:T(8,128)(2,1)}, bf16[512,512]{1,0:T(8,128)(2,1)}, u32[]{:S(2)}, u32[]{:S(2)}) collective-permute-start(bf16[512,512]{1,0:T(8,128)(2,1)} %get-tuple-element.51), channel_id=1, source_target_pairs={{0,1},{3,2},{4,5},{7,6},{8,9},{11,10},{12,13},{15,14},{16,17},{19,... | collective-permute-start | bytes 1572872 | tf_op jit(solution)/shard_map/ppermute | solution.py:244
  16.3 5.4 %forward_rows.9 = (f32[512,512]{1,0:T(8,128)}, bf16[512,512]{1,0:T(8,128)(2,1)}) custom-call(s32[16,18]{1,0:T(8,128)} %get-tuple-element.72.meta_ref, bf16[16,16,128,128]{3,2,1,0:T(8,128)(2,1)} %t_ref.21, bf16[2048,512]{1,0:T(8,128)(2,1)S(1)} %copy-done), custom_call_target="tpu_custom_call" | custom-call | tf_op jit(solution)/shard_map/forward_rows/pallas_call | solution.py:47
  21.7 2.1 collective-permute-start.3
  23.8 4.3 %collective-permute-done = bf16[512,512]{1,0:T(8,128)(2,1)} collective-permute-done((bf16[512,512]{1,0:T(8,128)(2,1)}, bf16[512,512]{1,0:T(8,128)(2,1)}, u32[]{:S(2)}, u32[]{:S(2)}) %collective-permute-start) | collective-permute-done | bytes 524320 | tf_op jit(solution)/shard_map/ppermute | solution.py:244
  28.1 1.5 convert_add_fusion.6
  30.5 1.5 collective-permute-start.1
  32.0 5.6 %forward_rows.10 = (f32[512,512]{1,0:T(8,128)}, bf16[512,512]{1,0:T(8,128)(2,1)}) custom-call(s32[16,18]{1,0:T(8,128)} %get-tuple-element.72.meta_ref, bf16[16,16,128,128]{3,2,1,0:T(8,128)(2,1)} %t_ref.21, bf16[2048,512]{1,0:T(8,128)(2,1)S(1)} %copy-done), custom_call_target="tpu_custom_call" | custom-call | tf_op jit(solution)/shard_map/forward_rows/pallas_call | solution.py:47
  37.5 7.8 %collective-permute-start.6 = (bf16[512,512]{1,0:T(8,128)(2,1)}, bf16[512,512]{1,0:T(8,128)(2,1)}, u32[]{:S(2)}, u32[]{:S(2)}) collective-permute-start(bf16[512,512]{1,0:T(8,128)(2,1)} %get-tuple-element.63), channel_id=1, source_target_pairs={{0,1},{3,2},{4,5},{7,6},{8,9},{11,10},{12,13},{15,14},{16,17},{19,... | collective-permute-start | bytes 1572872 | tf_op jit(solution)/shard_map/ppermute | solution.py:244
  45.4 2.3 fusion
  47.7 1.5 collective-permute-start.4
  49.2 2.0 add_convert_fusion.5
  52.6 5.9 %forward_rows.11 = (f32[512,512]{1,0:T(8,128)}, bf16[512,512]{1,0:T(8,128)(2,1)}) custom-call(s32[16,18]{1,0:T(8,128)} %get-tuple-element.72.meta_ref, bf16[16,16,128,128]{3,2,1,0:T(8,128)(2,1)} %t_ref.21, bf16[2048,512]{1,0:T(8,128)(2,1)S(1)} %copy-done), custom_call_target="tpu_custom_call" | custom-call | tf_op jit(solution)/shard_map/forward_rows/pallas_call | solution.py:47
  58.6 5.2 %collective-permute-start.9 = (bf16[512,512]{1,0:T(8,128)(2,1)}, bf16[512,512]{1,0:T(8,128)(2,1)S(1)}, u32[]{:S(2)}, u32[]{:S(2)}) collective-permute-start(bf16[512,512]{1,0:T(8,128)(2,1)} %get-tuple-element.65), channel_id=1, source_target_pairs={{0,1},{3,2},{4,5},{7,6},{8,9},{11,10},{12,13},{15,14},{16,17},{19,... | collective-permute-start | bytes 1572872 | tf_op jit(solution)/shard_map/ppermute | solution.py:244
  68.4 3.1 collective-permute-done.9
  74.9 1.9 broadcast_select_fusion.5.refs_0_
  77.0 1.5 collective-permute-start.11
  80.3 12.8 %backward_rows.3.refs_1_ = f32[2048,512]{1,0:T(8,128)} custom-call(s32[16,18]{1,0:T(8,128)} %get-tuple-element.72.meta_ref, bf16[16,16,128,128]{3,2,1,0:T(8,128)(2,1)} %t_ref.21, bf16[512,512]{1,0:T(8,128)(2,1)} %broadcast_select_fusion.5.refs_0_, bf16[512,512]{1,0:T(8,128)(2,1)} %broadcast_select_fusion.4.refs_1_), custom_call_target="tpu_custom_call" | custom-call | tf_op jit(solution)/shard_map/backward_rows/pallas_call | solution.py:110
  93.1 8.0 %collective-permute-done.11 = bf16[512,512]{1,0:T(8,128)(2,1)S(1)} collective-permute-done((bf16[512,512]{1,0:T(8,128)(2,1)S(1)}, bf16[512,512]{1,0:T(8,128)(2,1)S(1)}, u32[]{:S(2)}, u32[]{:S(2)}) %collective-permute-start.11) | collective-permute-done | bytes 524320 | tf_op jit(solution)/shard_map/ppermute | solution.py:259
  101.2 1.8 fusion.6
  103.2 9.5 %backward_rows.4.refs_1_ = f32[2048,512]{1,0:T(8,128)} custom-call(s32[16,18]{1,0:T(8,128)} %get-tuple-element.72.meta_ref, bf16[16,16,128,128]{3,2,1,0:T(8,128)(2,1)} %t_ref.21, bf16[512,512]{1,0:T(8,128)(2,1)} %copy-done.9, f32[2048,512]{1,0:T(8,128)} %backward_rows.3.refs_1_), custom_call_target="tpu_custom_call" | custom-call | tf_op jit(solution)/shard_map/backward_rows/pallas_call | solution.py:110
  112.9 10.8 %backward_rows.5 = f32[2048,512]{1,0:T(8,128)} custom-call(s32[16,18]{1,0:T(8,128)} %get-tuple-element.72.meta_ref, bf16[16,16,128,128]{3,2,1,0:T(8,128)(2,1)} %t_ref.21, bf16[512,512]{1,0:T(8,128)(2,1)} %copy-done.8, f32[2048,512]{1,0:T(8,128)} %backward_rows.4.refs_1_), custom_call_target="tpu_custom_call" | custom-call | tf_op jit(solution)/shard_map/backward_rows/pallas_call | solution.py:110
  123.7 1.8 constant_dynamic-slice_fusion.4
  125.7 5.0 %collective-permute-done.14 = f32[64,512]{1,0:T(8,128)S(1)} collective-permute-done((f32[64,512]{1,0:T(8,128)S(1)}, f32[64,512]{1,0:T(8,128)S(1)}, u32[]{:S(2)}, u32[]{:S(2)}) %collective-permute-start.14) | collective-permute-done | bytes 131104 | tf_op jit(solution)/shard_map/ppermute | solution.py:289
  132.0 3.7 collective-permute-done.15
  135.7 2.6 collective-permute-start.16
  138.4 5.3 %collective-permute-done.16 = f32[64,512]{1,0:T(8,128)S(1)} collective-permute-done((f32[64,512]{1,0:T(8,128)S(1)}, f32[64,512]{1,0:T(8,128)S(1)}, u32[]{:S(2)}, u32[]{:S(2)}) %collective-permute-start.16) | collective-permute-done | bytes 131104 | tf_op jit(solution)/shard_map/ppermute | solution.py:267
  143.7 2.7 dynamic-slice_add_fusion
  147.4 4.1 %collective-permute-done.18 = f32[64,512]{1,0:T(8,128)S(1)} collective-permute-done((f32[64,512]{1,0:T(8,128)S(1)}, f32[64,512]{1,0:T(8,128)S(1)}, u32[]{:S(2)}, u32[]{:S(2)}) %collective-permute-start.18) | collective-permute-done | bytes 131104 | tf_op jit(solution)/shard_map/ppermute | solution.py:296
  152.1 1.7 collective-permute-start.21
  153.7 4.3 %collective-permute-done.19 = f32[128,512]{1,0:T(8,128)} collective-permute-done((f32[128,512]{1,0:T(8,128)S(1)}, f32[128,512]{1,0:T(8,128)}, u32[]{:S(2)}, u32[]{:S(2)}) %collective-permute-start.19) | collective-permute-done | bytes 262176 | tf_op jit(solution)/shard_map/ppermute | solution.py:296
  159.9 3.7 %collective-permute-done.21 = bf16[512,512]{1,0:T(8,128)(2,1)} collective-permute-done((bf16[512,512]{1,0:T(8,128)(2,1)S(1)}, bf16[512,512]{1,0:T(8,128)(2,1)}, u32[]{:S(2)}, u32[]{:S(2)}) %collective-permute-start.21) | collective-permute-done | bytes 524320 | tf_op jit(solution)/shard_map/ppermute | solution.py:289
  168.1 27.4 %factorize.2 = (f32[512,512]{1,0:T(8,128)}, f32[512,512]{1,0:T(8,128)}) custom-call(f32[512,512]{1,0:T(8,128)} %pad_maximum_fusion.1.g_ref), custom_call_target="tpu_custom_call" | custom-call | tf_op jit(solution)/shard_map/factorize/pallas_call | solution.py:225
  195.5 2.3 convolution_convert_fusion
  199.0 5.6 %collective-permute-done.23 = bf16[256,512]{1,0:T(8,128)(2,1)S(1)} collective-permute-done((bf16[256,512]{1,0:T(8,128)(2,1)S(1)}, bf16[256,512]{1,0:T(8,128)(2,1)S(1)}, u32[]{:S(2)}, u32[]{:S(2)}) %collective-permute-start.23) | collective-permute-done | bytes 262176 | tf_op jit(solution)/shard_map/ppermute | solution.py:296
  204.7 2.9 collective-permute-start.24
  207.5 7.2 %collective-permute-done.24 = bf16[512,512]{1,0:T(8,128)(2,1)S(1)} collective-permute-done((bf16[512,512]{1,0:T(8,128)(2,1)S(1)}, bf16[512,512]{1,0:T(8,128)(2,1)S(1)}, u32[]{:S(2)}, u32[]{:S(2)}) %collective-permute-start.24) | collective-permute-done | bytes 524320 | tf_op jit(solution)/shard_map/ppermute | solution.py:296
  215.1 2.6 collective-permute-done.25
  218.2 5.9 %forward_rows.15 = (f32[512,512]{1,0:T(8,128)}, bf16[512,512]{1,0:T(8,128)(2,1)}) custom-call(s32[16,18]{1,0:T(8,128)} %get-tuple-element.121.meta_ref, bf16[16,16,128,128]{3,2,1,0:T(8,128)(2,1)} %t_ref.21, bf16[2048,512]{1,0:T(8,128)(2,1)S(1)} %pad_maximum_fusion.x_ref), custom_call_target="tpu_custom_call" | custom-call | tf_op jit(solution)/shard_map/forward_rows/pallas_call | solution.py:47
  224.1 2.3 collective-permute-start.26
  226.4 1.5 collective-permute-start.27
  227.9 5.7 %forward_rows.13 = (f32[512,512]{1,0:T(8,128)}, bf16[512,512]{1,0:T(8,128)(2,1)}) custom-call(s32[16,18]{1,0:T(8,128)} %get-tuple-element.119.meta_ref, bf16[16,16,128,128]{3,2,1,0:T(8,128)(2,1)} %t_ref.21, bf16[2048,512]{1,0:T(8,128)(2,1)S(1)} %pad_maximum_fusion.x_ref), custom_call_target="tpu_custom_call" | custom-call | tf_op jit(solution)/shard_map/forward_rows/pallas_call | solution.py:47
  233.6 4.0 %collective-permute-done.26 = bf16[512,512]{1,0:T(8,128)(2,1)} collective-permute-done((bf16[512,512]{1,0:T(8,128)(2,1)}, bf16[512,512]{1,0:T(8,128)(2,1)}, u32[]{:S(2)}, u32[]{:S(2)}) %collective-permute-start.26) | collective-permute-done | bytes 524320 | tf_op jit(solution)/shard_map/ppermute | solution.py:337
  237.5 2.9 add_convert_fusion
  240.4 5.2 %collective-permute-start.28 = (bf16[512,512]{1,0:T(8,128)(2,1)}, bf16[512,512]{1,0:T(8,128)(2,1)}, u32[]{:S(2)}, u32[]{:S(2)}) collective-permute-start(bf16[512,512]{1,0:T(8,128)(2,1)} %get-tuple-element.99), channel_id=1, source_target_pairs={{0,1},{1,2},{4,5},{5,6},{8,9},{9,10},{12,13},{13,14},{16,17},{17,1... | collective-permute-start | bytes 1572872 | tf_op jit(solution)/shard_map/ppermute | solution.py:337
  247.1 5.6 %forward_rows.14 = (f32[512,512]{1,0:T(8,128)}, bf16[512,512]{1,0:T(8,128)(2,1)}) custom-call(s32[16,18]{1,0:T(8,128)} %get-tuple-element.118.meta_ref, bf16[16,16,128,128]{3,2,1,0:T(8,128)(2,1)} %t_ref.21, bf16[2048,512]{1,0:T(8,128)(2,1)S(1)} %pad_maximum_fusion.x_ref), custom_call_target="tpu_custom_call" | custom-call | tf_op jit(solution)/shard_map/forward_rows/pallas_call | solution.py:47
  252.6 3.3 collective-permute-done.28
  255.9 3.2 convert_add_fusion
  259.0 10.7 %collective-permute-start.30 = (f32[512,512]{1,0:T(8,128)}, f32[512,512]{1,0:T(8,128)S(1)}, u32[]{:S(2)}, u32[]{:S(2)}) collective-permute-start(f32[512,512]{1,0:T(8,128)} %get-tuple-element.97), channel_id=1, source_target_pairs={{0,1},{1,2},{2,3},{4,5},{5,6},{6,7},{8,9},{9,10},{10,11},{12,13},{... | collective-permute-start | bytes 3145736 | tf_op jit(solution)/shard_map/ppermute | solution.py:337
  271.1 5.9 %forward_rows.12 = (f32[512,512]{1,0:T(8,128)}, bf16[512,512]{1,0:T(8,128)(2,1)}) custom-call(s32[16,18]{1,0:T(8,128)} %get-tuple-element.94.meta_ref, bf16[16,16,128,128]{3,2,1,0:T(8,128)(2,1)} %t_ref.21, bf16[2048,512]{1,0:T(8,128)(2,1)S(1)} %pad_maximum_fusion.x_ref), custom_call_target="tpu_custom_call" | custom-call | tf_op jit(solution)/shard_map/forward_rows/pallas_call | solution.py:47
  277.0 13.4 %collective-permute-done.30 = f32[512,512]{1,0:T(8,128)S(1)} collective-permute-done((f32[512,512]{1,0:T(8,128)}, f32[512,512]{1,0:T(8,128)S(1)}, u32[]{:S(2)}, u32[]{:S(2)}) %collective-permute-start.30) | collective-permute-done | bytes 1048608 | tf_op jit(solution)/shard_map/ppermute | solution.py:337
  290.4 4.2 %collective-permute-done.31 = f32[512,512]{1,0:T(8,128)} collective-permute-done((f32[512,512]{1,0:T(8,128)}, f32[512,512]{1,0:T(8,128)}, u32[]{:S(2)}, u32[]{:S(2)}) %collective-permute-start.31) | collective-permute-done | bytes 1048608 | tf_op jit(solution)/shard_map/ppermute | solution.py:338
  294.6 4.2 %fusion.14 = f32[512,512]{1,0:T(8,128)S(1)} fusion(f32[512,512]{1,0:T(8,128)} %collective-permute-done.31, f32[512,512]{1,0:T(8,128)} %get-tuple-element.81, f32[512,512]{1,0:T(8,128)S(1)} %collective-permute-done.30), kind=kOutput, calls=%fused_computation.85 | convolution fusion | flops 1611137024 | bytes 4194304 | tf_op jit(solution)/shard_map/dot_general | solution.py:413
  298.9 1.9 collective-permute-done.32
  301.7 5.7 %collective-permute-done.33 = f32[128,512]{1,0:T(8,128)S(1)} collective-permute-done((f32[128,512]{1,0:T(8,128)S(1)}, f32[128,512]{1,0:T(8,128)S(1)}, u32[]{:S(2)}, u32[]{:S(2)}) %collective-permute-start.33) | collective-permute-done | bytes 262176 | tf_op jit(solution)/shard_map/ppermute | solution.py:289
  308.2 4.3 %collective-permute-done.34 = f32[64,512]{1,0:T(8,128)S(1)} collective-permute-done((f32[64,512]{1,0:T(8,128)S(1)}, f32[64,512]{1,0:T(8,128)S(1)}, u32[]{:S(2)}, u32[]{:S(2)}) %collective-permute-start.34) | collective-permute-done | bytes 131104 | tf_op jit(solution)/shard_map/ppermute | solution.py:289
  312.8 4.7 %collective-permute-done.35 = f32[64,512]{1,0:T(8,128)S(1)} collective-permute-done((f32[64,512]{1,0:T(8,128)S(1)}, f32[64,512]{1,0:T(8,128)S(1)}, u32[]{:S(2)}, u32[]{:S(2)}) %collective-permute-start.35) | collective-permute-done | bytes 131104 | tf_op jit(solution)/shard_map/ppermute | solution.py:267
  317.7 7.2 %collective-permute-done.36 = f32[64,512]{1,0:T(8,128)S(1)} collective-permute-done((f32[64,512]{1,0:T(8,128)S(1)}, f32[64,512]{1,0:T(8,128)S(1)}, u32[]{:S(2)}, u32[]{:S(2)}) %collective-permute-start.36) | collective-permute-done | bytes 131104 | tf_op jit(solution)/shard_map/ppermute | solution.py:267
  325.6 5.7 %collective-permute-done.37 = f32[64,512]{1,0:T(8,128)S(1)} collective-permute-done((f32[64,512]{1,0:T(8,128)S(1)}, f32[64,512]{1,0:T(8,128)S(1)}, u32[]{:S(2)}, u32[]{:S(2)}) %collective-permute-start.37) | collective-permute-done | bytes 131104 | tf_op jit(solution)/shard_map/ppermute | solution.py:296
  332.1 5.7 %collective-permute-done.38 = f32[128,512]{1,0:T(8,128)S(1)} collective-permute-done((f32[128,512]{1,0:T(8,128)S(1)}, f32[128,512]{1,0:T(8,128)S(1)}, u32[]{:S(2)}, u32[]{:S(2)}) %collective-permute-start.38) | collective-permute-done | bytes 262176 | tf_op jit(solution)/shard_map/ppermute | solution.py:296
  338.0 1.9 collective-permute-done.39
  341.0 27.4 %factorize.3 = (f32[512,512]{1,0:T(8,128)}, f32[512,512]{1,0:T(8,128)}) custom-call(f32[512,512]{1,0:T(8,128)} %pad_maximum_fusion.3.g_ref), custom_call_target="tpu_custom_call" | custom-call | tf_op jit(solution)/shard_map/factorize/pallas_call | solution.py:225
  368.4 4.4 %fusion.13 = f32[512,512]{1,0:T(8,128)} fusion(f32[512,512]{1,0:T(8,128)} %get-tuple-element.92, f32[512,512]{1,0:T(8,128)} %collective-permute-done.31, f32[512,512]{1,0:T(8,128)S(1)} %copy-done.1, f32[512,512]{1,0:T(8,128)S(1)} %collective-permute-done.30), kind=kOutput, calls=%fused_computation.84 | convolution fusion | flops 1611137024 | bytes 5242880 | tf_op jit(solution)/shard_map/dot_general | solution.py:415
  (121 shorter events, 35.2 us)
Async XLA Ops:
  3.7 1.6 copy-start
  11.2 16.9 %collective-permute-start = (bf16[512,512]{1,0:T(8,128)(2,1)}, bf16[512,512]{1,0:T(8,128)(2,1)}, u32[]{:S(2)}, u32[]{:S(2)}) collective-permute-start(bf16[512,512]{1,0:T(8,128)(2,1)} %get-tuple-element.51), channel_id=1, source_target_pairs={{0,1},{3,2},{4,5},{7,6},{8,9},{11,10},{12,13},{15,14},{16,17},{19,... | collective-permute-start | bytes 1572872 | tf_op jit(solution)/shard_map/ppermute | solution.py:244
  21.7 23.6 %collective-permute-start.3 = (bf16[512,512]{1,0:T(8,128)(2,1)}, bf16[512,512]{1,0:T(8,128)(2,1)}, u32[]{:S(2)}, u32[]{:S(2)}) collective-permute-start(bf16[512,512]{1,0:T(8,128)(2,1)} %get-tuple-element.58), channel_id=1, source_target_pairs={{0,1},{3,2},{4,5},{7,6},{8,9},{11,10},{12,13},{15,14},{16,17},{19,... | collective-permute-start | bytes 1572872 | tf_op jit(solution)/shard_map/ppermute | solution.py:244
  30.5 18.7 %collective-permute-start.1 = (bf16[512,512]{1,0:T(8,128)(2,1)}, bf16[512,512]{1,0:T(8,128)(2,1)}, u32[]{:S(2)}, u32[]{:S(2)}) collective-permute-start(bf16[512,512]{1,0:T(8,128)(2,1)} %convert_element_type.76), channel_id=1, source_target_pairs={{1,2},{2,1},{5,6},{6,5},{9,10},{10,9},{13,14},{14,13},{17,18},{18,... | collective-permute-start | bytes 1572872 | tf_op jit(solution)/shard_map/ppermute | solution.py:251
  37.5 26.2 %collective-permute-start.6 = (bf16[512,512]{1,0:T(8,128)(2,1)}, bf16[512,512]{1,0:T(8,128)(2,1)}, u32[]{:S(2)}, u32[]{:S(2)}) collective-permute-start(bf16[512,512]{1,0:T(8,128)(2,1)} %get-tuple-element.63), channel_id=1, source_target_pairs={{0,1},{3,2},{4,5},{7,6},{8,9},{11,10},{12,13},{15,14},{16,17},{19,... | collective-permute-start | bytes 1572872 | tf_op jit(solution)/shard_map/ppermute | solution.py:244
  47.7 17.9 %collective-permute-start.4 = (bf16[512,512]{1,0:T(8,128)(2,1)}, bf16[512,512]{1,0:T(8,128)(2,1)}, u32[]{:S(2)}, u32[]{:S(2)}) collective-permute-start(bf16[512,512]{1,0:T(8,128)(2,1)} %fusion), channel_id=1, source_target_pairs={{1,2},{2,1},{5,6},{6,5},{9,10},{10,9},{13,14},{14,13},{17,18},{18,... | collective-permute-start | bytes 1572872 | tf_op jit(solution)/shard_map/ppermute | solution.py:251
  51.2 12.5 %copy-start.3 = (f32[512,512]{1,0:T(8,128)S(1)}, f32[512,512]{1,0:T(8,128)}, u32[]{:S(2)}) copy-start(f32[512,512]{1,0:T(8,128)} %get-tuple-element.62) | copy-start | bytes 3145732
  51.2 23.7 %collective-permute-start.2 = (bf16[512,512]{1,0:T(8,128)(2,1)}, bf16[512,512]{1,0:T(8,128)(2,1)}, u32[]{:S(2)}, u32[]{:S(2)}) collective-permute-start(bf16[512,512]{1,0:T(8,128)(2,1)} %add_convert_fusion.5), channel_id=1, source_target_pairs={{1,0},{2,3},{5,4},{6,7},{9,8},{10,11},{13,12},{14,15},{17,16},{18,... | collective-permute-start | bytes 1572872 | tf_op jit(solution)/shard_map/ppermute | solution.py:259
  58.5 7.1 %copy-start.2 = (f32[512,512]{1,0:T(8,128)S(1)}, f32[512,512]{1,0:T(8,128)}, u32[]{:S(2)}) copy-start(f32[512,512]{1,0:T(8,128)} %get-tuple-element.57) | copy-start | bytes 3145732
  58.6 12.9 %copy-start.4 = (f32[512,512]{1,0:T(8,128)S(1)}, f32[512,512]{1,0:T(8,128)}, u32[]{:S(2)}) copy-start(f32[512,512]{1,0:T(8,128)} %get-tuple-element.64) | copy-start | bytes 3145732
  58.6 12.9 %collective-permute-start.9 = (bf16[512,512]{1,0:T(8,128)(2,1)}, bf16[512,512]{1,0:T(8,128)(2,1)S(1)}, u32[]{:S(2)}, u32[]{:S(2)}) collective-permute-start(bf16[512,512]{1,0:T(8,128)(2,1)} %get-tuple-element.65), channel_id=1, source_target_pairs={{0,1},{3,2},{4,5},{7,6},{8,9},{11,10},{12,13},{15,14},{16,17},{19,... | collective-permute-start | bytes 1572872 | tf_op jit(solution)/shard_map/ppermute | solution.py:244
  65.0 7.4 %collective-permute-start.7 = (bf16[512,512]{1,0:T(8,128)(2,1)S(1)}, bf16[512,512]{1,0:T(8,128)(2,1)S(1)}, u32[]{:S(2)}, u32[]{:S(2)}) collective-permute-start(bf16[512,512]{1,0:T(8,128)(2,1)S(1)} %fusion.1), channel_id=1, source_target_pairs={{1,2},{2,1},{5,6},{6,5},{9,10},{10,9},{13,14},{14,13},{17,18},{18,... | collective-permute-start | bytes 1572872 | tf_op jit(solution)/shard_map/ppermute | solution.py:251
  67.1 12.3 %collective-permute-start.5 = (bf16[512,512]{1,0:T(8,128)(2,1)S(1)}, bf16[512,512]{1,0:T(8,128)(2,1)S(1)}, u32[]{:S(2)}, u32[]{:S(2)}) collective-permute-start(bf16[512,512]{1,0:T(8,128)(2,1)S(1)} %add_convert_fusion.4), channel_id=1, source_target_pairs={{1,0},{2,3},{5,4},{6,7},{9,8},{10,11},{13,12},{14,15},{17,16},{18,... | collective-permute-start | bytes 1572872 | tf_op jit(solution)/shard_map/ppermute | solution.py:259
  71.6 5.2 %collective-permute-start.10 = (bf16[512,512]{1,0:T(8,128)(2,1)S(1)}, bf16[512,512]{1,0:T(8,128)(2,1)S(1)}, u32[]{:S(2)}, u32[]{:S(2)}) collective-permute-start(bf16[512,512]{1,0:T(8,128)(2,1)S(1)} %fusion.2), channel_id=1, source_target_pairs={{1,2},{2,1},{5,6},{6,5},{9,10},{10,9},{13,14},{14,13},{17,18},{18,... | collective-permute-start | bytes 1572872 | tf_op jit(solution)/shard_map/ppermute | solution.py:251
  73.6 19.4 %collective-permute-start.8 = (bf16[512,512]{1,0:T(8,128)(2,1)S(1)}, bf16[512,512]{1,0:T(8,128)(2,1)S(1)}, u32[]{:S(2)}, u32[]{:S(2)}) collective-permute-start(bf16[512,512]{1,0:T(8,128)(2,1)S(1)} %add_convert_fusion.3), channel_id=1, source_target_pairs={{1,0},{2,3},{5,4},{6,7},{9,8},{10,11},{13,12},{14,15},{17,16},{18,... | collective-permute-start | bytes 1572872 | tf_op jit(solution)/shard_map/ppermute | solution.py:259
  77.0 24.1 %collective-permute-start.11 = (bf16[512,512]{1,0:T(8,128)(2,1)S(1)}, bf16[512,512]{1,0:T(8,128)(2,1)S(1)}, u32[]{:S(2)}, u32[]{:S(2)}) collective-permute-start(bf16[512,512]{1,0:T(8,128)(2,1)S(1)} %add_convert_fusion.2), channel_id=1, source_target_pairs={{1,0},{2,3},{5,4},{6,7},{9,8},{10,11},{13,12},{14,15},{17,16},{18,... | collective-permute-start | bytes 1572872 | tf_op jit(solution)/shard_map/ppermute | solution.py:259
  93.0 8.2 %copy-start.10 = (bf16[512,512]{1,0:T(8,128)(2,1)S(1)}, bf16[512,512]{1,0:T(8,128)(2,1)}, u32[]{:S(2)}) copy-start(bf16[512,512]{1,0:T(8,128)(2,1)} %broadcast_select_fusion.5.refs_0_) | copy-start | bytes 1572868
  93.0 8.2 %copy-start.11 = (bf16[512,512]{1,0:T(8,128)(2,1)S(1)}, bf16[512,512]{1,0:T(8,128)(2,1)}, u32[]{:S(2)}) copy-start(bf16[512,512]{1,0:T(8,128)(2,1)} %broadcast_select_fusion.4.refs_1_) | copy-start | bytes 1572868
  93.1 10.0 %copy-start.9 = (bf16[512,512]{1,0:T(8,128)(2,1)}, bf16[512,512]{1,0:T(8,128)(2,1)S(1)}, u32[]{:S(2)}) copy-start(bf16[512,512]{1,0:T(8,128)(2,1)S(1)} %broadcast_select_fusion.3.refs_0_) | copy-start | bytes 1572868
  101.2 1.9 copy-start.8
  103.1 9.6 %collective-permute-start.12 = (f32[256,512]{1,0:T(8,128)S(1)}, f32[256,512]{1,0:T(8,128)S(1)}, u32[]{:S(2)}, u32[]{:S(2)}) collective-permute-start(f32[256,512]{1,0:T(8,128)S(1)} %constant_dynamic-slice_fusion.7), channel_id=1, source_target_pairs={{0,4},{4,0},{8,12},{12,8},{16,20},{20,16},{24,28},{28,24},{1,5},{5... | collective-permute-start | bytes 1572872 | tf_op jit(solution)/shard_map/ppermute | solution.py:289
  112.8 10.8 %collective-permute-start.13 = (f32[128,512]{1,0:T(8,128)S(1)}, f32[128,512]{1,0:T(8,128)S(1)}, u32[]{:S(2)}, u32[]{:S(2)}) collective-permute-start(f32[128,512]{1,0:T(8,128)S(1)} %constant_dynamic-slice_fusion.6), channel_id=1, source_target_pairs={{0,8},{4,20},{8,0},{12,28},{16,24},{20,4},{24,16},{28,12},{1,9},{5... | collective-permute-start | bytes 786440 | tf_op jit(solution)/shard_map/ppermute | solution.py:289
  125.5 18.2 %collective-permute-start.17 = (f32[1024,512]{1,0:T(8,128)S(1)}, f32[1024,512]{1,0:T(8,128)}, u32[]{:S(2)}, u32[]{:S(2)}) collective-permute-start(f32[1024,512]{1,0:T(8,128)S(1)} %constant_dynamic-slice_fusion.4), channel_id=1, source_target_pairs={{0,4},{4,0},{8,12},{12,8},{16,20},{20,16},{24,28},{28,24},{1,5},{5... | collective-permute-start | bytes 6291464 | tf_op jit(solution)/shard_map/ppermute | solution.py:289
  125.6 5.0 %collective-permute-start.14 = (f32[64,512]{1,0:T(8,128)S(1)}, f32[64,512]{1,0:T(8,128)S(1)}, u32[]{:S(2)}, u32[]{:S(2)}) collective-permute-start(f32[64,512]{1,0:T(8,128)S(1)} %constant_dynamic-slice_fusion.5), channel_id=1, source_target_pairs={{0,16},{4,12},{8,24},{12,4},{16,0},{20,28},{24,8},{28,20},{1,17},{... | collective-permute-start | bytes 393224 | tf_op jit(solution)/shard_map/ppermute | solution.py:289
  130.6 5.1 %collective-permute-start.15 = (f32[64,512]{1,0:T(8,128)S(1)}, f32[64,512]{1,0:T(8,128)S(1)}, u32[]{:S(2)}, u32[]{:S(2)}) collective-permute-start(f32[64,512]{1,0:T(8,128)S(1)} %dynamic-slice_add_fusion.6), channel_id=1, source_target_pairs={{0,1},{1,0},{2,3},{3,2},{4,5},{5,4},{6,7},{7,6},{8,9},{9,8},{10,11... | collective-permute-start | bytes 393224 | tf_op jit(solution)/shard_map/ppermute | solution.py:267
  135.7 7.9 %collective-permute-start.16 = (f32[64,512]{1,0:T(8,128)S(1)}, f32[64,512]{1,0:T(8,128)S(1)}, u32[]{:S(2)}, u32[]{:S(2)}) collective-permute-start(f32[64,512]{1,0:T(8,128)S(1)} %add.144), channel_id=1, source_target_pairs={{0,2},{1,3},{2,0},{3,1},{4,6},{5,7},{6,4},{7,5},{8,10},{9,11},{10,... | collective-permute-start | bytes 393224 | tf_op jit(solution)/shard_map/ppermute | solution.py:267
  146.4 5.0 %collective-permute-start.18 = (f32[64,512]{1,0:T(8,128)S(1)}, f32[64,512]{1,0:T(8,128)S(1)}, u32[]{:S(2)}, u32[]{:S(2)}) collective-permute-start(f32[64,512]{1,0:T(8,128)S(1)} %add.145), channel_id=1, source_target_pairs={{0,16},{4,12},{8,24},{12,4},{16,0},{20,28},{24,8},{28,20},{1,17},{... | collective-permute-start | bytes 393224 | tf_op jit(solution)/shard_map/ppermute | solution.py:296
  151.5 6.5 %collective-permute-start.19 = (f32[128,512]{1,0:T(8,128)S(1)}, f32[128,512]{1,0:T(8,128)}, u32[]{:S(2)}, u32[]{:S(2)}) collective-permute-start(f32[128,512]{1,0:T(8,128)S(1)} %pad_maximum_fusion.7), channel_id=1, source_target_pairs={{0,8},{4,20},{8,0},{12,28},{16,24},{20,4},{24,16},{28,12},{1,9},{5... | collective-permute-start | bytes 786440 | tf_op jit(solution)/shard_map/ppermute | solution.py:296
  152.1 11.6 %collective-permute-start.21 = (bf16[512,512]{1,0:T(8,128)(2,1)S(1)}, bf16[512,512]{1,0:T(8,128)(2,1)}, u32[]{:S(2)}, u32[]{:S(2)}) collective-permute-start(bf16[512,512]{1,0:T(8,128)(2,1)S(1)} %dynamic-slice_convert_fusion), channel_id=1, source_target_pairs={{0,8},{4,20},{8,0},{12,28},{16,24},{20,4},{24,16},{28,12},{1,9},{5... | collective-permute-start | bytes 1572872 | tf_op jit(solution)/shard_map/ppermute | solution.py:289
  159.1 0.9 copy-start.6
  159.9 5.0 %collective-permute-start.20 = (f32[256,512]{1,0:T(8,128)}, f32[256,512]{1,0:T(8,128)}, u32[]{:S(2)}, u32[]{:S(2)}) collective-permute-start(f32[256,512]{1,0:T(8,128)} %pad_maximum_fusion.4), channel_id=1, source_target_pairs={{0,4},{4,0},{8,12},{12,8},{16,20},{20,16},{24,28},{28,24},{1,5},{5... | collective-permute-start | bytes 1572872 | tf_op jit(solution)/shard_map/ppermute | solution.py:296
  163.7 1.3 copy-start.7
  167.2 28.3 %collective-permute-start.22 = (f32[256,512]{1,0:T(8,128)S(1)}, f32[256,512]{1,0:T(8,128)S(1)}, u32[]{:S(2)}, u32[]{:S(2)}) collective-permute-start(f32[256,512]{1,0:T(8,128)S(1)} %constant_dynamic-slice_fusion.3), channel_id=1, source_target_pairs={{0,16},{4,12},{8,24},{12,4},{16,0},{20,28},{24,8},{28,20},{1,17},{... | collective-permute-start | bytes 1572872 | tf_op jit(solution)/shard_map/ppermute | solution.py:289
  197.8 6.8 %collective-permute-start.23 = (bf16[256,512]{1,0:T(8,128)(2,1)S(1)}, bf16[256,512]{1,0:T(8,128)(2,1)S(1)}, u32[]{:S(2)}, u32[]{:S(2)}) collective-permute-start(bf16[256,512]{1,0:T(8,128)(2,1)S(1)} %convolution_convert_fusion), channel_id=1, source_target_pairs={{0,16},{4,12},{8,24},{12,4},{16,0},{20,28},{24,8},{28,20},{1,17},{... | collective-permute-start | bytes 786440 | tf_op jit(solution)/shard_map/ppermute | solution.py:296
  204.7 10.0 %collective-permute-start.24 = (bf16[512,512]{1,0:T(8,128)(2,1)S(1)}, bf16[512,512]{1,0:T(8,128)(2,1)S(1)}, u32[]{:S(2)}, u32[]{:S(2)}) collective-permute-start(bf16[512,512]{1,0:T(8,128)(2,1)S(1)} %pad_maximum_fusion.5), channel_id=1, source_target_pairs={{0,8},{4,20},{8,0},{12,28},{16,24},{20,4},{24,16},{28,12},{1,9},{5... | collective-permute-start | bytes 1572872 | tf_op jit(solution)/shard_map/ppermute | solution.py:296
  215.0 2.7 collective-permute-start.25
  224.1 13.4 %collective-permute-start.26 = (bf16[512,512]{1,0:T(8,128)(2,1)}, bf16[512,512]{1,0:T(8,128)(2,1)}, u32[]{:S(2)}, u32[]{:S(2)}) collective-permute-start(bf16[512,512]{1,0:T(8,128)(2,1)} %get-tuple-element.85), channel_id=1, source_target_pairs={{0,1},{4,5},{8,9},{12,13},{16,17},{20,21},{24,25},{28,29}} | collective-permute-start | bytes 1572872 | tf_op jit(solution)/shard_map/ppermute | solution.py:337
  226.4 11.1 %collective-permute-start.27 = (bf16[512,512]{1,0:T(8,128)(2,1)}, bf16[512,512]{1,0:T(8,128)(2,1)}, u32[]{:S(2)}, u32[]{:S(2)}) collective-permute-start(bf16[512,512]{1,0:T(8,128)(2,1)} %get-tuple-element.85), channel_id=1, source_target_pairs={{3,2},{7,6},{11,10},{15,14},{19,18},{23,22},{27,26},{31,30}} | collective-permute-start | bytes 1572872 | tf_op jit(solution)/shard_map/ppermute | solution.py:338
  227.9 9.7 %copy-start.12 = (f32[512,512]{1,0:T(8,128)S(1)}, f32[512,512]{1,0:T(8,128)}, u32[]{:S(2)}) copy-start(f32[512,512]{1,0:T(8,128)} %get-tuple-element.84) | copy-start | bytes 3145732
  240.4 15.5 %collective-permute-start.28 = (bf16[512,512]{1,0:T(8,128)(2,1)}, bf16[512,512]{1,0:T(8,128)(2,1)}, u32[]{:S(2)}, u32[]{:S(2)}) collective-permute-start(bf16[512,512]{1,0:T(8,128)(2,1)} %get-tuple-element.99), channel_id=1, source_target_pairs={{0,1},{1,2},{4,5},{5,6},{8,9},{9,10},{12,13},{13,14},{16,17},{17,1... | collective-permute-start | bytes 1572872 | tf_op jit(solution)/shard_map/ppermute | solution.py:337
  245.6 10.3 %collective-permute-start.29 = (bf16[512,512]{1,0:T(8,128)(2,1)}, bf16[512,512]{1,0:T(8,128)(2,1)}, u32[]{:S(2)}, u32[]{:S(2)}) collective-permute-start(bf16[512,512]{1,0:T(8,128)(2,1)} %get-tuple-element.98), channel_id=1, source_target_pairs={{3,2},{2,1},{7,6},{6,5},{11,10},{10,9},{15,14},{14,13},{19,18},{18... | collective-permute-start | bytes 1572872 | tf_op jit(solution)/shard_map/ppermute | solution.py:338
  247.0 8.8 %copy-start.5 = (f32[512,512]{1,0:T(8,128)S(1)}, f32[512,512]{1,0:T(8,128)}, u32[]{:S(2)}) copy-start(f32[512,512]{1,0:T(8,128)} %get-tuple-element.82) | copy-start | bytes 3145732
  259.0 31.4 %collective-permute-start.30 = (f32[512,512]{1,0:T(8,128)}, f32[512,512]{1,0:T(8,128)S(1)}, u32[]{:S(2)}, u32[]{:S(2)}) collective-permute-start(f32[512,512]{1,0:T(8,128)} %get-tuple-element.97), channel_id=1, source_target_pairs={{0,1},{1,2},{2,3},{4,5},{5,6},{6,7},{8,9},{9,10},{10,11},{12,13},{... | collective-permute-start | bytes 3145736 | tf_op jit(solution)/shard_map/ppermute | solution.py:337
  269.8 24.8 %collective-permute-start.31 = (f32[512,512]{1,0:T(8,128)}, f32[512,512]{1,0:T(8,128)}, u32[]{:S(2)}, u32[]{:S(2)}) collective-permute-start(f32[512,512]{1,0:T(8,128)} %get-tuple-element.96), channel_id=1, source_target_pairs={{3,2},{2,1},{1,0},{7,6},{6,5},{5,4},{11,10},{10,9},{9,8},{15,14},{... | collective-permute-start | bytes 3145736 | tf_op jit(solution)/shard_map/ppermute | solution.py:338
  298.9 2.0 collective-permute-start.32
  301.0 6.4 %collective-permute-start.33 = (f32[128,512]{1,0:T(8,128)S(1)}, f32[128,512]{1,0:T(8,128)S(1)}, u32[]{:S(2)}, u32[]{:S(2)}) collective-permute-start(f32[128,512]{1,0:T(8,128)S(1)} %constant_dynamic-slice_fusion.1), channel_id=1, source_target_pairs={{0,8},{4,20},{8,0},{12,28},{16,24},{20,4},{24,16},{28,12},{1,9},{5... | collective-permute-start | bytes 786440 | tf_op jit(solution)/shard_map/ppermute | solution.py:289
  307.5 5.0 %collective-permute-start.34 = (f32[64,512]{1,0:T(8,128)S(1)}, f32[64,512]{1,0:T(8,128)S(1)}, u32[]{:S(2)}, u32[]{:S(2)}) collective-permute-start(f32[64,512]{1,0:T(8,128)S(1)} %constant_dynamic-slice_fusion), channel_id=1, source_target_pairs={{0,16},{4,12},{8,24},{12,4},{16,0},{20,28},{24,8},{28,20},{1,17},{... | collective-permute-start | bytes 393224 | tf_op jit(solution)/shard_map/ppermute | solution.py:289
  312.5 5.0 %collective-permute-start.35 = (f32[64,512]{1,0:T(8,128)S(1)}, f32[64,512]{1,0:T(8,128)S(1)}, u32[]{:S(2)}, u32[]{:S(2)}) collective-permute-start(f32[64,512]{1,0:T(8,128)S(1)} %dynamic-slice_add_fusion.5), channel_id=1, source_target_pairs={{0,1},{1,0},{2,3},{3,2},{4,5},{5,4},{6,7},{7,6},{8,9},{9,8},{10,11... | collective-permute-start | bytes 393224 | tf_op jit(solution)/shard_map/ppermute | solution.py:267
  317.6 7.3 %collective-permute-start.36 = (f32[64,512]{1,0:T(8,128)S(1)}, f32[64,512]{1,0:T(8,128)S(1)}, u32[]{:S(2)}, u32[]{:S(2)}) collective-permute-start(f32[64,512]{1,0:T(8,128)S(1)} %add.164), channel_id=1, source_target_pairs={{0,2},{1,3},{2,0},{3,1},{4,6},{5,7},{6,4},{7,5},{8,10},{9,11},{10,... | collective-permute-start | bytes 393224 | tf_op jit(solution)/shard_map/ppermute | solution.py:267
  324.9 6.4 %collective-permute-start.37 = (f32[64,512]{1,0:T(8,128)S(1)}, f32[64,512]{1,0:T(8,128)S(1)}, u32[]{:S(2)}, u32[]{:S(2)}) collective-permute-start(f32[64,512]{1,0:T(8,128)S(1)} %add.165), channel_id=1, source_target_pairs={{0,16},{4,12},{8,24},{12,4},{16,0},{20,28},{24,8},{28,20},{1,17},{... | collective-permute-start | bytes 393224 | tf_op jit(solution)/shard_map/ppermute | solution.py:296
  331.4 6.4 %collective-permute-start.38 = (f32[128,512]{1,0:T(8,128)S(1)}, f32[128,512]{1,0:T(8,128)S(1)}, u32[]{:S(2)}, u32[]{:S(2)}) collective-permute-start(f32[128,512]{1,0:T(8,128)S(1)} %pad_maximum_fusion.8), channel_id=1, source_target_pairs={{0,8},{4,20},{8,0},{12,28},{16,24},{20,4},{24,16},{28,12},{1,9},{5... | collective-permute-start | bytes 786440 | tf_op jit(solution)/shard_map/ppermute | solution.py:296
  337.9 2.0 collective-permute-start.39
  340.0 28.4 %copy-start.1 = (f32[512,512]{1,0:T(8,128)S(1)}, f32[512,512]{1,0:T(8,128)}, u32[]{:S(2)}) copy-start(f32[512,512]{1,0:T(8,128)} %get-tuple-element.81) | copy-start | bytes 3145732

commit v6 on v4

--- a/solution.py
+++ b/solution.py
@@ -290,9 +290,8 @@
     steps = list(halving(bits))
     for pairs, own in reversed(steps):
         got = lax.ppermute(part, "row", pairs)
-        low = jnp.where(own == 0, part, got)
-        high = jnp.where(own == 0, got, part)
-        part = jnp.concatenate([low, high], 0)
+        mine = (jnp.arange(2) == own)[:, None, None]
+        part = jnp.where(mine, part[None], got[None]).reshape(2 * part.shape[0], part.shape[1])
     return part
 
 

time: 370 us -> 367 us (level)
  waiting for transfers between devices: 128 us -> 123 us
  Pallas kernels: 125 us -> 121 us
    select_n x9, other arithmetic: 2.91 us -> 6.69 us  [row_gather(): jnp.where(mine, part[None], got[None])]
    ppermute x9, waiting for transfers between devices: 18.8 us -> 15 us  [row_step(): return keep + lax.ppermute(give, 'row', pairs).astype(value.dtype)]
  transfers between devices with their start and end apart: 40 -> 40, of which waited for: 26 -> 26; matrix products, arithmetic and copies ran while one was open for 5% -> 5% of each run, Pallas kernels for 24% -> 23%
where the time goes in v6:
time: 367 us; the launch traced here: 363 us
  waiting for transfers between devices  123 us (34%)
  Pallas kernels  121 us (33%)
  starting transfers between devices  70 us (19%)
  other arithmetic  30.9 us (8%)
  matrix products  12.8 us (3%)
  local copies, waits for them, and re-layouts  4.28 us (1%)
    pallas_call x2, Pallas kernels, cholesky(): pl.pallas_call(functools.partial(chol_body, scale, group), out_shape=(s,...  54.7 us
    pallas_call x8, Pallas kernels, forward(): pl.pallas_call(functools.partial(forward_body, group), out_shape=[jax.Sha...  41.4 us
    ppermute x9, waiting for transfers between devices, row_gather(): got = lax.ppermute(part, 'row', pairs)  39.8 us
    pallas_call x3, Pallas kernels, backward(): pl.pallas_call(functools.partial(backward_body, group, base, len(panels))...  24.6 us
    ppermute x3, waiting for transfers between devices, line_scatter(): right = lax.ppermute(up.astype(wire), 'col', [(i, i + 1) for i in range(t)])  22.2 us
    ppermute x4, waiting for transfers between devices, col_sum(): lax.ppermute(value, 'col', [(i, i ^ 1 << bit) for i in range(n)])  21.3 us
    ppermute x4, starting transfers between devices, line_inward(): got = lax.ppermute(rounded, 'col', [(s, s + 1), (n - 1 - s, n - 2 - s)])  20.6 us
    ppermute x3, starting transfers between devices, line_scatter(): right = lax.ppermute(up.astype(wire), 'col', [(i, i + 1) for i in range(t)])  15.8 us
  transfers between devices with their start and end apart: 40, of which 26 were waited for; matrix products, arithmetic and copies ran while one was open for 5% of the time, Pallas kernels for 23%

profile of v6, /device:TPU:0, one launch (start us, length us, event | category | flops | bytes accessed | tf_op | source)
XLA Modules:
  0.0 363.2 jit_solution(16694536137068191226)
XLA Ops:
  0.6 1.6 copy-done
  2.2 5.1 %forward_rows.8 = (f32[512,512]{1,0:T(8,128)}, bf16[512,512]{1,0:T(8,128)(2,1)}) custom-call(s32[1]{0:T(128)} %constant.9.clone.1.base_ref, s32[16,16]{1,0:T(8,128)} %idx_ref.21, s32[16]{0:T(128)} %bitcast.45, bf16[16,16,128,128]{3,2,1,0:T(8,128)(2,1)} %t_ref.21, bf16[2048,512]{1,0:T(8,128)(2,1)S(1)} %copy-done), custom_call_target="tpu_custom_call" | custom-call | tf_op jit(solution)/shard_map/forward_rows/pallas_call | solution.py:43
  7.3 5.8 %collective-permute-start = (bf16[512,512]{1,0:T(8,128)(2,1)}, bf16[512,512]{1,0:T(8,128)(2,1)}, u32[]{:S(2)}, u32[]{:S(2)}) collective-permute-start(bf16[512,512]{1,0:T(8,128)(2,1)} %get-tuple-element.51), channel_id=1, source_target_pairs={{0,1},{3,2},{4,5},{7,6},{8,9},{11,10},{12,13},{15,14},{16,17},{19,... | collective-permute-start | bytes 1572872 | tf_op jit(solution)/shard_map/ppermute | solution.py:240
  13.1 5.1 %forward_rows.9 = (f32[512,512]{1,0:T(8,128)}, bf16[512,512]{1,0:T(8,128)(2,1)}) custom-call(s32[1]{0:T(128)} %constant.10.clone.1.base_ref, s32[16,16]{1,0:T(8,128)} %idx_ref.21, s32[16]{0:T(128)} %bitcast.46, bf16[16,16,128,128]{3,2,1,0:T(8,128)(2,1)} %t_ref.21, bf16[2048,512]{1,0:T(8,128)(2,1)S(1)} %copy-done), custom_call_target="tpu_custom_call" | custom-call | tf_op jit(solution)/shard_map/forward_rows/pallas_call | solution.py:43
  18.3 2.1 collective-permute-start.3
  20.3 4.6 %collective-permute-done = bf16[512,512]{1,0:T(8,128)(2,1)} collective-permute-done((bf16[512,512]{1,0:T(8,128)(2,1)}, bf16[512,512]{1,0:T(8,128)(2,1)}, u32[]{:S(2)}, u32[]{:S(2)}) %collective-permute-start) | collective-permute-done | bytes 524320 | tf_op jit(solution)/shard_map/ppermute | solution.py:240
  24.9 1.5 convert_add_fusion.6
  28.8 5.1 %forward_rows.10 = (f32[512,512]{1,0:T(8,128)}, bf16[512,512]{1,0:T(8,128)(2,1)}) custom-call(s32[1]{0:T(128)} %constant.11.clone.1.base_ref, s32[16,16]{1,0:T(8,128)} %idx_ref.21, s32[16]{0:T(128)} %bitcast.47, bf16[16,16,128,128]{3,2,1,0:T(8,128)(2,1)} %t_ref.21, bf16[2048,512]{1,0:T(8,128)(2,1)S(1)} %copy-done), custom_call_target="tpu_custom_call" | custom-call | tf_op jit(solution)/shard_map/forward_rows/pallas_call | solution.py:43
  33.9 7.2 %collective-permute-start.6 = (bf16[512,512]{1,0:T(8,128)(2,1)}, bf16[512,512]{1,0:T(8,128)(2,1)}, u32[]{:S(2)}, u32[]{:S(2)}) collective-permute-start(bf16[512,512]{1,0:T(8,128)(2,1)} %get-tuple-element.63), channel_id=1, source_target_pairs={{0,1},{3,2},{4,5},{7,6},{8,9},{11,10},{12,13},{15,14},{16,17},{19,... | collective-permute-start | bytes 1572872 | tf_op jit(solution)/shard_map/ppermute | solution.py:240
  41.1 2.3 fusion
  43.5 1.5 collective-permute-start.4
  45.0 2.0 add_convert_fusion.5
  48.4 5.1 %forward_rows.11 = (f32[512,512]{1,0:T(8,128)}, bf16[512,512]{1,0:T(8,128)(2,1)}) custom-call(s32[1]{0:T(128)} %constant.12.clone.1.base_ref, s32[16,16]{1,0:T(8,128)} %idx_ref.21, s32[16]{0:T(128)} %bitcast.48, bf16[16,16,128,128]{3,2,1,0:T(8,128)(2,1)} %t_ref.21, bf16[2048,512]{1,0:T(8,128)(2,1)S(1)} %copy-done), custom_call_target="tpu_custom_call" | custom-call | tf_op jit(solution)/shard_map/forward_rows/pallas_call | solution.py:43
  53.5 5.5 %collective-permute-start.9 = (bf16[512,512]{1,0:T(8,128)(2,1)}, bf16[512,512]{1,0:T(8,128)(2,1)S(1)}, u32[]{:S(2)}, u32[]{:S(2)}) collective-permute-start(bf16[512,512]{1,0:T(8,128)(2,1)} %get-tuple-element.65), channel_id=1, source_target_pairs={{0,1},{3,2},{4,5},{7,6},{8,9},{11,10},{12,13},{15,14},{16,17},{19,... | collective-permute-start | bytes 1572872 | tf_op jit(solution)/shard_map/ppermute | solution.py:240
  63.7 4.0 %collective-permute-done.9 = bf16[512,512]{1,0:T(8,128)(2,1)S(1)} collective-permute-done((bf16[512,512]{1,0:T(8,128)(2,1)}, bf16[512,512]{1,0:T(8,128)(2,1)S(1)}, u32[]{:S(2)}, u32[]{:S(2)}) %collective-permute-start.9) | collective-permute-done | bytes 524320 | tf_op jit(solution)/shard_map/ppermute | solution.py:240
  71.1 1.9 broadcast_select_fusion.3.refs_0_
  74.7 3.1 collective-permute-done.5
  78.7 9.4 %backward_rows.3.refs_1_ = f32[2048,512]{1,0:T(8,128)} custom-call(s32[16,16]{1,0:T(8,128)} %idx_ref.21, s32[16]{0:T(128)} %bitcast.49, bf16[16,16,128,128]{3,2,1,0:T(8,128)(2,1)} %t_ref.21, bf16[512,512]{1,0:T(8,128)(2,1)} %broadcast_select_fusion.3.refs_0_, bf16[512,512]{1,0:T(8,128)(2,1)} %broadcast_select_fusion.2.refs_1_), custom_call_target="tpu_custom_call" | custom-call | tf_op jit(solution)/shard_map/backward_rows/pallas_call | solution.py:106
  89.2 8.1 %collective-permute-done.11 = bf16[512,512]{1,0:T(8,128)(2,1)S(1)} collective-permute-done((bf16[512,512]{1,0:T(8,128)(2,1)S(1)}, bf16[512,512]{1,0:T(8,128)(2,1)S(1)}, u32[]{:S(2)}, u32[]{:S(2)}) %collective-permute-start.11) | collective-permute-done | bytes 524320 | tf_op jit(solution)/shard_map/ppermute | solution.py:255
  97.4 1.8 fusion.6
  99.4 7.6 %backward_rows.4.refs_1_ = f32[2048,512]{1,0:T(8,128)} custom-call(s32[16,16]{1,0:T(8,128)} %idx_ref.21, s32[16]{0:T(128)} %bitcast.50, bf16[16,16,128,128]{3,2,1,0:T(8,128)(2,1)} %t_ref.21, bf16[512,512]{1,0:T(8,128)(2,1)} %copy-done.7, f32[2048,512]{1,0:T(8,128)} %backward_rows.3.refs_1_), custom_call_target="tpu_custom_call" | custom-call | tf_op jit(solution)/shard_map/backward_rows/pallas_call | solution.py:106
  107.2 2.3 collective-permute-start.13
  109.5 7.6 %backward_rows.5 = f32[2048,512]{1,0:T(8,128)} custom-call(s32[16,16]{1,0:T(8,128)} %idx_ref.21, s32[16]{0:T(128)} %bitcast.51, bf16[16,16,128,128]{3,2,1,0:T(8,128)(2,1)} %t_ref.21, bf16[512,512]{1,0:T(8,128)(2,1)} %copy-done.6, f32[2048,512]{1,0:T(8,128)} %backward_rows.4.refs_1_), custom_call_target="tpu_custom_call" | custom-call | tf_op jit(solution)/shard_map/backward_rows/pallas_call | solution.py:106
  117.2 1.8 constant_dynamic-slice_fusion.4
  119.7 2.4 collective-permute-start.14
  122.1 2.9 collective-permute-done.14
  125.1 2.0 collective-permute-start.15
  127.1 3.3 collective-permute-done.15
  130.4 2.1 collective-permute-start.16
  132.5 6.1 %collective-permute-done.16 = f32[64,512]{1,0:T(8,128)S(1)} collective-permute-done((f32[64,512]{1,0:T(8,128)S(1)}, f32[64,512]{1,0:T(8,128)S(1)}, u32[]{:S(2)}, u32[]{:S(2)}) %collective-permute-start.16) | collective-permute-done | bytes 131104 | tf_op jit(solution)/shard_map/ppermute | solution.py:263
  138.6 2.7 dynamic-slice_add_fusion
  143.4 4.3 %collective-permute-done.18 = f32[64,512]{1,0:T(8,128)S(1)} collective-permute-done((f32[64,512]{1,0:T(8,128)S(1)}, f32[64,512]{1,0:T(8,128)S(1)}, u32[]{:S(2)}, u32[]{:S(2)}) %collective-permute-start.18) | collective-permute-done | bytes 131104 | tf_op jit(solution)/shard_map/ppermute | solution.py:292
  149.3 5.7 %collective-permute-done.19 = f32[128,512]{1,0:T(8,128)S(1)} collective-permute-done((f32[128,512]{1,0:T(8,128)S(1)}, f32[128,512]{1,0:T(8,128)S(1)}, u32[]{:S(2)}, u32[]{:S(2)}) %collective-permute-start.19) | collective-permute-done | bytes 262176 | tf_op jit(solution)/shard_map/ppermute | solution.py:292
  158.1 2.4 bitcast_select_fusion.3.g_ref
  161.3 27.4 %factorize.2 = (f32[512,512]{1,0:T(8,128)}, f32[512,512]{1,0:T(8,128)}) custom-call(f32[512,512]{1,0:T(8,128)} %bitcast_select_fusion.3.g_ref), custom_call_target="tpu_custom_call" | custom-call | tf_op jit(solution)/shard_map/factorize/pallas_call | solution.py:221
  188.7 2.3 convolution_convert_fusion
  192.5 5.0 %collective-permute-done.23 = bf16[256,512]{1,0:T(8,128)(2,1)S(1)} collective-permute-done((bf16[256,512]{1,0:T(8,128)(2,1)S(1)}, bf16[256,512]{1,0:T(8,128)(2,1)S(1)}, u32[]{:S(2)}, u32[]{:S(2)}) %collective-permute-start.23) | collective-permute-done | bytes 262176 | tf_op jit(solution)/shard_map/ppermute | solution.py:292
  199.1 7.8 %collective-permute-done.24 = bf16[512,512]{1,0:T(8,128)(2,1)S(1)} collective-permute-done((bf16[512,512]{1,0:T(8,128)(2,1)S(1)}, bf16[512,512]{1,0:T(8,128)(2,1)S(1)}, u32[]{:S(2)}, u32[]{:S(2)}) %collective-permute-start.24) | collective-permute-done | bytes 524320 | tf_op jit(solution)/shard_map/ppermute | solution.py:292
  207.3 2.7 collective-permute-done.25
  209.9 1.6 bitcast_select_fusion.x_ref
  211.6 5.1 %forward_rows.15 = (f32[512,512]{1,0:T(8,128)}, bf16[512,512]{1,0:T(8,128)(2,1)}) custom-call(s32[1]{0:T(128)} %bitcast.17.base_ref, s32[16,16]{1,0:T(8,128)} %idx_ref.21, s32[16]{0:T(128)} %bitcast.52, bf16[16,16,128,128]{3,2,1,0:T(8,128)(2,1)} %t_ref.21, bf16[2048,512]{1,0:T(8,128)(2,1)S(1)} %bitcast_select_fusion.x_ref), custom_call_target="tpu_custom_call" | custom-call | tf_op jit(solution)/shard_map/forward_rows/pallas_call | solution.py:43
  216.7 2.3 collective-permute-start.26
  220.5 5.3 %forward_rows.13 = (f32[512,512]{1,0:T(8,128)}, bf16[512,512]{1,0:T(8,128)(2,1)}) custom-call(s32[1]{0:T(128)} %bitcast.15.base_ref, s32[16,16]{1,0:T(8,128)} %idx_ref.21, s32[16]{0:T(128)} %bitcast.53, bf16[16,16,128,128]{3,2,1,0:T(8,128)(2,1)} %t_ref.21, bf16[2048,512]{1,0:T(8,128)(2,1)S(1)} %bitcast_select_fusion.x_ref), custom_call_target="tpu_custom_call" | custom-call | tf_op jit(solution)/shard_map/forward_rows/pallas_call | solution.py:43
  225.8 4.3 %collective-permute-done.26 = bf16[512,512]{1,0:T(8,128)(2,1)} collective-permute-done((bf16[512,512]{1,0:T(8,128)(2,1)}, bf16[512,512]{1,0:T(8,128)(2,1)}, u32[]{:S(2)}, u32[]{:S(2)}) %collective-permute-start.26) | collective-permute-done | bytes 524320 | tf_op jit(solution)/shard_map/ppermute | solution.py:332
  230.1 2.9 add_convert_fusion
  233.0 5.2 %collective-permute-start.28 = (bf16[512,512]{1,0:T(8,128)(2,1)}, bf16[512,512]{1,0:T(8,128)(2,1)}, u32[]{:S(2)}, u32[]{:S(2)}) collective-permute-start(bf16[512,512]{1,0:T(8,128)(2,1)} %get-tuple-element.97), channel_id=1, source_target_pairs={{0,1},{1,2},{4,5},{5,6},{8,9},{9,10},{12,13},{13,14},{16,17},{17,1... | collective-permute-start | bytes 1572872 | tf_op jit(solution)/shard_map/ppermute | solution.py:332
  239.6 5.3 %forward_rows.14 = (f32[512,512]{1,0:T(8,128)}, bf16[512,512]{1,0:T(8,128)(2,1)}) custom-call(s32[1]{0:T(128)} %bitcast.16.base_ref, s32[16,16]{1,0:T(8,128)} %idx_ref.21, s32[16]{0:T(128)} %bitcast.54, bf16[16,16,128,128]{3,2,1,0:T(8,128)(2,1)} %t_ref.21, bf16[2048,512]{1,0:T(8,128)(2,1)S(1)} %bitcast_select_fusion.x_ref), custom_call_target="tpu_custom_call" | custom-call | tf_op jit(solution)/shard_map/forward_rows/pallas_call | solution.py:43
  244.9 3.4 collective-permute-done.28
  248.3 3.2 convert_add_fusion
  251.5 8.3 %collective-permute-start.30 = (f32[512,512]{1,0:T(8,128)}, f32[512,512]{1,0:T(8,128)S(1)}, u32[]{:S(2)}, u32[]{:S(2)}) collective-permute-start(f32[512,512]{1,0:T(8,128)} %get-tuple-element.95), channel_id=1, source_target_pairs={{0,1},{1,2},{2,3},{4,5},{5,6},{6,7},{8,9},{9,10},{10,11},{12,13},{... | collective-permute-start | bytes 3145736 | tf_op jit(solution)/shard_map/ppermute | solution.py:332
  261.1 5.2 %forward_rows.12 = (f32[512,512]{1,0:T(8,128)}, bf16[512,512]{1,0:T(8,128)(2,1)}) custom-call(s32[1]{0:T(128)} %bitcast.base_ref, s32[16,16]{1,0:T(8,128)} %idx_ref.21, s32[16]{0:T(128)} %bitcast.55, bf16[16,16,128,128]{3,2,1,0:T(8,128)(2,1)} %t_ref.21, bf16[2048,512]{1,0:T(8,128)(2,1)S(1)} %bitcast_select_fusion.x_ref), custom_call_target="tpu_custom_call" | custom-call | tf_op jit(solution)/shard_map/forward_rows/pallas_call | solution.py:43
  266.3 14.5 %collective-permute-done.30 = f32[512,512]{1,0:T(8,128)S(1)} collective-permute-done((f32[512,512]{1,0:T(8,128)}, f32[512,512]{1,0:T(8,128)S(1)}, u32[]{:S(2)}, u32[]{:S(2)}) %collective-permute-start.30) | collective-permute-done | bytes 1048608 | tf_op jit(solution)/shard_map/ppermute | solution.py:332
  280.8 4.2 %collective-permute-done.31 = f32[512,512]{1,0:T(8,128)} collective-permute-done((f32[512,512]{1,0:T(8,128)}, f32[512,512]{1,0:T(8,128)}, u32[]{:S(2)}, u32[]{:S(2)}) %collective-permute-start.31) | collective-permute-done | bytes 1048608 | tf_op jit(solution)/shard_map/ppermute | solution.py:333
  284.9 4.2 %fusion.14 = f32[512,512]{1,0:T(8,128)S(1)} fusion(f32[512,512]{1,0:T(8,128)} %collective-permute-done.31, f32[512,512]{1,0:T(8,128)} %get-tuple-element.81, f32[512,512]{1,0:T(8,128)S(1)} %collective-permute-done.30), kind=kOutput, calls=%fused_computation.65 | convolution fusion | flops 1611137024 | bytes 4194304 | tf_op jit(solution)/shard_map/dot_general | solution.py:403
  289.3 1.9 collective-permute-done.32
  292.1 5.7 %collective-permute-done.33 = f32[128,512]{1,0:T(8,128)S(1)} collective-permute-done((f32[128,512]{1,0:T(8,128)S(1)}, f32[128,512]{1,0:T(8,128)S(1)}, u32[]{:S(2)}, u32[]{:S(2)}) %collective-permute-start.33) | collective-permute-done | bytes 262176 | tf_op jit(solution)/shard_map/ppermute | solution.py:285
  298.4 4.5 %collective-permute-done.34 = f32[64,512]{1,0:T(8,128)S(1)} collective-permute-done((f32[64,512]{1,0:T(8,128)S(1)}, f32[64,512]{1,0:T(8,128)S(1)}, u32[]{:S(2)}, u32[]{:S(2)}) %collective-permute-start.34) | collective-permute-done | bytes 131104 | tf_op jit(solution)/shard_map/ppermute | solution.py:285
  303.2 4.7 %collective-permute-done.35 = f32[64,512]{1,0:T(8,128)S(1)} collective-permute-done((f32[64,512]{1,0:T(8,128)S(1)}, f32[64,512]{1,0:T(8,128)S(1)}, u32[]{:S(2)}, u32[]{:S(2)}) %collective-permute-start.35) | collective-permute-done | bytes 131104 | tf_op jit(solution)/shard_map/ppermute | solution.py:263
  308.0 7.2 %collective-permute-done.36 = f32[64,512]{1,0:T(8,128)S(1)} collective-permute-done((f32[64,512]{1,0:T(8,128)S(1)}, f32[64,512]{1,0:T(8,128)S(1)}, u32[]{:S(2)}, u32[]{:S(2)}) %collective-permute-start.36) | collective-permute-done | bytes 131104 | tf_op jit(solution)/shard_map/ppermute | solution.py:263
  315.8 5.9 %collective-permute-done.37 = f32[64,512]{1,0:T(8,128)S(1)} collective-permute-done((f32[64,512]{1,0:T(8,128)S(1)}, f32[64,512]{1,0:T(8,128)S(1)}, u32[]{:S(2)}, u32[]{:S(2)}) %collective-permute-start.37) | collective-permute-done | bytes 131104 | tf_op jit(solution)/shard_map/ppermute | solution.py:292
  322.6 5.7 %collective-permute-done.38 = f32[128,512]{1,0:T(8,128)S(1)} collective-permute-done((f32[128,512]{1,0:T(8,128)S(1)}, f32[128,512]{1,0:T(8,128)S(1)}, u32[]{:S(2)}, u32[]{:S(2)}) %collective-permute-start.38) | collective-permute-done | bytes 262176 | tf_op jit(solution)/shard_map/ppermute | solution.py:292
  328.4 1.9 collective-permute-done.39
  331.5 27.3 %factorize.3 = (f32[512,512]{1,0:T(8,128)}, f32[512,512]{1,0:T(8,128)}) custom-call(f32[512,512]{1,0:T(8,128)} %bitcast_select_fusion.1.g_ref), custom_call_target="tpu_custom_call" | custom-call | tf_op jit(solution)/shard_map/factorize/pallas_call | solution.py:221
  358.8 4.4 %fusion.13 = f32[512,512]{1,0:T(8,128)} fusion(f32[512,512]{1,0:T(8,128)} %get-tuple-element.92, f32[512,512]{1,0:T(8,128)} %collective-permute-done.31, f32[512,512]{1,0:T(8,128)S(1)} %copy-done.1, f32[512,512]{1,0:T(8,128)S(1)} %collective-permute-done.30), kind=kOutput, calls=%fused_computation.64 | convolution fusion | flops 1611137024 | bytes 5242880 | tf_op jit(solution)/shard_map/dot_general | solution.py:405
  (114 shorter events, 36.7 us)
Async XLA Ops:
  0.6 1.6 copy-start
  7.3 17.6 %collective-permute-start = (bf16[512,512]{1,0:T(8,128)(2,1)}, bf16[512,512]{1,0:T(8,128)(2,1)}, u32[]{:S(2)}, u32[]{:S(2)}) collective-permute-start(bf16[512,512]{1,0:T(8,128)(2,1)} %get-tuple-element.51), channel_id=1, source_target_pairs={{0,1},{3,2},{4,5},{7,6},{8,9},{11,10},{12,13},{15,14},{16,17},{19,... | collective-permute-start | bytes 1572872 | tf_op jit(solution)/shard_map/ppermute | solution.py:240
  18.3 22.9 %collective-permute-start.3 = (bf16[512,512]{1,0:T(8,128)(2,1)}, bf16[512,512]{1,0:T(8,128)(2,1)}, u32[]{:S(2)}, u32[]{:S(2)}) collective-permute-start(bf16[512,512]{1,0:T(8,128)(2,1)} %get-tuple-element.58), channel_id=1, source_target_pairs={{0,1},{3,2},{4,5},{7,6},{8,9},{11,10},{12,13},{15,14},{16,17},{19,... | collective-permute-start | bytes 1572872 | tf_op jit(solution)/shard_map/ppermute | solution.py:240
  27.3 17.7 %collective-permute-start.1 = (bf16[512,512]{1,0:T(8,128)(2,1)}, bf16[512,512]{1,0:T(8,128)(2,1)}, u32[]{:S(2)}, u32[]{:S(2)}) collective-permute-start(bf16[512,512]{1,0:T(8,128)(2,1)} %convert_element_type.76), channel_id=1, source_target_pairs={{1,2},{2,1},{5,6},{6,5},{9,10},{10,9},{13,14},{14,13},{17,18},{18,... | collective-permute-start | bytes 1572872 | tf_op jit(solution)/shard_map/ppermute | solution.py:247
  33.9 25.1 %collective-permute-start.6 = (bf16[512,512]{1,0:T(8,128)(2,1)}, bf16[512,512]{1,0:T(8,128)(2,1)}, u32[]{:S(2)}, u32[]{:S(2)}) collective-permute-start(bf16[512,512]{1,0:T(8,128)(2,1)} %get-tuple-element.63), channel_id=1, source_target_pairs={{0,1},{3,2},{4,5},{7,6},{8,9},{11,10},{12,13},{15,14},{16,17},{19,... | collective-permute-start | bytes 1572872 | tf_op jit(solution)/shard_map/ppermute | solution.py:240
  43.5 17.5 %collective-permute-start.4 = (bf16[512,512]{1,0:T(8,128)(2,1)}, bf16[512,512]{1,0:T(8,128)(2,1)}, u32[]{:S(2)}, u32[]{:S(2)}) collective-permute-start(bf16[512,512]{1,0:T(8,128)(2,1)} %fusion), channel_id=1, source_target_pairs={{1,2},{2,1},{5,6},{6,5},{9,10},{10,9},{13,14},{14,13},{17,18},{18,... | collective-permute-start | bytes 1572872 | tf_op jit(solution)/shard_map/ppermute | solution.py:247
  47.0 12.1 %copy-start.3 = (f32[512,512]{1,0:T(8,128)S(1)}, f32[512,512]{1,0:T(8,128)}, u32[]{:S(2)}) copy-start(f32[512,512]{1,0:T(8,128)} %get-tuple-element.62) | copy-start | bytes 3145732
  47.0 24.1 %collective-permute-start.2 = (bf16[512,512]{1,0:T(8,128)(2,1)}, bf16[512,512]{1,0:T(8,128)(2,1)}, u32[]{:S(2)}, u32[]{:S(2)}) collective-permute-start(bf16[512,512]{1,0:T(8,128)(2,1)} %add_convert_fusion.5), channel_id=1, source_target_pairs={{1,0},{2,3},{5,4},{6,7},{9,8},{10,11},{13,12},{14,15},{17,16},{18,... | collective-permute-start | bytes 1572872 | tf_op jit(solution)/shard_map/ppermute | solution.py:255
  53.5 7.5 %copy-start.2 = (f32[512,512]{1,0:T(8,128)S(1)}, f32[512,512]{1,0:T(8,128)}, u32[]{:S(2)}) copy-start(f32[512,512]{1,0:T(8,128)} %get-tuple-element.57) | copy-start | bytes 3145732
  53.5 14.1 %copy-start.5 = (f32[512,512]{1,0:T(8,128)S(1)}, f32[512,512]{1,0:T(8,128)}, u32[]{:S(2)}) copy-start(f32[512,512]{1,0:T(8,128)} %get-tuple-element.64) | copy-start | bytes 3145732
  53.5 14.1 %collective-permute-start.9 = (bf16[512,512]{1,0:T(8,128)(2,1)}, bf16[512,512]{1,0:T(8,128)(2,1)S(1)}, u32[]{:S(2)}, u32[]{:S(2)}) collective-permute-start(bf16[512,512]{1,0:T(8,128)(2,1)} %get-tuple-element.65), channel_id=1, source_target_pairs={{0,1},{3,2},{4,5},{7,6},{8,9},{11,10},{12,13},{15,14},{16,17},{19,... | collective-permute-start | bytes 1572872 | tf_op jit(solution)/shard_map/ppermute | solution.py:240
  60.3 8.3 %collective-permute-start.7 = (bf16[512,512]{1,0:T(8,128)(2,1)S(1)}, bf16[512,512]{1,0:T(8,128)(2,1)S(1)}, u32[]{:S(2)}, u32[]{:S(2)}) collective-permute-start(bf16[512,512]{1,0:T(8,128)(2,1)S(1)} %fusion.1), channel_id=1, source_target_pairs={{1,2},{2,1},{5,6},{6,5},{9,10},{10,9},{13,14},{14,13},{17,18},{18,... | collective-permute-start | bytes 1572872 | tf_op jit(solution)/shard_map/ppermute | solution.py:247
  62.4 15.4 %collective-permute-start.5 = (bf16[512,512]{1,0:T(8,128)(2,1)S(1)}, bf16[512,512]{1,0:T(8,128)(2,1)S(1)}, u32[]{:S(2)}, u32[]{:S(2)}) collective-permute-start(bf16[512,512]{1,0:T(8,128)(2,1)S(1)} %add_convert_fusion.4), channel_id=1, source_target_pairs={{1,0},{2,3},{5,4},{6,7},{9,8},{10,11},{13,12},{14,15},{17,16},{18,... | collective-permute-start | bytes 1572872 | tf_op jit(solution)/shard_map/ppermute | solution.py:255
  67.8 5.2 %collective-permute-start.10 = (bf16[512,512]{1,0:T(8,128)(2,1)S(1)}, bf16[512,512]{1,0:T(8,128)(2,1)S(1)}, u32[]{:S(2)}, u32[]{:S(2)}) collective-permute-start(bf16[512,512]{1,0:T(8,128)(2,1)S(1)} %fusion.2), channel_id=1, source_target_pairs={{1,2},{2,1},{5,6},{6,5},{9,10},{10,9},{13,14},{14,13},{17,18},{18,... | collective-permute-start | bytes 1572872 | tf_op jit(solution)/shard_map/ppermute | solution.py:247
  69.8 19.4 %collective-permute-start.8 = (bf16[512,512]{1,0:T(8,128)(2,1)S(1)}, bf16[512,512]{1,0:T(8,128)(2,1)S(1)}, u32[]{:S(2)}, u32[]{:S(2)}) collective-permute-start(bf16[512,512]{1,0:T(8,128)(2,1)S(1)} %add_convert_fusion.3), channel_id=1, source_target_pairs={{1,0},{2,3},{5,4},{6,7},{9,8},{10,11},{13,12},{14,15},{17,16},{18,... | collective-permute-start | bytes 1572872 | tf_op jit(solution)/shard_map/ppermute | solution.py:255
  73.2 24.1 %collective-permute-start.11 = (bf16[512,512]{1,0:T(8,128)(2,1)S(1)}, bf16[512,512]{1,0:T(8,128)(2,1)S(1)}, u32[]{:S(2)}, u32[]{:S(2)}) collective-permute-start(bf16[512,512]{1,0:T(8,128)(2,1)S(1)} %add_convert_fusion.2), channel_id=1, source_target_pairs={{1,0},{2,3},{5,4},{6,7},{9,8},{10,11},{13,12},{14,15},{17,16},{18,... | collective-permute-start | bytes 1572872 | tf_op jit(solution)/shard_map/ppermute | solution.py:255
  88.0 9.4 %copy-start.8 = (bf16[512,512]{1,0:T(8,128)(2,1)S(1)}, bf16[512,512]{1,0:T(8,128)(2,1)}, u32[]{:S(2)}) copy-start(bf16[512,512]{1,0:T(8,128)(2,1)} %broadcast_select_fusion.3.refs_0_) | copy-start | bytes 1572868
  88.0 9.4 %copy-start.9 = (bf16[512,512]{1,0:T(8,128)(2,1)S(1)}, bf16[512,512]{1,0:T(8,128)(2,1)}, u32[]{:S(2)}) copy-start(bf16[512,512]{1,0:T(8,128)(2,1)} %broadcast_select_fusion.2.refs_1_) | copy-start | bytes 1572868
  89.2 10.0 %copy-start.7 = (bf16[512,512]{1,0:T(8,128)(2,1)}, bf16[512,512]{1,0:T(8,128)(2,1)S(1)}, u32[]{:S(2)}) copy-start(bf16[512,512]{1,0:T(8,128)(2,1)S(1)} %broadcast_select_fusion.1.refs_0_) | copy-start | bytes 1572868
  97.4 1.9 copy-start.6
  99.3 7.7 %collective-permute-start.12 = (f32[256,512]{1,0:T(8,128)S(1)}, f32[256,512]{1,0:T(8,128)S(1)}, u32[]{:S(2)}, u32[]{:S(2)}) collective-permute-start(f32[256,512]{1,0:T(8,128)S(1)} %constant_dynamic-slice_fusion.7), channel_id=1, source_target_pairs={{0,4},{4,0},{8,12},{12,8},{16,20},{20,16},{24,28},{28,24},{1,5},{5... | collective-permute-start | bytes 1572872 | tf_op jit(solution)/shard_map/ppermute | solution.py:285
  107.2 10.0 %collective-permute-start.13 = (f32[128,512]{1,0:T(8,128)S(1)}, f32[128,512]{1,0:T(8,128)S(1)}, u32[]{:S(2)}, u32[]{:S(2)}) collective-permute-start(f32[128,512]{1,0:T(8,128)S(1)} %constant_dynamic-slice_fusion.6), channel_id=1, source_target_pairs={{0,8},{4,20},{8,0},{12,28},{16,24},{20,4},{24,16},{28,12},{1,9},{5... | collective-permute-start | bytes 786440 | tf_op jit(solution)/shard_map/ppermute | solution.py:285
  119.0 19.6 %collective-permute-start.17 = (f32[1024,512]{1,0:T(8,128)S(1)}, f32[1024,512]{1,0:T(8,128)}, u32[]{:S(2)}, u32[]{:S(2)}) collective-permute-start(f32[1024,512]{1,0:T(8,128)S(1)} %constant_dynamic-slice_fusion.4), channel_id=1, source_target_pairs={{0,4},{4,0},{8,12},{12,8},{16,20},{20,16},{24,28},{28,24},{1,5},{5... | collective-permute-start | bytes 6291464 | tf_op jit(solution)/shard_map/ppermute | solution.py:285
  119.7 5.4 %collective-permute-start.14 = (f32[64,512]{1,0:T(8,128)S(1)}, f32[64,512]{1,0:T(8,128)S(1)}, u32[]{:S(2)}, u32[]{:S(2)}) collective-permute-start(f32[64,512]{1,0:T(8,128)S(1)} %constant_dynamic-slice_fusion.5), channel_id=1, source_target_pairs={{0,16},{4,12},{8,24},{12,4},{16,0},{20,28},{24,8},{28,20},{1,17},{... | collective-permute-start | bytes 393224 | tf_op jit(solution)/shard_map/ppermute | solution.py:285
  125.1 5.3 %collective-permute-start.15 = (f32[64,512]{1,0:T(8,128)S(1)}, f32[64,512]{1,0:T(8,128)S(1)}, u32[]{:S(2)}, u32[]{:S(2)}) collective-permute-start(f32[64,512]{1,0:T(8,128)S(1)} %dynamic-slice_add_fusion.6), channel_id=1, source_target_pairs={{0,1},{1,0},{2,3},{3,2},{4,5},{5,4},{6,7},{7,6},{8,9},{9,8},{10,11... | collective-permute-start | bytes 393224 | tf_op jit(solution)/shard_map/ppermute | solution.py:263
  130.4 8.2 %collective-permute-start.16 = (f32[64,512]{1,0:T(8,128)S(1)}, f32[64,512]{1,0:T(8,128)S(1)}, u32[]{:S(2)}, u32[]{:S(2)}) collective-permute-start(f32[64,512]{1,0:T(8,128)S(1)} %add.144), channel_id=1, source_target_pairs={{0,2},{1,3},{2,0},{3,1},{4,6},{5,7},{6,4},{7,5},{8,10},{9,11},{10,... | collective-permute-start | bytes 393224 | tf_op jit(solution)/shard_map/ppermute | solution.py:263
  141.3 6.4 %collective-permute-start.18 = (f32[64,512]{1,0:T(8,128)S(1)}, f32[64,512]{1,0:T(8,128)S(1)}, u32[]{:S(2)}, u32[]{:S(2)}) collective-permute-start(f32[64,512]{1,0:T(8,128)S(1)} %add.145), channel_id=1, source_target_pairs={{0,16},{4,12},{8,24},{12,4},{16,0},{20,28},{24,8},{28,20},{1,17},{... | collective-permute-start | bytes 393224 | tf_op jit(solution)/shard_map/ppermute | solution.py:292
  142.9 13.1 %collective-permute-start.21 = (bf16[512,512]{1,0:T(8,128)(2,1)S(1)}, bf16[512,512]{1,0:T(8,128)(2,1)}, u32[]{:S(2)}, u32[]{:S(2)}) collective-permute-start(bf16[512,512]{1,0:T(8,128)(2,1)S(1)} %dynamic-slice_convert_fusion), channel_id=1, source_target_pairs={{0,8},{4,20},{8,0},{12,28},{16,24},{20,4},{24,16},{28,12},{1,9},{5... | collective-permute-start | bytes 1572872 | tf_op jit(solution)/shard_map/ppermute | solution.py:285
  147.8 7.1 %collective-permute-start.19 = (f32[128,512]{1,0:T(8,128)S(1)}, f32[128,512]{1,0:T(8,128)S(1)}, u32[]{:S(2)}, u32[]{:S(2)}) collective-permute-start(f32[128,512]{1,0:T(8,128)S(1)} %bitcast_select_fusion.8), channel_id=1, source_target_pairs={{0,8},{4,20},{8,0},{12,28},{16,24},{20,4},{24,16},{28,12},{1,9},{5... | collective-permute-start | bytes 786440 | tf_op jit(solution)/shard_map/ppermute | solution.py:292
  155.9 2.3 collective-permute-start.20
  160.5 28.2 %collective-permute-start.22 = (f32[256,512]{1,0:T(8,128)S(1)}, f32[256,512]{1,0:T(8,128)S(1)}, u32[]{:S(2)}, u32[]{:S(2)}) collective-permute-start(f32[256,512]{1,0:T(8,128)S(1)} %constant_dynamic-slice_fusion.3), channel_id=1, source_target_pairs={{0,16},{4,12},{8,24},{12,4},{16,0},{20,28},{24,8},{28,20},{1,17},{... | collective-permute-start | bytes 1572872 | tf_op jit(solution)/shard_map/ppermute | solution.py:285
  191.0 6.4 %collective-permute-start.23 = (bf16[256,512]{1,0:T(8,128)(2,1)S(1)}, bf16[256,512]{1,0:T(8,128)(2,1)S(1)}, u32[]{:S(2)}, u32[]{:S(2)}) collective-permute-start(bf16[256,512]{1,0:T(8,128)(2,1)S(1)} %convolution_convert_fusion), channel_id=1, source_target_pairs={{0,16},{4,12},{8,24},{12,4},{16,0},{20,28},{24,8},{28,20},{1,17},{... | collective-permute-start | bytes 786440 | tf_op jit(solution)/shard_map/ppermute | solution.py:292
  197.6 9.2 %collective-permute-start.24 = (bf16[512,512]{1,0:T(8,128)(2,1)S(1)}, bf16[512,512]{1,0:T(8,128)(2,1)S(1)}, u32[]{:S(2)}, u32[]{:S(2)}) collective-permute-start(bf16[512,512]{1,0:T(8,128)(2,1)S(1)} %bitcast_select_fusion.5), channel_id=1, source_target_pairs={{0,8},{4,20},{8,0},{12,28},{16,24},{20,4},{24,16},{28,12},{1,9},{5... | collective-permute-start | bytes 1572872 | tf_op jit(solution)/shard_map/ppermute | solution.py:292
  207.1 2.9 collective-permute-start.25
  216.7 13.3 %collective-permute-start.26 = (bf16[512,512]{1,0:T(8,128)(2,1)}, bf16[512,512]{1,0:T(8,128)(2,1)}, u32[]{:S(2)}, u32[]{:S(2)}) collective-permute-start(bf16[512,512]{1,0:T(8,128)(2,1)} %get-tuple-element.85), channel_id=1, source_target_pairs={{0,1},{4,5},{8,9},{12,13},{16,17},{20,21},{24,25},{28,29}} | collective-permute-start | bytes 1572872 | tf_op jit(solution)/shard_map/ppermute | solution.py:332
  219.0 11.0 %collective-permute-start.27 = (bf16[512,512]{1,0:T(8,128)(2,1)}, bf16[512,512]{1,0:T(8,128)(2,1)}, u32[]{:S(2)}, u32[]{:S(2)}) collective-permute-start(bf16[512,512]{1,0:T(8,128)(2,1)} %get-tuple-element.85), channel_id=1, source_target_pairs={{3,2},{7,6},{11,10},{15,14},{19,18},{23,22},{27,26},{31,30}} | collective-permute-start | bytes 1572872 | tf_op jit(solution)/shard_map/ppermute | solution.py:333
  220.5 9.6 %copy-start.10 = (f32[512,512]{1,0:T(8,128)S(1)}, f32[512,512]{1,0:T(8,128)}, u32[]{:S(2)}) copy-start(f32[512,512]{1,0:T(8,128)} %get-tuple-element.84) | copy-start | bytes 3145732
  233.0 15.4 %collective-permute-start.28 = (bf16[512,512]{1,0:T(8,128)(2,1)}, bf16[512,512]{1,0:T(8,128)(2,1)}, u32[]{:S(2)}, u32[]{:S(2)}) collective-permute-start(bf16[512,512]{1,0:T(8,128)(2,1)} %get-tuple-element.97), channel_id=1, source_target_pairs={{0,1},{1,2},{4,5},{5,6},{8,9},{9,10},{12,13},{13,14},{16,17},{17,1... | collective-permute-start | bytes 1572872 | tf_op jit(solution)/shard_map/ppermute | solution.py:332
  238.2 10.2 %collective-permute-start.29 = (bf16[512,512]{1,0:T(8,128)(2,1)}, bf16[512,512]{1,0:T(8,128)(2,1)}, u32[]{:S(2)}, u32[]{:S(2)}) collective-permute-start(bf16[512,512]{1,0:T(8,128)(2,1)} %get-tuple-element.96), channel_id=1, source_target_pairs={{3,2},{2,1},{7,6},{6,5},{11,10},{10,9},{15,14},{14,13},{19,18},{18... | collective-permute-start | bytes 1572872 | tf_op jit(solution)/shard_map/ppermute | solution.py:333
  239.6 8.7 %copy-start.4 = (f32[512,512]{1,0:T(8,128)S(1)}, f32[512,512]{1,0:T(8,128)}, u32[]{:S(2)}) copy-start(f32[512,512]{1,0:T(8,128)} %get-tuple-element.82) | copy-start | bytes 3145732
  251.5 29.3 %collective-permute-start.30 = (f32[512,512]{1,0:T(8,128)}, f32[512,512]{1,0:T(8,128)S(1)}, u32[]{:S(2)}, u32[]{:S(2)}) collective-permute-start(f32[512,512]{1,0:T(8,128)} %get-tuple-element.95), channel_id=1, source_target_pairs={{0,1},{1,2},{2,3},{4,5},{5,6},{6,7},{8,9},{9,10},{10,11},{12,13},{... | collective-permute-start | bytes 3145736 | tf_op jit(solution)/shard_map/ppermute | solution.py:332
  259.8 25.1 %collective-permute-start.31 = (f32[512,512]{1,0:T(8,128)}, f32[512,512]{1,0:T(8,128)}, u32[]{:S(2)}, u32[]{:S(2)}) collective-permute-start(f32[512,512]{1,0:T(8,128)} %get-tuple-element.94), channel_id=1, source_target_pairs={{3,2},{2,1},{1,0},{7,6},{6,5},{5,4},{11,10},{10,9},{9,8},{15,14},{... | collective-permute-start | bytes 3145736 | tf_op jit(solution)/shard_map/ppermute | solution.py:333
  289.2 2.0 collective-permute-start.32
  291.3 6.4 %collective-permute-start.33 = (f32[128,512]{1,0:T(8,128)S(1)}, f32[128,512]{1,0:T(8,128)S(1)}, u32[]{:S(2)}, u32[]{:S(2)}) collective-permute-start(f32[128,512]{1,0:T(8,128)S(1)} %constant_dynamic-slice_fusion.1), channel_id=1, source_target_pairs={{0,8},{4,20},{8,0},{12,28},{16,24},{20,4},{24,16},{28,12},{1,9},{5... | collective-permute-start | bytes 786440 | tf_op jit(solution)/shard_map/ppermute | solution.py:285
  297.8 5.0 %collective-permute-start.34 = (f32[64,512]{1,0:T(8,128)S(1)}, f32[64,512]{1,0:T(8,128)S(1)}, u32[]{:S(2)}, u32[]{:S(2)}) collective-permute-start(f32[64,512]{1,0:T(8,128)S(1)} %constant_dynamic-slice_fusion), channel_id=1, source_target_pairs={{0,16},{4,12},{8,24},{12,4},{16,0},{20,28},{24,8},{28,20},{1,17},{... | collective-permute-start | bytes 393224 | tf_op jit(solution)/shard_map/ppermute | solution.py:285
  302.9 5.0 %collective-permute-start.35 = (f32[64,512]{1,0:T(8,128)S(1)}, f32[64,512]{1,0:T(8,128)S(1)}, u32[]{:S(2)}, u32[]{:S(2)}) collective-permute-start(f32[64,512]{1,0:T(8,128)S(1)} %dynamic-slice_add_fusion.5), channel_id=1, source_target_pairs={{0,1},{1,0},{2,3},{3,2},{4,5},{5,4},{6,7},{7,6},{8,9},{9,8},{10,11... | collective-permute-start | bytes 393224 | tf_op jit(solution)/shard_map/ppermute | solution.py:263
  308.0 7.3 %collective-permute-start.36 = (f32[64,512]{1,0:T(8,128)S(1)}, f32[64,512]{1,0:T(8,128)S(1)}, u32[]{:S(2)}, u32[]{:S(2)}) collective-permute-start(f32[64,512]{1,0:T(8,128)S(1)} %add.164), channel_id=1, source_target_pairs={{0,2},{1,3},{2,0},{3,1},{4,6},{5,7},{6,4},{7,5},{8,10},{9,11},{10,... | collective-permute-start | bytes 393224 | tf_op jit(solution)/shard_map/ppermute | solution.py:263
  315.3 6.4 %collective-permute-start.37 = (f32[64,512]{1,0:T(8,128)S(1)}, f32[64,512]{1,0:T(8,128)S(1)}, u32[]{:S(2)}, u32[]{:S(2)}) collective-permute-start(f32[64,512]{1,0:T(8,128)S(1)} %add.165), channel_id=1, source_target_pairs={{0,16},{4,12},{8,24},{12,4},{16,0},{20,28},{24,8},{28,20},{1,17},{... | collective-permute-start | bytes 393224 | tf_op jit(solution)/shard_map/ppermute | solution.py:292
  321.8 37.0 %copy-start.1 = (f32[512,512]{1,0:T(8,128)S(1)}, f32[512,512]{1,0:T(8,128)}, u32[]{:S(2)}) copy-start(f32[512,512]{1,0:T(8,128)} %get-tuple-element.81) | copy-start | bytes 3145732
  321.8 6.4 %collective-permute-start.38 = (f32[128,512]{1,0:T(8,128)S(1)}, f32[128,512]{1,0:T(8,128)S(1)}, u32[]{:S(2)}, u32[]{:S(2)}) collective-permute-start(f32[128,512]{1,0:T(8,128)S(1)} %bitcast_select_fusion.7), channel_id=1, source_target_pairs={{0,8},{4,20},{8,0},{12,28},{16,24},{20,4},{24,16},{28,12},{1,9},{5... | collective-permute-start | bytes 786440 | tf_op jit(solution)/shard_map/ppermute | solution.py:292
  328.4 2.0 collective-permute-start.39
